TPU v7x, 32 devices: a whole 2x2x4 slice. The times are simulated.
32 devices in a mesh: train: 16 (over z, y, core), cand: 2 (over x).
Axes of the slice: x: 2, y: 2, z: 4, core: 2. Of those that a mesh axis runs over, the one named last changes fastest.
Arguments:
- x_train: float32 [8, 2048], P(None, 'train'), may hold values from -4 to 4
- x_cand: float32 [8, 1024], P(None, 'cand'), may hold values from -4 to 4
- targets: float32 [2048], P(('train', 'cand')), may hold values from -6 to 6
- noise: float32 [2048, 64], P(('train', 'cand')), may hold values from -5 to 5
- omega: float32 [8, 4096], replicated, may hold values from -6 to 6
- phase: float32 [4096], replicated, may hold values from -3.140625 to 3.140625
- prior_weights: bfloat16 [4096, 64], P('cand'), may hold values from -6 to 6
Outputs:
- samples: float32 [1024, 64], P(('cand', 'train'))
- solution: float32 [2048, 64], P(('train', 'cand'))
All inputs are finite; a program needn't handle non-finite values.
Results may differ from a plain program's by a relative error of at most 0.0019.
The roundings to bfloat16 on the way count: a program that leaves them out, or rounds other values in their place, can miss the bound.
Values may be sent and summed in bfloat16 or wider, within the bound.
No kernel may reach another device: no remote copies, remote signals or barrier semaphores. Data moves between devices by JAX's collectives and lax.ppermute only.
A program may use at most 64 MiB of HBM per device.

v0:
```python
import math

import jax
import jax.numpy as jnp
from jax import lax
from jax.sharding import PartitionSpec as P

ITERS = 2


noise_level = 0.5


def squares_of(points):
    return jnp.sum(points * points, axis=0)


def kernel_tile(row_points, row_norms, column_points, column_norms):
    inner = jnp.dot(row_points.T, column_points, precision=lax.Precision.HIGHEST)
    return jnp.exp(-0.5 * (row_norms[:, None] + column_norms[None, :] - 2.0 * inner)).astype(
        jnp.bfloat16
    )


def features(points, omega, phase):
    angles = jnp.dot(points.T, omega, precision=lax.Precision.HIGHEST) + phase[None, :]
    return (math.sqrt(2.0 / omega.shape[1]) * jnp.cos(angles)).astype(jnp.bfloat16)


def kernel_rows(points, every_point, every_norm, weights):
    count = points.shape[1]
    size = math.gcd(count, 1024)
    stacked = points.reshape(points.shape[0], count // size, size).transpose(1, 0, 2)

    def one_block(block_points):
        tile = kernel_tile(block_points, squares_of(block_points), every_point, every_norm)
        return jnp.dot(tile, weights, preferred_element_type=jnp.float32)

    return lax.map(one_block, stacked).reshape(count, weights.shape[1])


def body(x_train, x_cand, targets, noise, omega, phase, prior_weights):
    own_rows = noise.shape[0]
    cand_index = lax.axis_index("cand")
    train_index = lax.axis_index("train")
    own_points = lax.dynamic_slice_in_dim(x_train, cand_index * own_rows, own_rows, 1)
    full_weights = lax.all_gather(prior_weights, "cand", axis=0, tiled=True)
    prior_train = jnp.dot(
        features(own_points, omega, phase), full_weights, preferred_element_type=jnp.float32
    )
    rhs = targets[:, None] - prior_train - noise
    column_points = lax.all_gather(own_points, "train", axis=1, tiled=True)
    row_norms = squares_of(x_train)
    column_norms = squares_of(column_points)
    width = max(128, 262144 // x_train.shape[1])

    def squares(values):
        return lax.psum(jnp.sum(values * values, axis=0), ("train", "cand"))

    solution = jnp.zeros(rhs.shape, jnp.float32)
    residual = rhs
    direction = rhs
    norm_now = squares(residual)
    for step in range(ITERS):
        packed = direction.astype(jnp.bfloat16)
        empty = jnp.zeros((x_train.shape[1], packed.shape[1]), jnp.float32)
        total = empty
        piece = lax.all_gather(packed, "train", axis=0, tiled=True)
        for offset in range(0, piece.shape[0], width):
            count = min(width, piece.shape[0] - offset)
            accumulate_points = lax.dynamic_slice_in_dim(column_points, offset, count, 1)
            norms = lax.dynamic_slice_in_dim(column_norms, offset, count, 0)
            tile = kernel_tile(x_train, row_norms, accumulate_points, norms)
            total = total + jnp.dot(
                tile, piece[offset : offset + count], preferred_element_type=jnp.float32
            )
        apply_total = total
        apply_total = lax.psum_scatter(apply_total, "cand", scatter_dimension=0, tiled=True)
        image = apply_total + noise_level * direction
        curve = lax.psum(jnp.sum(direction * image, axis=0), ("train", "cand"))
        alpha = norm_now / curve
        solution = solution + alpha * direction
        residual = residual - alpha * image
        norm_next = squares(residual)
        direction = residual + norm_next / norm_now * direction
        norm_now = norm_next
    per_device = x_cand.shape[1] // lax.axis_size("train")
    mine = lax.dynamic_slice_in_dim(x_cand, train_index * per_device, per_device, 1)
    packed_solution = solution.astype(jnp.bfloat16)
    block_weights = lax.all_gather(packed_solution, "cand", axis=0, tiled=True)
    train_norms = squares_of(x_train)
    kernel_part = lax.psum_scatter(
        kernel_rows(x_cand, x_train, train_norms, block_weights),
        "train",
        scatter_dimension=0,
        tiled=True,
    )
    prior_cand = jnp.dot(
        features(mine, omega, phase), full_weights, preferred_element_type=jnp.float32
    )
    return (prior_cand + kernel_part, solution)


def solution(mesh):
    placed = (
        P(None, "train"),
        P(None, "cand"),
        P(("train", "cand")),
        P(("train", "cand"), None),
        P(),
        P(),
        P("cand", None),
    )
    return jax.shard_map(
        body,
        mesh=mesh,
        in_specs=placed,
        out_specs=(P(("cand", "train"), None), P(("train", "cand"), None)),
        check_vma=False,
    )
```

profile of v0, /device:TPU:0, one launch (start us, length us, event | category | flops | bytes accessed | tf_op | source)
XLA Modules:
  0.0 296.1 jit_solution(272035158380049314)
XLA Ops:
  7.2 0.0 reduce-scatter.4.cloned.1.call-start
  7.2 0.7 multiply_reduce_fusion.6
  8.0 10.3 %all_gather.15 = bf16[4096,64]{0,1:T(8,128)(2,1)S(1)} all-gather(bf16[2048,64]{0,1:T(8,128)(2,1)} %param.13), channel_id=1, replica_groups=mesh['train'=16,'cand'=2] {'cand'}, dimensions={0}, use_global_device_ids=true | all-gather | bytes 786432 | tf_op jit(solution)/shard_map/all_gather | solution.py:47
  18.3 0.1 dynamic-slice_bitcast_fusion
  18.4 22.0 %all-gather = f32[16,64,8]{1,2,0:T(8,128)S(1)} all-gather(f32[1,64,8]{1,2,0:T(8,128)S(1)} %dynamic-slice_bitcast_fusion), channel_id=1, replica_groups=mesh['train'=16,'cand'=2] {'train'}, dimensions={0}, use_global_device_ids=true | all-gather | bytes 34816 | tf_op jit(solution)/shard_map/all_gather | solution.py:52
  40.4 0.1 reshape.18
  40.5 0.7 copy-done.2
  41.2 4.7 %fusion.2 = bf16[64,4096]{1,0:T(8,128)(2,1)S(1)} fusion(f32[8,4096]{1,0:T(8,128)S(1)} %copy-done, f32[4096]{0:T(1024)S(1)} %copy-done.2, f32[8,128]{1,0:T(8,128)S(1)} %copy-done.3, s32[]{:T(128)S(6)} %select_n.7), kind=kOutput, calls=%fused_computation.3 | convolution fusion | flops 25952256 | bytes 675844 | tf_op jit(solution)/shard_map/dot_general | solution.py:26
  46.0 0.3 fusion.22
  46.3 18.1 %all_gather.17 = bf16[1024,64]{1,0:T(8,128)(2,1)S(1)} all-gather(bf16[64,64]{1,0:T(8,128)(2,1)S(1)} %get-tuple-element.26), channel_id=1, replica_groups=mesh['train'=16,'cand'=2] {'train'}, dimensions={0}, use_global_device_ids=true | all-gather | bytes 139264 | tf_op jit(solution)/shard_map/all_gather | solution.py:68
  64.4 1.0 fusion.10
  65.5 0.9 fusion.23
  66.4 0.0 reduce-scatter.4.cloned.1.call-update
  66.4 0.0 reduce-scatter.6.cloned.1.call-start
  66.5 0.6 copy-done.5
  67.1 7.8 %reduce-scatter.4.cloned.1.call-done = f32[64,64]{1,0:T(8,128)} async-done(((f32[128,64]{1,0:T(8,128)}), f32[64,64]{1,0:T(8,128)}) %reduce-scatter.4.cloned.1.call-update) | async-done | bytes 16400 | tf_op jit(solution)/shard_map/reduce_scatter | solution.py:78
  74.9 0.9 multiply_reduce_fusion.3
  75.8 39.3 %all-reduce = (f32[64]{0:T(128)S(1)}, f32[64]{0:T(128)S(1)}) all-reduce(f32[64]{0:T(128)S(1)} %get-tuple-element.15, f32[64]{0:T(128)S(1)} %get-tuple-element.14), channel_id=1, replica_groups=mesh['train'=16,'cand'=2] {'train','cand'}, use_global_device_ids=true, to_apply=%region_3.0 | all-reduce | flops 128 | bytes 1024 | tf_op jit(solution)/shard_map/psum | solution.py:58
  115.2 41.0 %psum.30 = f32[64]{0:T(128)S(1)} all-reduce(f32[64]{0:T(128)S(1)} %multiply_reduce_fusion.2), channel_id=1, replica_groups=mesh['train'=16,'cand'=2] {'train','cand'}, use_global_device_ids=true, to_apply=%region_9.0 | all-reduce | flops 64 | bytes 512 | tf_op jit(solution)/shard_map/psum | solution.py:58
  156.2 21.8 %all_gather.18 = bf16[1024,64]{1,0:T(8,128)(2,1)S(1)} all-gather(bf16[64,64]{1,0:T(8,128)(2,1)S(1)} %fusion.20), channel_id=1, replica_groups=mesh['train'=16,'cand'=2] {'train'}, dimensions={0}, use_global_device_ids=true | all-gather | bytes 139264 | tf_op jit(solution)/shard_map/all_gather | solution.py:68
  178.0 0.9 fusion.24
  178.9 0.0 reduce-scatter.8.cloned.1.call-start
  178.9 0.6 fusion.14
  179.6 5.8 %reduce-scatter.6.cloned.1.call-done = f32[64,64]{1,0:T(8,128)} async-done(((f32[128,64]{1,0:T(8,128)}), f32[64,64]{1,0:T(8,128)}) %reduce-scatter.6.cloned.1.call-update) | async-done | bytes 16400 | tf_op jit(solution)/shard_map/reduce_scatter | solution.py:78
  185.4 0.8 multiply_reduce_fusion.1
  186.1 39.3 %psum.31 = f32[64]{0:T(128)S(1)} all-reduce(f32[64]{0:T(128)S(1)} %multiply_reduce_fusion.1), channel_id=1, replica_groups=mesh['train'=16,'cand'=2] {'train','cand'}, use_global_device_ids=true, to_apply=%region_12.0 | all-reduce | flops 64 | bytes 512 | tf_op jit(solution)/shard_map/psum | solution.py:80
  225.5 0.6 fusion.21
  226.1 4.6 %all_gather.19 = bf16[128,64]{1,0:T(8,128)(2,1)S(1)} all-gather(bf16[64,64]{1,0:T(8,128)(2,1)S(1)} %get-tuple-element.24), channel_id=1, replica_groups=mesh['train'=16,'cand'=2] {'cand'}, dimensions={0}, use_global_device_ids=true | all-gather | bytes 24576 | tf_op jit(solution)/shard_map/all_gather | solution.py:90
  230.7 0.9 fusion.25
  231.6 2.7 fusion.5
  234.3 53.7 %reduce-scatter.8.cloned.1.call-done = f32[32,64]{1,0:T(8,128)} async-done(((f32[512,64]{1,0:T(8,128)}), f32[32,64]{1,0:T(8,128)}) %reduce-scatter.8.cloned.1.call-update) | async-done | bytes 8208 | tf_op jit(solution)/shard_map/reduce_scatter | solution.py:92
  288.0 1.6 convolution_add_fusion.2
  (22 shorter events, 0.2 us)
Async XLA Ops:
  7.2 33.3 %copy-start = (f32[8,4096]{1,0:T(8,128)S(1)}, f32[8,4096]{1,0:T(8,128)}, u32[]{:S(2)}) copy-start(f32[8,4096]{1,0:T(8,128)} %param.11) | copy-start | bytes 393220
  7.2 67.8 %reduce-scatter.4.cloned.1.call-start = ((), (), s32[]{:S(2)}) async-start(), calls=%async_computation.3 | async-start | bytes 98304 | tf_op jit(solution)/shard_map/reduce_scatter | solution.py:78
  8.0 10.3 %copy-start.3 = (f32[8,128]{1,0:T(8,128)S(1)}, f32[8,128]{1,0:T(8,128)}, u32[]{:S(2)}) copy-start(f32[8,128]{1,0:T(8,128)} %param.7) | copy-start | bytes 12292
  40.5 0.7 copy-start.2
  41.2 4.8 %copy-start.4 = (f32[64,64]{1,0:T(8,128)S(1)}, f32[64,64]{1,0:T(8,128)}, u32[]{:S(2)}) copy-start(f32[64,64]{1,0:T(8,128)} %param.10) | copy-start | bytes 49156
  41.2 4.8 %copy-start.6 = (f32[64]{0:T(128)S(1)}, f32[64]{0:T(128)}, u32[]{:S(2)}) copy-start(f32[64]{0:T(128)} %param.9) | copy-start | bytes 772
  66.4 0.7 copy-start.5
  66.4 119.0 %reduce-scatter.6.cloned.1.call-start = ((), (), s32[]{:S(2)}) async-start(), calls=%async_computation.4 | async-start | bytes 98304 | tf_op jit(solution)/shard_map/reduce_scatter | solution.py:78
  74.9 40.2 %copy-start.1 = (f32[64,64]{1,0:T(8,128)S(1)}, f32[64,64]{1,0:T(8,128)}, u32[]{:S(2)}) copy-start(f32[64,64]{1,0:T(8,128)} %reduce-scatter.4.cloned.1.call-done) | copy-start | bytes 49156
  178.9 109.1 %reduce-scatter.8.cloned.1.call-start = ((), (), s32[]{:S(2)}) async-start(), calls=%async_computation.5 | async-start | bytes 278528 | tf_op jit(solution)/shard_map/reduce_scatter | solution.py:92
Sparse Core Ops, SparseCore 0:
  66.5 8.3 reduce-scatter.3
  179.0 6.2 reduce-scatter.5
  231.8 56.2 reduce-scatter.7
where the time goes:
time: 297 us; the launch traced here: 296 us
  blocking collectives  197 us (66%)
  waiting for transfers between devices  67.3 us (23%)
  between operations  13.9 us (5%)
  matrix products  13.6 us (5%)
  other arithmetic  3.1 us (1%)
    psum x2, blocking collectives, squares(): return lax.psum(jnp.sum(values * values, axis=0), ('train', 'cand'))  80.3 us
    reduce_scatter x1, waiting for transfers between devices, body(): lax.psum_scatter(kernel_rows(x_cand, x_train, train_norms, block_weights)...  53.7 us
    all_gather x2, blocking collectives, body(): piece = lax.all_gather(packed, 'train', axis=0, tiled=True)  40 us
    psum x1, blocking collectives, body(): curve = lax.psum(jnp.sum(direction * image, axis=0), ('train', 'cand'))  39.3 us
    all_gather x1, blocking collectives, body(): column_points = lax.all_gather(own_points, 'train', axis=1, tiled=True)  22 us
    reduce_scatter x2, waiting for transfers between devices, body(): lax.psum_scatter(apply_total, 'cand', scatter_dimension=0, tiled=True)  13.6 us
    all_gather x1, blocking collectives, body(): full_weights = lax.all_gather(prior_weights, 'cand', axis=0, tiled=True)  10.3 us
    dot_general x2, matrix products, features(): jnp.dot(points.T, omega, precision=lax.Precision.HIGHEST) + phase[None, :]  7.44 us
  transfers between devices with their start and end apart: 3, of which 3 were waited for; matrix products, arithmetic and copies ran while one was open for 1% of the time, Pallas kernels for 0%

commit v1 on v0

--- a/solution.py
+++ b/solution.py
@@ -1,14 +1,252 @@
+import functools
 import math
 
 import jax
 import jax.numpy as jnp
 from jax import lax
+from jax.experimental import pallas as pl
+from jax.experimental.pallas import tpu as pltpu
 from jax.sharding import PartitionSpec as P
 
 ITERS = 2
 
 
 noise_level = 0.5
+LOG2E = math.log2(math.e)
+COS = (
+    1.0,
+    -19.739208743087787,
+    64.93938905249153,
+    -85.45665775372363,
+    60.24212493122888,
+    -26.404630623401626,
+    7.8000222194698186,
+    -1.4529875517062139,
+)
+KERNEL_BYTES = 16 << 20
+f32, bf16 = jnp.float32, jnp.bfloat16
+
+
+def split3(values):
+    high = values.astype(bf16)
+    rest = values - high.astype(f32)
+    middle = rest.astype(bf16)
+    low = (rest - middle.astype(f32)).astype(bf16)
+    return high, middle, low
+
+
+def left_stack(values, extra):
+    h, m, l = (part.astype(f32) for part in split3(values))
+    return jnp.concatenate([h, h, m, m, h, l] + extra, axis=0).astype(bf16)
+
+
+def right_stack(values, extra):
+    h, m, l = (part.astype(f32) for part in split3(values))
+    return jnp.concatenate([h, m, h, m, l, h] + extra, axis=0).astype(bf16)
+
+
+def eight_rows(rows, columns):
+    index = lax.broadcasted_iota(jnp.int32, (8, columns), 0)
+    out = jnp.zeros((8, columns), f32)
+    for k, row in enumerate(rows):
+        out = jnp.where(index == k, row, out)
+    return [out, jnp.zeros((8, columns), f32)]
+
+
+def three(values):
+    return [part.astype(f32) for part in split3(values)]
+
+
+def feature_tile(points, omega, phase, total):
+    turn = 1.0 / (2.0 * math.pi)
+    ones = [1.0] * 3
+    left = left_stack(points, eight_rows(ones, points.shape[1]))
+    right = right_stack(omega * turn, eight_rows(three(phase * turn), omega.shape[1]))
+    turns = lax.dot_general(
+        left.astype(f32).T.astype(bf16), right, (((1,), (0,)), ((), ())), preferred_element_type=f32
+    )
+    rest = turns - jnp.floor(turns + 0.5)
+    square = rest * rest
+    scale = math.sqrt(2.0 / total)
+    value = jnp.full(square.shape, COS[-1] * scale, f32)
+    for coefficient in COS[-2::-1]:
+        value = value * square + coefficient * scale
+    return value.astype(bf16)
+
+
+def prior_kernel(which, x_ref, omega_ref, phase_ref, weights_ref, targets_ref, noise_ref, out_ref):
+    half = weights_ref.shape[1]
+    start = pl.multiple_of(which[0] * half, 128)
+    feats = feature_tile(
+        x_ref[...], omega_ref[:, pl.ds(start, half)], phase_ref[:, pl.ds(start, half)], omega_ref.shape[1]
+    )
+    prior = lax.dot_general(weights_ref[...], feats, (((1,), (1,)), ((), ())), preferred_element_type=f32)
+    own = targets_ref[...] - noise_ref[...].T
+    copies = out_ref.shape[1] // own.shape[1]
+    lane = lax.broadcasted_iota(jnp.int32, out_ref.shape, 1)
+    here = lane // own.shape[1] == which[0]
+    out_ref[...] = jnp.where(here, jnp.concatenate([own] * copies, axis=1), 0.0) - prior
+
+
+def pack_kernel(mine_ref, other_ref, x_ref, payload_ref):
+    samples = mine_ref.shape[0]
+    payload_ref[:samples, :] = mine_ref[...] + other_ref[...]
+    payload_ref[samples:, :] = x_ref[...]
+
+
+def cand_kernel(which, x_ref, omega_ref, phase_ref, mine_ref, other_ref, out_ref):
+    half = mine_ref.shape[1]
+    total = omega_ref.shape[1]
+    here = pl.multiple_of(which[0] * half, 128)
+    there = pl.multiple_of((1 - which[0]) * half, 128)
+    out = None
+    for start, weights in ((here, mine_ref), (there, other_ref)):
+        feats = feature_tile(x_ref[...], omega_ref[:, pl.ds(start, half)], phase_ref[:, pl.ds(start, half)], total)
+        part = lax.dot_general(feats, weights[...], (((1,), (1,)), ((), ())), preferred_element_type=f32)
+        out = part if out is None else out + part
+    out_ref[...] = out
+
+
+def solve_kernel(
+    own_rows, which, gathered_ref, cand_ref, prior_ref, samples_ref, solution_ref,
+    field_ref, first_ref, rhs_ref, left_ref, right_ref, kernel_ref,
+):
+    blocks, _, width = gathered_ref.shape
+    samples = prior_ref.shape[1]
+    count = blocks * width
+    points = []
+    for k in range(blocks):
+        columns = pl.ds(k * width, width)
+        rhs_ref[:, columns] = gathered_ref[k, :samples, :]
+        first_ref[:, columns] = gathered_ref[k, :samples, :].astype(bf16)
+        points.append(gathered_ref[k, samples:, :])
+    points = jnp.concatenate(points, axis=1)
+    ones = [1.0] * 3
+    halves = three((-0.5 * LOG2E) * jnp.sum(points * points, axis=0, keepdims=True))
+    right_ref[...] = right_stack(points, eight_rows(ones + halves, count))
+    left = left_stack(points * LOG2E, eight_rows(halves + ones, count))
+    left_ref[...] = left.astype(f32).T.astype(bf16)
+
+    size = min(256, count)
+    wide = min(512, count)
+    field_ref[...] = jnp.zeros_like(field_ref)
+
+    def panel(i, carry):
+        rows = pl.ds(pl.multiple_of(i * size, size), size)
+        lhs = left_ref[rows, :]
+        for j in range(0, count, wide):
+            exponent = jnp.dot(lhs, right_ref[:, j : j + wide], preferred_element_type=f32)
+            tile = jnp.exp2(exponent).astype(bf16)
+            kernel_ref[rows, j : j + wide] = tile
+            field_ref[:, j : j + wide] += jnp.dot(
+                first_ref[:, rows], tile, preferred_element_type=f32
+            )
+        return carry
+
+    lax.fori_loop(0, count // size, panel, 0)
+
+    def total(values):
+        return jnp.sum(values, axis=1, keepdims=True)
+
+    start = rhs_ref[...]
+    image = field_ref[...] + noise_level * start
+    norm0 = total(start * start)
+    alpha0 = norm0 / total(start * image)
+    residual = start - alpha0 * image
+    norm1 = total(residual * residual)
+    beta = norm1 / norm0
+    direction = residual + beta * start
+    packed = direction.astype(bf16)
+    second = jnp.dot(packed, kernel_ref[...], preferred_element_type=f32) + noise_level * direction
+    alpha1 = norm1 / total(direction * second)
+    field = alpha0 * start + alpha1 * direction
+    weights = field.astype(bf16)
+    own_solution = field[:, :width].T
+    solution_ref[...] = jnp.where(which[0] == 0, own_solution[:own_rows], own_solution[own_rows:])
+
+    cand = cand_ref[...]
+    cand_halves = three((-0.5 * LOG2E) * jnp.sum(cand * cand, axis=0, keepdims=True))
+    lhs = left_stack(cand * LOG2E, eight_rows(cand_halves + ones, cand.shape[1]))
+    exponent = jnp.dot(lhs.astype(f32).T.astype(bf16), right_ref[...], preferred_element_type=f32)
+    tile = jnp.exp2(exponent).astype(bf16)
+    samples_ref[...] = prior_ref[...] + lax.dot_general(
+        tile, weights, (((1,), (1,)), ((), ())), preferred_element_type=f32
+    )
+
+
+def call(kernel, out_shape, scratch=(), scalars=0, inputs=0, flops=0, transcendentals=0):
+    vmem = pl.BlockSpec(memory_space=pltpu.VMEM)
+    smem = pl.BlockSpec(memory_space=pltpu.SMEM)
+    outs = jax.tree.map(lambda _: vmem, out_shape)
+    return pl.pallas_call(
+        kernel,
+        out_shape=out_shape,
+        in_specs=[smem] * scalars + [vmem] * inputs,
+        out_specs=outs,
+        scratch_shapes=list(scratch),
+        cost_estimate=pl.CostEstimate(flops=flops, transcendentals=transcendentals, bytes_accessed=1 << 20),
+        compiler_params=pltpu.CompilerParams(vmem_limit_bytes=48 << 20),
+    )
+
+
+def local_body(x_train, x_cand, targets, noise, omega, phase, prior_weights):
+    own_rows, samples = noise.shape
+    dim, width = x_train.shape
+    blocks = lax.axis_size("train")
+    count = blocks * width
+    cand_index = lax.axis_index("cand")
+    train_index = lax.axis_index("train")
+    which = cand_index.astype(jnp.int32).reshape(1)
+    phase = phase.reshape(1, -1)
+    swap = [(0, 1), (1, 0)]
+    weights = prior_weights.T
+    partial = call(
+        prior_kernel,
+        jax.ShapeDtypeStruct((samples, width), f32),
+        scalars=1, inputs=6, flops=1 << 30,
+    )(which, x_train, omega, phase, weights, targets.reshape(1, -1), noise)
+    other = lax.ppermute(partial, "cand", swap)
+    payload = call(
+        pack_kernel, jax.ShapeDtypeStruct((samples + dim, width), f32), inputs=3
+    )(partial, other, x_train)
+    payload, late_weights = lax.optimization_barrier((payload, weights))
+    other_weights = lax.ppermute(late_weights, "cand", swap)
+    gathered = payload[None]
+    bit = blocks // 2
+    while bit:
+        moved = lax.ppermute(gathered, "train", [(i, i ^ bit) for i in range(blocks)])
+        gathered = jnp.concatenate([gathered, moved], axis=0)
+        bit //= 2
+    per_device = x_cand.shape[1] // blocks
+    mine = lax.dynamic_slice_in_dim(x_cand, train_index * per_device, per_device, 1)
+    prior_cand = call(
+        cand_kernel, jax.ShapeDtypeStruct((per_device, samples), f32), scalars=1, inputs=5, flops=1 << 30
+    )(which, mine, omega, phase, weights, other_weights)
+    stack = 6 * dim + 16
+    return tuple(
+        call(
+            functools.partial(solve_kernel, own_rows),
+            (
+                jax.ShapeDtypeStruct((per_device, samples), f32),
+                jax.ShapeDtypeStruct((own_rows, samples), f32),
+            ),
+            scratch=[
+                pltpu.VMEM((samples, count), f32),
+                pltpu.VMEM((samples, count), bf16),
+                pltpu.VMEM((samples, count), f32),
+                pltpu.VMEM((count, stack), bf16),
+                pltpu.VMEM((stack, count), bf16),
+                pltpu.VMEM((count, count), bf16),
+            ],
+            scalars=1, inputs=3, flops=1 << 34,
+        )(which, gathered, mine, prior_cand)
+    )
+
+
+def is_local(mesh, x_train):
+    train, cand = mesh.shape["train"], mesh.shape["cand"]
+    count = x_train.shape[1]
+    return cand == 2 and train & (train - 1) == 0 and 2 * count * count <= KERNEL_BYTES
 
 
 def squares_of(points):
@@ -111,10 +349,17 @@
         P(),
         P("cand", None),
     )
-    return jax.shard_map(
-        body,
-        mesh=mesh,
-        in_specs=placed,
-        out_specs=(P(("cand", "train"), None), P(("train", "cand"), None)),
-        check_vma=False,
-    )
+    def sharded(chosen):
+        return jax.shard_map(
+            chosen,
+            mesh=mesh,
+            in_specs=placed,
+            out_specs=(P(("cand", "train"), None), P(("train", "cand"), None)),
+            check_vma=False,
+        )
+
+    def step(x_train, *rest):
+        chosen = local_body if is_local(mesh, x_train) else body
+        return sharded(chosen)(x_train, *rest)
+
+    return step

time: 297 us -> 40.5 us (0.14)
  blocking collectives: 197 us -> 0 us
  waiting for transfers between devices: 67.3 us -> 10.9 us
  matrix products: 13.6 us -> 0 us
  between operations: 13.9 us -> 0.74 us
  Pallas kernels: 0 us -> 12.7 us
  starting transfers between devices: 0.12 us -> 11.5 us
  other arithmetic: 3.1 us -> 0.04 us
    psum x3 -> x0, blocking collectives: 120 us -> none  [the longest x2 80.3 us: squares(): return lax.psum(jnp.sum(values * values, axis=0), ('train', 'cand'))]
    all_gather x5 -> x0, blocking collectives: 76.9 us -> none  [the longest x2 40 us: body(): piece = lax.all_gather(packed, 'train', axis=0, tiled=True)]
    reduce_scatter x3 -> x0, waiting for transfers between devices: 67.3 us -> none  [the longest x1 53.7 us: body(): lax.psum_scatter(kernel_rows(x_cand, x_train, train_norms, block_weights)...]
    dot_general x9 -> x0, matrix products: 13.6 us -> none  [the longest x2 7.44 us: features(): jnp.dot(points.T, omega, precision=lax.Precision.HIGHEST) + phase[None, :]]
    pallas_call x0 -> x4, Pallas kernels: none -> 12.7 us  [the longest x1 11.1 us: local_body(): call(functools.partial(solve_kernel, own_rows), (jax.ShapeDtypeStruct((pe...]
    ppermute x0 -> x6, starting transfers between devices: none -> 11.5 us  [the longest x4 7.01 us: local_body(): lax.ppermute(gathered, 'train', [(i, i ^ bit) for i in range(blocks)])]
    ppermute x0 -> x6, waiting for transfers between devices: none -> 10.9 us  [the longest x4 6.11 us: local_body(): lax.ppermute(gathered, 'train', [(i, i ^ bit) for i in range(blocks)])]
  transfers between devices with their start and end apart: 3 -> 6, of which waited for: 3 -> 5; matrix products, arithmetic and copies ran while one was open for 1% -> 0% of each run, Pallas kernels for 0% -> 2%
where the time goes in v1:
time: 40.5 us; the launch traced here: 40.2 us
  Pallas kernels  12.7 us (31%)
  starting transfers between devices  11.5 us (28%)
  waiting for transfers between devices  10.9 us (27%)
  local copies, waits for them, and re-layouts  4.17 us (10%)
  between operations  0.74 us (2%)
    pallas_call x1, Pallas kernels, local_body(): call(functools.partial(solve_kernel, own_rows), (jax.ShapeDtypeStruct((pe...  11.1 us
    ppermute x4, starting transfers between devices, local_body(): lax.ppermute(gathered, 'train', [(i, i ^ bit) for i in range(blocks)])  7.01 us
    ppermute x4, waiting for transfers between devices, local_body(): lax.ppermute(gathered, 'train', [(i, i ^ bit) for i in range(blocks)])  6.11 us
    unnamed x24, local copies, waits for them, and re-layouts  4.06 us
    ppermute x1, starting transfers between devices, local_body(): other = lax.ppermute(partial, 'cand', swap)  3.03 us
    ppermute x1, waiting for transfers between devices, local_body(): other_weights = lax.ppermute(late_weights, 'cand', swap)  2.92 us
    ppermute x1, waiting for transfers between devices, local_body(): other = lax.ppermute(partial, 'cand', swap)  1.89 us
    ppermute x1, starting transfers between devices, local_body(): other_weights = lax.ppermute(late_weights, 'cand', swap)  1.49 us
  transfers between devices with their start and end apart: 6, of which 5 were waited for; matrix products, arithmetic and copies ran while one was open for 0% of the time, Pallas kernels for 2%

profile of v1, /device:TPU:0, one launch (start us, length us, event | category | flops | bytes accessed | tf_op | source)
XLA Modules:
  0.0 40.2 jit_solution(2030974436392630328)
XLA Ops:
  0.6 0.0 copy-start
  0.7 0.0 copy-start.1
  0.7 0.0 copy-start.9
  0.7 0.7 %copy-done.1 = f32[8,128]{1,0:T(8,128)S(1)} copy-done((f32[8,128]{1,0:T(8,128)S(1)}, f32[8,128]{1,0:T(8,128)}, u32[]{:S(2)}) %copy-start.1) | copy-done | bytes 4120
  1.3 0.0 copy-done.9
  1.3 0.0 copy-start.2
  1.3 0.9 %copy-done.2 = bf16[2048,64]{0,1:T(8,128)(2,1)S(1)} copy-done((bf16[2048,64]{0,1:T(8,128)(2,1)S(1)}, bf16[2048,64]{0,1:T(8,128)(2,1)}, u32[]{:S(2)}) %copy-start.2) | copy-done | bytes 262168
  2.3 0.9 %copy-done.4 = f32[8,4096]{1,0:T(8,128)S(1)} copy-done((f32[8,4096]{1,0:T(8,128)S(1)}, f32[8,4096]{1,0:T(8,128)}, u32[]{:S(2)}) %copy-start.4) | copy-done | bytes 131096
  3.2 0.8 %copy-done.6 = f32[64,64]{1,0:T(8,128)S(1)} copy-done((f32[64,64]{1,0:T(8,128)S(1)}, f32[64,64]{1,0:T(8,128)}, u32[]{:S(2)}) %copy-start.6) | copy-done | bytes 16408
  4.0 0.7 %copy-done.7 = f32[4096]{0:T(1024)S(1)} copy-done((f32[4096]{0:T(1024)S(1)}, f32[4096]{0:T(1024)}, u32[]{:S(2)}) %copy-start.7) | copy-done | bytes 16408
  4.7 1.0 %shard_map.86.mine_ref = f32[64,128]{1,0:T(8,128)S(1)} custom-call(s32[1]{0:T(128)} %bitcast.which, f32[8,128]{1,0:T(8,128)S(1)} %copy-done.1, f32[8,4096]{1,0:T(8,128)S(1)} %copy-done.4, f32[1,4096]{1,0:T(1,128)S(1)} %bitcast.13, bf16[64,2048]{1,0:T(8,128)(2,1)S(1)} %bitcast.10, f32[1,64]{1,0:T(1,128)S(1)} %bitcast.15, f32[64,64]{1,0:T(8,128)S(1)} %copy-done.6), custom_call_target="tpu_custom_call" | custom-call | flops 1073741824 | bytes 1048576 | tf_op jit(solution)/shard_map/pallas_call | solution.py:203
  5.7 3.0 %collective-permute-start = (f32[64,128]{1,0:T(8,128)S(1)}, f32[64,128]{1,0:T(8,128)S(1)}, u32[]{:S(2)}, u32[]{:S(2)}) collective-permute-start(f32[64,128]{1,0:T(8,128)S(1)} %shard_map.86.mine_ref), channel_id=1, source_target_pairs={{0,1},{1,0},{2,3},{3,2},{4,5},{5,4},{6,7},{7,6},{8,9},{9,8},{10,11... | collective-permute-start | bytes 98312 | tf_op jit(solution)/shard_map/ppermute | solution.py:208
  8.7 1.9 %collective-permute-done.other_ref = f32[64,128]{1,0:T(8,128)S(1)} collective-permute-done((f32[64,128]{1,0:T(8,128)S(1)}, f32[64,128]{1,0:T(8,128)S(1)}, u32[]{:S(2)}, u32[]{:S(2)}) %collective-permute-start) | collective-permute-done | bytes 32800 | tf_op jit(solution)/shard_map/ppermute | solution.py:208
  10.6 3.1 %collective-permute-start.1 = (f32[1,72,128]{2,1,0:T(8,128)S(1)}, f32[1,72,128]{2,1,0:T(8,128)S(1)}, u32[]{:S(2)}, u32[]{:S(2)}) collective-permute-start(f32[1,72,128]{2,1,0:T(8,128)S(1)} %bitcast.6), channel_id=1, source_target_pairs={{0,16},{2,18},{4,20},{6,22},{8,24},{10,26},{12,28},{14,30},{16,0},... | collective-permute-start | bytes 110600 | tf_op jit(solution)/shard_map/ppermute | solution.py:217
  13.7 1.9 %collective-permute-done.1 = f32[1,72,128]{2,1,0:T(8,128)S(1)} collective-permute-done((f32[1,72,128]{2,1,0:T(8,128)S(1)}, f32[1,72,128]{2,1,0:T(8,128)S(1)}, u32[]{:S(2)}, u32[]{:S(2)}) %collective-permute-start.1) | collective-permute-done | bytes 36896 | tf_op jit(solution)/shard_map/ppermute | solution.py:217
  15.7 1.9 %collective-permute-start.2 = (f32[2,72,128]{2,1,0:T(8,128)S(1)}, f32[2,72,128]{2,1,0:T(8,128)S(1)}, u32[]{:S(2)}, u32[]{:S(2)}) collective-permute-start(f32[2,72,128]{2,1,0:T(8,128)S(1)} %pad_maximum_fusion.2), channel_id=1, source_target_pairs={{0,8},{2,10},{4,12},{6,14},{8,0},{10,2},{12,4},{14,6},{16,24},{18,... | collective-permute-start | bytes 221192 | tf_op jit(solution)/shard_map/ppermute | solution.py:217
  17.6 0.0 copy-done
  17.6 0.1 constant_dynamic-slice_fusion.x_ref.cand_ref
  17.6 2.4 %collective-permute-done.2 = f32[2,72,128]{2,1,0:T(8,128)S(1)} collective-permute-done((f32[2,72,128]{2,1,0:T(8,128)S(1)}, f32[2,72,128]{2,1,0:T(8,128)S(1)}, u32[]{:S(2)}, u32[]{:S(2)}) %collective-permute-start.2) | collective-permute-done | bytes 73760 | tf_op jit(solution)/shard_map/ppermute | solution.py:217
  20.0 1.9 %collective-permute-start.3 = (f32[4,72,128]{2,1,0:T(8,128)S(1)}, f32[4,72,128]{2,1,0:T(8,128)S(1)}, u32[]{:S(2)}, u32[]{:S(2)}) collective-permute-start(f32[4,72,128]{2,1,0:T(8,128)S(1)} %pad_maximum_fusion.1), channel_id=1, source_target_pairs={{0,4},{2,6},{4,0},{6,2},{8,12},{10,14},{12,8},{14,10},{16,20},{18,... | collective-permute-start | bytes 442376 | tf_op jit(solution)/shard_map/ppermute | solution.py:217
  22.0 0.0 copy-done.3
  22.0 1.5 %collective-permute-start.5 = (bf16[64,2048]{1,0:T(8,128)(2,1)S(1)}, bf16[64,2048]{1,0:T(8,128)(2,1)S(1)}, u32[]{:S(2)}, u32[]{:S(2)}) collective-permute-start(bf16[64,2048]{1,0:T(8,128)(2,1)S(1)} %bitcast.11), channel_id=1, source_target_pairs={{0,1},{1,0},{2,3},{3,2},{4,5},{5,4},{6,7},{7,6},{8,9},{9,8},{10,11... | collective-permute-start | bytes 786440 | tf_op jit(solution)/shard_map/ppermute | solution.py:213
  23.4 1.8 %collective-permute-done.3 = f32[4,72,128]{2,1,0:T(8,128)S(1)} collective-permute-done((f32[4,72,128]{2,1,0:T(8,128)S(1)}, f32[4,72,128]{2,1,0:T(8,128)S(1)}, u32[]{:S(2)}, u32[]{:S(2)}) %collective-permute-start.3) | collective-permute-done | bytes 147488 | tf_op jit(solution)/shard_map/ppermute | solution.py:217
  25.3 0.1 collective-permute-start.4
  25.4 0.0 copy-start.5
  25.4 0.0 copy-start.8
  25.4 2.9 %collective-permute-done.5.other_ref = bf16[64,2048]{1,0:T(8,128)(2,1)S(1)} collective-permute-done((bf16[64,2048]{1,0:T(8,128)(2,1)S(1)}, bf16[64,2048]{1,0:T(8,128)(2,1)S(1)}, u32[]{:S(2)}, u32[]{:S(2)}) %collective-permute-start.5) | collective-permute-done | bytes 262176 | tf_op jit(solution)/shard_map/ppermute | solution.py:213
  28.3 0.0 copy-done.5
  28.3 0.0 copy-done.8
  28.3 0.6 %shard_map.88.prior_ref = f32[32,64]{1,0:T(8,128)S(1)} custom-call(s32[1]{0:T(128)} %bitcast.which, f32[8,32]{1,0:T(8,128)S(1)} %constant_dynamic-slice_fusion.x_ref.cand_ref, f32[8,4096]{1,0:T(8,128)S(1)} %copy-done.5, f32[1,4096]{1,0:T(1,128)S(1)} %bitcast.14, bf16[64,2048]{1,0:T(8,128)(2,1)S(1)} %bitcast.12, ...), custom_call_target="tpu_custom_call" | custom-call | flops 1073741824 | bytes 1048576 | tf_op jit(solution)/shard_map/pallas_call | solution.py:222
  29.0 0.0 collective-permute-done.4
  29.0 11.1 %shard_map.89 = (f32[32,64]{1,0:T(8,128)}, f32[64,64]{1,0:T(8,128)}) custom-call(s32[1]{0:T(128)} %bitcast.which, f32[16,72,128]{2,1,0:T(8,128)S(1)} %constant_dynamic-update-slice_fusion.gathered_ref, f32[8,32]{1,0:T(8,128)S(1)} %constant_dynamic-slice_fusion.x_ref.cand_ref, f32[32,64]{1,0:T(8,128)S(1)} %shard_map.88.prior_ref), custom_call_target="tpu_custom_call" | custom-call | flops 17179869184 | bytes 1048576 | tf_op jit(solution)/shard_map/pallas_call | solution.py:227
  (13 shorter events, 0.1 us)
Async XLA Ops:
  0.6 16.9 %copy-start = (f32[8,512]{1,0:T(8,128)S(1)}, f32[8,512]{1,0:T(8,128)}, u32[]{:S(2)}) copy-start(f32[8,512]{1,0:T(8,128)} %param.8) | copy-start | bytes 49156
  0.7 0.7 %copy-start.1 = (f32[8,128]{1,0:T(8,128)S(1)}, f32[8,128]{1,0:T(8,128)}, u32[]{:S(2)}) copy-start(f32[8,128]{1,0:T(8,128)} %x_ref.3) | copy-start | bytes 12292
  0.7 0.7 %copy-start.9 = (f32[64]{0:T(128)S(1)}, f32[64]{0:T(128)}, u32[]{:S(2)}) copy-start(f32[64]{0:T(128)} %param.9) | copy-start | bytes 772
  1.3 1.0 %copy-start.2 = (bf16[2048,64]{0,1:T(8,128)(2,1)S(1)}, bf16[2048,64]{0,1:T(8,128)(2,1)}, u32[]{:S(2)}) copy-start(bf16[2048,64]{0,1:T(8,128)(2,1)} %param.13) | copy-start | bytes 786436
  2.3 0.9 %copy-start.4 = (f32[8,4096]{1,0:T(8,128)S(1)}, f32[8,4096]{1,0:T(8,128)}, u32[]{:S(2)}) copy-start(f32[8,4096]{1,0:T(8,128)} %omega_ref.3) | copy-start | bytes 393220
  3.2 0.8 %copy-start.6 = (f32[64,64]{1,0:T(8,128)S(1)}, f32[64,64]{1,0:T(8,128)}, u32[]{:S(2)}) copy-start(f32[64,64]{1,0:T(8,128)} %noise_ref.1) | copy-start | bytes 49156
  4.0 0.7 %copy-start.7 = (f32[4096]{0:T(1024)S(1)}, f32[4096]{0:T(1024)}, u32[]{:S(2)}) copy-start(f32[4096]{0:T(1024)} %param.12) | copy-start | bytes 49156
  5.7 4.9 %collective-permute-start = (f32[64,128]{1,0:T(8,128)S(1)}, f32[64,128]{1,0:T(8,128)S(1)}, u32[]{:S(2)}, u32[]{:S(2)}) collective-permute-start(f32[64,128]{1,0:T(8,128)S(1)} %shard_map.86.mine_ref), channel_id=1, source_target_pairs={{0,1},{1,0},{2,3},{3,2},{4,5},{5,4},{6,7},{7,6},{8,9},{9,8},{10,11... | collective-permute-start | bytes 98312 | tf_op jit(solution)/shard_map/ppermute | solution.py:208
  10.6 5.1 %collective-permute-start.1 = (f32[1,72,128]{2,1,0:T(8,128)S(1)}, f32[1,72,128]{2,1,0:T(8,128)S(1)}, u32[]{:S(2)}, u32[]{:S(2)}) collective-permute-start(f32[1,72,128]{2,1,0:T(8,128)S(1)} %bitcast.6), channel_id=1, source_target_pairs={{0,16},{2,18},{4,20},{6,22},{8,24},{10,26},{12,28},{14,30},{16,0},... | collective-permute-start | bytes 110600 | tf_op jit(solution)/shard_map/ppermute | solution.py:217
  13.7 8.2 %copy-start.3 = (bf16[2048,64]{0,1:T(8,128)(2,1)S(1)}, bf16[2048,64]{0,1:T(8,128)(2,1)}, u32[]{:S(2)}) copy-start(bf16[2048,64]{0,1:T(8,128)(2,1)} %param.13) | copy-start | bytes 786436
  15.7 4.4 %collective-permute-start.2 = (f32[2,72,128]{2,1,0:T(8,128)S(1)}, f32[2,72,128]{2,1,0:T(8,128)S(1)}, u32[]{:S(2)}, u32[]{:S(2)}) collective-permute-start(f32[2,72,128]{2,1,0:T(8,128)S(1)} %pad_maximum_fusion.2), channel_id=1, source_target_pairs={{0,8},{2,10},{4,12},{6,14},{8,0},{10,2},{12,4},{14,6},{16,24},{18,... | collective-permute-start | bytes 221192 | tf_op jit(solution)/shard_map/ppermute | solution.py:217
  20.0 5.2 %collective-permute-start.3 = (f32[4,72,128]{2,1,0:T(8,128)S(1)}, f32[4,72,128]{2,1,0:T(8,128)S(1)}, u32[]{:S(2)}, u32[]{:S(2)}) collective-permute-start(f32[4,72,128]{2,1,0:T(8,128)S(1)} %pad_maximum_fusion.1), channel_id=1, source_target_pairs={{0,4},{2,6},{4,0},{6,2},{8,12},{10,14},{12,8},{14,10},{16,20},{18,... | collective-permute-start | bytes 442376 | tf_op jit(solution)/shard_map/ppermute | solution.py:217
  22.0 6.4 %collective-permute-start.5 = (bf16[64,2048]{1,0:T(8,128)(2,1)S(1)}, bf16[64,2048]{1,0:T(8,128)(2,1)S(1)}, u32[]{:S(2)}, u32[]{:S(2)}) collective-permute-start(bf16[64,2048]{1,0:T(8,128)(2,1)S(1)} %bitcast.11), channel_id=1, source_target_pairs={{0,1},{1,0},{2,3},{3,2},{4,5},{5,4},{6,7},{7,6},{8,9},{9,8},{10,11... | collective-permute-start | bytes 786440 | tf_op jit(solution)/shard_map/ppermute | solution.py:213
  25.3 3.7 %collective-permute-start.4 = (f32[8,72,128]{2,1,0:T(8,128)S(1)}, f32[8,72,128]{2,1,0:T(8,128)S(1)}, u32[]{:S(2)}, u32[]{:S(2)}) collective-permute-start(f32[8,72,128]{2,1,0:T(8,128)S(1)} %pad_maximum_fusion), channel_id=1, source_target_pairs={{0,2},{2,0},{4,6},{6,4},{8,10},{10,8},{12,14},{14,12},{16,18},{18,... | collective-permute-start | bytes 884744 | tf_op jit(solution)/shard_map/ppermute | solution.py:217
  25.4 3.0 %copy-start.5 = (f32[8,4096]{1,0:T(8,128)S(1)}, f32[8,4096]{1,0:T(8,128)}, u32[]{:S(2)}) copy-start(f32[8,4096]{1,0:T(8,128)} %omega_ref.3) | copy-start | bytes 393220
  25.4 3.0 %copy-start.8 = (f32[4096]{0:T(1024)S(1)}, f32[4096]{0:T(1024)}, u32[]{:S(2)}) copy-start(f32[4096]{0:T(1024)} %param.12) | copy-start | bytes 49156

commit v2 on v1

--- a/solution.py
+++ b/solution.py
@@ -24,6 +24,7 @@
     -1.4529875517062139,
 )
 KERNEL_BYTES = 16 << 20
+TILE = 256
 f32, bf16 = jnp.float32, jnp.bfloat16
 
 
@@ -74,24 +75,43 @@
     return value.astype(bf16)
 
 
-def prior_kernel(which, x_ref, omega_ref, phase_ref, weights_ref, targets_ref, noise_ref, out_ref):
-    half = weights_ref.shape[1]
-    start = pl.multiple_of(which[0] * half, 128)
-    feats = feature_tile(
-        x_ref[...], omega_ref[:, pl.ds(start, half)], phase_ref[:, pl.ds(start, half)], omega_ref.shape[1]
-    )
+def prior_kernel(
+    which, x_hbm, omega_hbm, phase_hbm, weights_hbm, targets_hbm, noise_hbm, out_ref,
+    x_ref, omega_ref, phase_ref, weights_ref, targets_ref, noise_ref, arrived,
+):
+    half = weights_hbm.shape[1]
+    columns = pl.ds(pl.multiple_of(which[0] * half, 128), half)
+    copies = [
+        pltpu.make_async_copy(source, target, arrived.at[k])
+        for k, (source, target) in enumerate((
+            (x_hbm, x_ref),
+            (omega_hbm.at[:, columns], omega_ref),
+            (phase_hbm.at[:, columns], phase_ref),
+            (weights_hbm, weights_ref),
+            (targets_hbm, targets_ref),
+            (noise_hbm, noise_ref),
+        ))
+    ]
+    for copy in copies:
+        copy.start()
+    for copy in copies[:3]:
+        copy.wait()
+    feats = feature_tile(x_ref[...], omega_ref[...], phase_ref[...], omega_hbm.shape[1])
+    for copy in copies[3:]:
+        copy.wait()
     prior = lax.dot_general(weights_ref[...], feats, (((1,), (1,)), ((), ())), preferred_element_type=f32)
     own = targets_ref[...] - noise_ref[...].T
-    copies = out_ref.shape[1] // own.shape[1]
+    repeats = out_ref.shape[1] // own.shape[1]
     lane = lax.broadcasted_iota(jnp.int32, out_ref.shape, 1)
     here = lane // own.shape[1] == which[0]
-    out_ref[...] = jnp.where(here, jnp.concatenate([own] * copies, axis=1), 0.0) - prior
-
-
-def pack_kernel(mine_ref, other_ref, x_ref, payload_ref):
-    samples = mine_ref.shape[0]
+    out_ref[...] = jnp.where(here, jnp.concatenate([own] * repeats, axis=1), 0.0) - prior
+
+
+def pack_kernel(mine_ref, other_ref, x_ref, pair_ref, payload_ref):
+    samples, dim = mine_ref.shape[0], x_ref.shape[0]
     payload_ref[:samples, :] = mine_ref[...] + other_ref[...]
-    payload_ref[samples:, :] = x_ref[...]
+    payload_ref[samples : samples + dim, :] = x_ref[...]
+    payload_ref[samples + dim :, :] = pair_ref[...]
 
 
 def cand_kernel(which, x_ref, omega_ref, phase_ref, mine_ref, other_ref, out_ref):
@@ -107,85 +127,166 @@
     out_ref[...] = out
 
 
+def halves_of(points):
+    return three((-0.5 * LOG2E) * jnp.sum(points * points, axis=0, keepdims=True))
+
+
+def left_of(points):
+    stack = left_stack(points * LOG2E, eight_rows(halves_of(points) + [1.0] * 3, points.shape[1]))
+    return stack.astype(f32).T.astype(bf16)
+
+
+def right_of(points):
+    return right_stack(points, eight_rows([1.0] * 3 + halves_of(points), points.shape[1]))
+
+
+def fill(out_ref, left_ref, right_ref):
+    rows, columns = out_ref.shape
+    for i in range(0, rows, TILE):
+        for j in range(0, columns, TILE):
+            height, width = min(TILE, rows - i), min(TILE, columns - j)
+            exponent = jnp.dot(
+                left_ref[i : i + height, :], right_ref[:, j : j + width], preferred_element_type=f32
+            )
+            out_ref[i : i + height, j : j + width] = jnp.exp2(exponent).astype(bf16)
+
+
+def points_of(block_ref, samples):
+    dim = (block_ref.shape[1] - samples) // 2
+    return jnp.concatenate(
+        [block_ref[k, samples : samples + dim, :] for k in range(block_ref.shape[0])]
+        + [block_ref[k, samples + dim :, :] for k in range(block_ref.shape[0])],
+        axis=1,
+    )
+
+
+def rows_of(block_ref, samples, first=0, last=None):
+    last = block_ref.shape[0] if last is None else last
+    return jnp.concatenate([block_ref[k, :samples, :] for k in range(first, last)], axis=1)
+
+
+def near_kernel(block_ref, cand_ref, left_ref, right_ref, cand_left_ref, kernel_ref, tile_ref):
+    samples = block_ref.shape[1] - 2 * cand_ref.shape[0]
+    points = points_of(block_ref, samples)
+    left_ref[...] = left_of(points)
+    right_ref[...] = right_of(points)
+    cand_left_ref[...] = left_of(cand_ref[...])
+    fill(kernel_ref, left_ref, right_ref)
+    fill(tile_ref, cand_left_ref, right_ref)
+
+
+def far_kernel(
+    block_ref, near_ref, left_ref, right_ref, cand_left_ref, kernel_ref,
+    near_far_ref, far_near_ref, far_far_ref, tile_ref, field_ref,
+    far_left_ref, far_right_ref,
+):
+    samples = field_ref.shape[0]
+    points = points_of(block_ref, samples)
+    far_left_ref[...] = left_of(points)
+    far_right_ref[...] = right_of(points)
+    fill(near_far_ref, left_ref, far_right_ref)
+    fill(far_near_ref, far_left_ref, right_ref)
+    fill(far_far_ref, far_left_ref, far_right_ref)
+    fill(tile_ref, cand_left_ref, far_right_ref)
+    add_field(
+        field_ref, None, slice(0, points.shape[1] // 2),
+        rows_of(near_ref, samples).astype(bf16), rows_of(block_ref, samples).astype(bf16),
+        kernel_ref, near_far_ref, far_near_ref, far_far_ref,
+    )
+
+
+def add_field(field_ref, before_ref, rows, near, far, near_near, near_far, far_near, far_far):
+    count = near_near.shape[0]
+    for j in range(0, count, TILE):
+        for offset, first, second in ((0, near_near, far_near), (count, near_far, far_far)):
+            width = min(TILE, count - j)
+            columns = slice(offset + j, offset + j + width)
+            value = jnp.dot(near, first[rows, j : j + width], preferred_element_type=f32)
+            value += jnp.dot(far, second[rows, j : j + width], preferred_element_type=f32)
+            if before_ref is not None:
+                value += before_ref[:, columns]
+            field_ref[:, columns] = value
+
+
 def solve_kernel(
-    own_rows, which, gathered_ref, cand_ref, prior_ref, samples_ref, solution_ref,
-    field_ref, first_ref, rhs_ref, left_ref, right_ref, kernel_ref,
+    own_rows, which, near_ref, far_ref, other_ref, before_ref,
+    near_near_ref, near_far_ref, far_near_ref, far_far_ref,
+    near_tile_ref, far_tile_ref, prior_ref, samples_ref, solution_ref,
+    field_ref, start_ref, direction_ref, packed_ref,
 ):
-    blocks, _, width = gathered_ref.shape
     samples = prior_ref.shape[1]
-    count = blocks * width
-    points = []
-    for k in range(blocks):
-        columns = pl.ds(k * width, width)
-        rhs_ref[:, columns] = gathered_ref[k, :samples, :]
-        first_ref[:, columns] = gathered_ref[k, :samples, :].astype(bf16)
-        points.append(gathered_ref[k, samples:, :])
-    points = jnp.concatenate(points, axis=1)
-    ones = [1.0] * 3
-    halves = three((-0.5 * LOG2E) * jnp.sum(points * points, axis=0, keepdims=True))
-    right_ref[...] = right_stack(points, eight_rows(ones + halves, count))
-    left = left_stack(points * LOG2E, eight_rows(halves + ones, count))
-    left_ref[...] = left.astype(f32).T.astype(bf16)
-
-    size = min(256, count)
-    wide = min(512, count)
-    field_ref[...] = jnp.zeros_like(field_ref)
-
-    def panel(i, carry):
-        rows = pl.ds(pl.multiple_of(i * size, size), size)
-        lhs = left_ref[rows, :]
-        for j in range(0, count, wide):
-            exponent = jnp.dot(lhs, right_ref[:, j : j + wide], preferred_element_type=f32)
-            tile = jnp.exp2(exponent).astype(bf16)
-            kernel_ref[rows, j : j + wide] = tile
-            field_ref[:, j : j + wide] += jnp.dot(
-                first_ref[:, rows], tile, preferred_element_type=f32
-            )
-        return carry
-
-    lax.fori_loop(0, count // size, panel, 0)
+    blocks, _, width = near_ref.shape
+    half = blocks * width
+    count = 2 * half
+    near_other = rows_of(other_ref, samples, 0, blocks)
+    far_other = rows_of(other_ref, samples, blocks, 2 * blocks)
+    add_field(
+        field_ref, before_ref, slice(half, count), near_other.astype(bf16), far_other.astype(bf16),
+        near_near_ref, near_far_ref, far_near_ref, far_far_ref,
+    )
+    start_ref[:, :half] = rows_of(near_ref, samples)
+    start_ref[:, half:count] = near_other
+    start_ref[:, count : count + half] = rows_of(far_ref, samples)
+    start_ref[:, count + half :] = far_other
 
     def total(values):
         return jnp.sum(values, axis=1, keepdims=True)
 
-    start = rhs_ref[...]
+    start = start_ref[...]
     image = field_ref[...] + noise_level * start
     norm0 = total(start * start)
     alpha0 = norm0 / total(start * image)
     residual = start - alpha0 * image
     norm1 = total(residual * residual)
-    beta = norm1 / norm0
-    direction = residual + beta * start
-    packed = direction.astype(bf16)
-    second = jnp.dot(packed, kernel_ref[...], preferred_element_type=f32) + noise_level * direction
-    alpha1 = norm1 / total(direction * second)
-    field = alpha0 * start + alpha1 * direction
+    direction = residual + (norm1 / norm0) * start
+    direction_ref[...] = direction
+    packed_ref[...] = direction.astype(bf16)
+
+    curve = jnp.zeros((samples, min(TILE, count)), f32)
+    for j in range(0, 2 * count, TILE):
+        columns = slice(j, j + TILE)
+        offset = j % count
+        diagonal, above = (near_near_ref, None) if j < count else (far_far_ref, near_far_ref)
+        value = jnp.zeros((samples, TILE), f32)
+        if above is not None:
+            value += jnp.dot(
+                packed_ref[:, :count], above[:, offset : offset + TILE], preferred_element_type=f32
+            )
+        if offset:
+            value += jnp.dot(
+                packed_ref[:, j - offset : j], diagonal[:offset, offset : offset + TILE],
+                preferred_element_type=f32,
+            )
+        value = 2.0 * value + jnp.dot(
+            packed_ref[:, columns], diagonal[offset : offset + TILE, offset : offset + TILE],
+            preferred_element_type=f32,
+        )
+        curve += direction_ref[:, columns] * (value + noise_level * direction_ref[:, columns])
+    alpha1 = norm1 / total(curve)
+    field = alpha0 * start_ref[...] + alpha1 * direction_ref[...]
     weights = field.astype(bf16)
     own_solution = field[:, :width].T
     solution_ref[...] = jnp.where(which[0] == 0, own_solution[:own_rows], own_solution[own_rows:])
-
-    cand = cand_ref[...]
-    cand_halves = three((-0.5 * LOG2E) * jnp.sum(cand * cand, axis=0, keepdims=True))
-    lhs = left_stack(cand * LOG2E, eight_rows(cand_halves + ones, cand.shape[1]))
-    exponent = jnp.dot(lhs.astype(f32).T.astype(bf16), right_ref[...], preferred_element_type=f32)
-    tile = jnp.exp2(exponent).astype(bf16)
-    samples_ref[...] = prior_ref[...] + lax.dot_general(
-        tile, weights, (((1,), (1,)), ((), ())), preferred_element_type=f32
-    )
-
-
-def call(kernel, out_shape, scratch=(), scalars=0, inputs=0, flops=0, transcendentals=0):
+    last = (((1,), (1,)), ((), ()))
+    samples_ref[...] = (
+        prior_ref[...]
+        + lax.dot_general(near_tile_ref[...], weights[:, :count], last, preferred_element_type=f32)
+        + lax.dot_general(far_tile_ref[...], weights[:, count:], last, preferred_element_type=f32)
+    )
+
+
+def call(kernel, out_shape, inputs, scratch=(), scalars=0, hbm=False, flops=0):
     vmem = pl.BlockSpec(memory_space=pltpu.VMEM)
     smem = pl.BlockSpec(memory_space=pltpu.SMEM)
-    outs = jax.tree.map(lambda _: vmem, out_shape)
+    source = pl.BlockSpec(memory_space=pltpu.HBM) if hbm else vmem
     return pl.pallas_call(
         kernel,
         out_shape=out_shape,
-        in_specs=[smem] * scalars + [vmem] * inputs,
-        out_specs=outs,
+        in_specs=[smem] * scalars + [source] * inputs,
+        out_specs=jax.tree.map(lambda _: vmem, out_shape),
         scratch_shapes=list(scratch),
-        cost_estimate=pl.CostEstimate(flops=flops, transcendentals=transcendentals, bytes_accessed=1 << 20),
-        compiler_params=pltpu.CompilerParams(vmem_limit_bytes=48 << 20),
+        cost_estimate=pl.CostEstimate(flops=flops, transcendentals=0, bytes_accessed=1 << 20),
+        compiler_params=pltpu.CompilerParams(vmem_limit_bytes=16 << 20),
     )
 
 
@@ -193,60 +294,102 @@
     own_rows, samples = noise.shape
     dim, width = x_train.shape
     blocks = lax.axis_size("train")
-    count = blocks * width
     cand_index = lax.axis_index("cand")
     train_index = lax.axis_index("train")
     which = cand_index.astype(jnp.int32).reshape(1)
     phase = phase.reshape(1, -1)
+    weights = prior_weights.T
+    half_features = weights.shape[1]
+    shape = jax.ShapeDtypeStruct
     swap = [(0, 1), (1, 0)]
-    weights = prior_weights.T
+
+    def in_hbm(values):
+        return pltpu.with_memory_space_constraint(values, pltpu.HBM)
+
+    def exchange(values, bit):
+        return lax.ppermute(values, "train", [(i, i ^ bit) for i in range(blocks)])
+
+    pair = exchange(x_train, 1)
     partial = call(
         prior_kernel,
-        jax.ShapeDtypeStruct((samples, width), f32),
-        scalars=1, inputs=6, flops=1 << 30,
-    )(which, x_train, omega, phase, weights, targets.reshape(1, -1), noise)
+        shape((samples, width), f32),
+        scalars=1, inputs=6, hbm=True, flops=1 << 30,
+        scratch=[
+            pltpu.VMEM((dim, width), f32),
+            pltpu.VMEM((dim, half_features), f32),
+            pltpu.VMEM((1, half_features), f32),
+            pltpu.VMEM(weights.shape, bf16),
+            pltpu.VMEM((1, own_rows), f32),
+            pltpu.VMEM(noise.shape, f32),
+            pltpu.SemaphoreType.DMA((6,)),
+        ],
+    )(which, *map(in_hbm, (x_train, omega, phase, weights, targets.reshape(1, -1), noise)))
     other = lax.ppermute(partial, "cand", swap)
-    payload = call(
-        pack_kernel, jax.ShapeDtypeStruct((samples + dim, width), f32), inputs=3
-    )(partial, other, x_train)
+    payload = call(pack_kernel, shape((samples + 2 * dim, width), f32), inputs=4)(
+        partial, other, x_train, pair
+    )
     payload, late_weights = lax.optimization_barrier((payload, weights))
     other_weights = lax.ppermute(late_weights, "cand", swap)
-    gathered = payload[None]
+    near = payload[None]
     bit = blocks // 2
-    while bit:
-        moved = lax.ppermute(gathered, "train", [(i, i ^ bit) for i in range(blocks)])
-        gathered = jnp.concatenate([gathered, moved], axis=0)
+    while bit > 2:
+        near = jnp.concatenate([near, exchange(near, bit)], axis=0)
         bit //= 2
+    far = exchange(near, 2)
     per_device = x_cand.shape[1] // blocks
     mine = lax.dynamic_slice_in_dim(x_cand, train_index * per_device, per_device, 1)
-    prior_cand = call(
-        cand_kernel, jax.ShapeDtypeStruct((per_device, samples), f32), scalars=1, inputs=5, flops=1 << 30
-    )(which, mine, omega, phase, weights, other_weights)
+    prior_cand = call(cand_kernel, shape((per_device, samples), f32), scalars=1, inputs=5, flops=1 << 30)(
+        which, mine, omega, phase, weights, other_weights
+    )
+    count = blocks * width // 2
     stack = 6 * dim + 16
+    left, right, cand_left, near_near, near_tile = call(
+        near_kernel,
+        (
+            shape((count, stack), bf16),
+            shape((stack, count), bf16),
+            shape((per_device, stack), bf16),
+            shape((count, count), bf16),
+            shape((per_device, count), bf16),
+        ),
+        inputs=2, flops=1 << 31,
+    )(near, mine)
+    other = exchange(jnp.concatenate([near[:, :samples], far[:, :samples]], axis=0), 1)
+    near_far, far_near, far_far, far_tile, before = call(
+        far_kernel,
+        (
+            shape((count, count), bf16),
+            shape((count, count), bf16),
+            shape((count, count), bf16),
+            shape((per_device, count), bf16),
+            shape((samples, 2 * count), f32),
+        ),
+        scratch=[pltpu.VMEM((count, stack), bf16), pltpu.VMEM((stack, count), bf16)],
+        inputs=6, flops=1 << 33,
+    )(far, near, left, right, cand_left, near_near)
     return tuple(
         call(
             functools.partial(solve_kernel, own_rows),
-            (
-                jax.ShapeDtypeStruct((per_device, samples), f32),
-                jax.ShapeDtypeStruct((own_rows, samples), f32),
-            ),
+            (shape((per_device, samples), f32), shape((own_rows, samples), f32)),
             scratch=[
-                pltpu.VMEM((samples, count), f32),
-                pltpu.VMEM((samples, count), bf16),
-                pltpu.VMEM((samples, count), f32),
-                pltpu.VMEM((count, stack), bf16),
-                pltpu.VMEM((stack, count), bf16),
-                pltpu.VMEM((count, count), bf16),
+                pltpu.VMEM((samples, 2 * count), f32),
+                pltpu.VMEM((samples, 2 * count), f32),
+                pltpu.VMEM((samples, 2 * count), f32),
+                pltpu.VMEM((samples, 2 * count), bf16),
             ],
-            scalars=1, inputs=3, flops=1 << 34,
-        )(which, gathered, mine, prior_cand)
+            scalars=1, inputs=11, flops=1 << 33,
+        )(
+            which, near, far, other, before, near_near, near_far, far_near, far_far,
+            near_tile, far_tile, prior_cand,
+        )
     )
 
 
 def is_local(mesh, x_train):
     train, cand = mesh.shape["train"], mesh.shape["cand"]
     count = x_train.shape[1]
-    return cand == 2 and train & (train - 1) == 0 and 2 * count * count <= KERNEL_BYTES
+    tiles = count // 2 % TILE == 0
+    return cand == 2 and train >= 4 and train & (train - 1) == 0 and tiles and 2 * count * count <= KERNEL_BYTES
 
 
 def squares_of(points):

time: 40.5 us -> 28.7 us (0.71)
  waiting for transfers between devices: 10.9 us -> 6.85 us
  local copies, waits for them, and re-layouts: 4.17 us -> 0.12 us
  Pallas kernels: 12.7 us -> 9.3 us
    unnamed x24 -> x10, local copies, waits for them, and re-layouts: 4.06 us -> 0.03 us
    pallas_call x4 -> x6, Pallas kernels: 12.7 us -> 9.3 us  [the longest x1 3.13 us: local_body(): call(functools.partial(solve_kernel, own_rows), (shape((per_device, sampl...]
    ppermute x1, waiting for transfers between devices: 2.92 us -> 1.15 us  [local_body(): other_weights = lax.ppermute(late_weights, 'cand', swap)]
    ppermute x1, waiting for transfers between devices: 1.89 us -> 0.72 us  [local_body(): other = lax.ppermute(partial, 'cand', swap)]
    ppermute x4 -> x5, waiting for transfers between devices: 6.11 us -> 4.97 us  [exchange(): return lax.ppermute(values, 'train', [(i, i ^ bit) for i in range(blocks)])]
    ppermute x4 -> x5, starting transfers between devices: 7.01 us -> 7.01 us  [exchange(): return lax.ppermute(values, 'train', [(i, i ^ bit) for i in range(blocks)])]
  transfers between devices with their start and end apart: 6 -> 7, of which waited for: 5 -> 6; matrix products, arithmetic and copies ran while one was open for 0% -> 0% of each run, Pallas kernels for 2% -> 14%
where the time goes in v2:
time: 28.7 us; the launch traced here: 28.6 us
  starting transfers between devices  11.5 us (40%)
  Pallas kernels  9.3 us (32%)
  waiting for transfers between devices  6.85 us (24%)
  between operations  0.75 us (3%)
    ppermute x5, starting transfers between devices, exchange(): return lax.ppermute(values, 'train', [(i, i ^ bit) for i in range(blocks)])  7.01 us
    ppermute x5, waiting for transfers between devices, exchange(): return lax.ppermute(values, 'train', [(i, i ^ bit) for i in range(blocks)])  4.97 us
    pallas_call x1, Pallas kernels, local_body(): call(functools.partial(solve_kernel, own_rows), (shape((per_device, sampl...  3.13 us
    ppermute x1, starting transfers between devices, local_body(): other = lax.ppermute(partial, 'cand', swap)  3.02 us
    pallas_call x1, Pallas kernels, local_body(): call(far_kernel, (shape((count, count), bf16), shape((count, count), bf16...  2.52 us
    pallas_call x1, Pallas kernels, local_body(): call(prior_kernel, shape((samples, width), f32), scalars=1, inputs=6, hbm...  2.22 us
    ppermute x1, starting transfers between devices, local_body(): other_weights = lax.ppermute(late_weights, 'cand', swap)  1.5 us
    ppermute x1, waiting for transfers between devices, local_body(): other_weights = lax.ppermute(late_weights, 'cand', swap)  1.15 us
  transfers between devices with their start and end apart: 7, of which 6 were waited for; matrix products, arithmetic and copies ran while one was open for 0% of the time, Pallas kernels for 14%

profile of v2, /device:TPU:0, one launch (start us, length us, event | category | flops | bytes accessed | tf_op | source)
XLA Modules:
  0.0 28.6 jit_solution(9553232795970502068)
XLA Ops:
  0.6 0.0 copy-start
  0.6 0.0 copy-start.1
  0.7 0.0 copy-start.2
  0.7 2.2 %shard_map.86.mine_ref = f32[64,128]{1,0:T(8,128)S(1)} custom-call(s32[1]{0:T(128)} %bitcast.which, f32[8,128]{1,0:T(8,128)} %x_ref.1, f32[8,4096]{1,0:T(8,128)} %omega_ref.1, f32[1,4096]{1,0:T(1,128)} %bitcast.11, bf16[64,2048]{1,0:T(8,128)(2,1)} %bitcast.8, f32[1,64]{1,0:T(1,128)} %bitcast.13, f32[64,64]{1,0:T(8,128)} %noise_hbm.1), custom_call_target="tpu_custom_call" | custom-call | flops 1073741824 | bytes 1048576 | tf_op jit(solution)/shard_map/pallas_call | solution.py:313
  2.9 3.0 %collective-permute-start = (f32[64,128]{1,0:T(8,128)S(1)}, f32[64,128]{1,0:T(8,128)S(1)}, u32[]{:S(2)}, u32[]{:S(2)}) collective-permute-start(f32[64,128]{1,0:T(8,128)S(1)} %shard_map.86.mine_ref), channel_id=1, source_target_pairs={{0,1},{1,0},{2,3},{3,2},{4,5},{5,4},{6,7},{7,6},{8,9},{9,8},{10,11... | collective-permute-start | bytes 98312 | tf_op jit(solution)/shard_map/ppermute | solution.py:327
  5.9 0.0 copy-done.1
  5.9 0.0 collective-permute-start.1
  5.9 1.2 %collective-permute-done.1.pair_ref = f32[8,128]{1,0:T(8,128)S(1)} collective-permute-done((f32[8,128]{1,0:T(8,128)S(1)}, f32[8,128]{1,0:T(8,128)S(1)}, u32[]{:S(2)}, u32[]{:S(2)}) %collective-permute-start.1) | collective-permute-done | bytes 4128 | tf_op jit(solution)/shard_map/ppermute | solution.py:310
  7.1 0.7 %collective-permute-done.other_ref = f32[64,128]{1,0:T(8,128)S(1)} collective-permute-done((f32[64,128]{1,0:T(8,128)S(1)}, f32[64,128]{1,0:T(8,128)S(1)}, u32[]{:S(2)}, u32[]{:S(2)}) %collective-permute-start) | collective-permute-done | bytes 32800 | tf_op jit(solution)/shard_map/ppermute | solution.py:327
  7.8 3.1 %collective-permute-start.2 = (f32[1,80,128]{2,1,0:T(8,128)S(1)}, f32[1,80,128]{2,1,0:T(8,128)S(1)}, u32[]{:S(2)}, u32[]{:S(2)}) collective-permute-start(f32[1,80,128]{2,1,0:T(8,128)S(1)} %bitcast.5), channel_id=1, source_target_pairs={{0,16},{2,18},{4,20},{6,22},{8,24},{10,26},{12,28},{14,30},{16,0},... | collective-permute-start | bytes 122888 | tf_op jit(solution)/shard_map/ppermute | solution.py:310
  10.9 2.0 %collective-permute-done.2 = f32[1,80,128]{2,1,0:T(8,128)S(1)} collective-permute-done((f32[1,80,128]{2,1,0:T(8,128)S(1)}, f32[1,80,128]{2,1,0:T(8,128)S(1)}, u32[]{:S(2)}, u32[]{:S(2)}) %collective-permute-start.2) | collective-permute-done | bytes 40992 | tf_op jit(solution)/shard_map/ppermute | solution.py:310
  12.9 1.9 %collective-permute-start.3 = (f32[2,80,128]{2,1,0:T(8,128)S(1)}, f32[2,80,128]{2,1,0:T(8,128)S(1)}, u32[]{:S(2)}, u32[]{:S(2)}) collective-permute-start(f32[2,80,128]{2,1,0:T(8,128)S(1)} %pad_maximum_fusion.2), channel_id=1, source_target_pairs={{0,8},{2,10},{4,12},{6,14},{8,0},{10,2},{12,4},{14,6},{16,24},{18,... | collective-permute-start | bytes 245768 | tf_op jit(solution)/shard_map/ppermute | solution.py:310
  14.8 0.0 copy-done
  14.8 0.1 constant_dynamic-slice_fusion.cand_ref.x_ref
  14.9 0.0 copy-done.2
  14.9 1.5 %collective-permute-start.6 = (bf16[64,2048]{1,0:T(8,128)(2,1)S(1)}, bf16[64,2048]{1,0:T(8,128)(2,1)S(1)}, u32[]{:S(2)}, u32[]{:S(2)}) collective-permute-start(bf16[64,2048]{1,0:T(8,128)(2,1)S(1)} %bitcast.9), channel_id=1, source_target_pairs={{0,1},{1,0},{2,3},{3,2},{4,5},{5,4},{6,7},{7,6},{8,9},{9,8},{10,11... | collective-permute-start | bytes 786440 | tf_op jit(solution)/shard_map/ppermute | solution.py:332
  16.4 1.0 %collective-permute-done.3 = f32[2,80,128]{2,1,0:T(8,128)S(1)} collective-permute-done((f32[2,80,128]{2,1,0:T(8,128)S(1)}, f32[2,80,128]{2,1,0:T(8,128)S(1)}, u32[]{:S(2)}, u32[]{:S(2)}) %collective-permute-start.3) | collective-permute-done | bytes 81952 | tf_op jit(solution)/shard_map/ppermute | solution.py:310
  17.4 0.0 copy-start.3
  17.4 0.0 copy-start.4
  17.4 1.9 %collective-permute-start.4 = (f32[4,80,128]{2,1,0:T(8,128)S(1)}, f32[4,80,128]{2,1,0:T(8,128)S(1)}, u32[]{:S(2)}, u32[]{:S(2)}) collective-permute-start(f32[4,80,128]{2,1,0:T(8,128)S(1)} %pad_maximum_fusion.1.block_ref.near_ref), channel_id=1, source_target_pairs={{0,4},{2,6},{4,0},{6,2},{8,12},{10,14},{12,8},{14,10},{16,20},{18,... | collective-permute-start | bytes 491528 | tf_op jit(solution)/shard_map/ppermute | solution.py:310
  19.3 0.8 %shard_map.88 = (bf16[1024,64]{1,0:T(8,128)(2,1)S(1)}, bf16[64,1024]{1,0:T(8,128)(2,1)S(1)}, bf16[32,64]{1,0:T(8,128)(2,1)S(1)}, bf16[1024,1024]{1,0:T(8,128)(2,1)S(1)}, bf16[32,1024]{1,0:T(8,128)(2,1)S(1)}) custom-call(f32[4,80,128]{2,1,0:T(8,128)S(1)} %pad_maximum_fusion.1.block_ref.near_ref, f32[8,32]{1,0:T(8,128)S(1)} %constant_dynamic-slice_fusion.cand_ref.x_ref), custom_call_target="tpu_custom_call" | custom-call | flops 2147483648 | bytes 1048576 | tf_op jit(solution)/shard_map/pallas_call | solution.py:346
  20.2 1.1 %collective-permute-done.6.other_ref = bf16[64,2048]{1,0:T(8,128)(2,1)S(1)} collective-permute-done((bf16[64,2048]{1,0:T(8,128)(2,1)S(1)}, bf16[64,2048]{1,0:T(8,128)(2,1)S(1)}, u32[]{:S(2)}, u32[]{:S(2)}) %collective-permute-start.6) | collective-permute-done | bytes 262176 | tf_op jit(solution)/shard_map/ppermute | solution.py:332
  21.3 0.0 copy-done.3
  21.3 0.0 copy-done.4
  21.3 0.6 %shard_map.90.prior_ref = f32[32,64]{1,0:T(8,128)S(1)} custom-call(s32[1]{0:T(128)} %bitcast.which, f32[8,32]{1,0:T(8,128)S(1)} %constant_dynamic-slice_fusion.cand_ref.x_ref, f32[8,4096]{1,0:T(8,128)S(1)} %copy-done.3, f32[1,4096]{1,0:T(1,128)S(1)} %bitcast.12, bf16[64,2048]{1,0:T(8,128)(2,1)S(1)} %bitcast.10, ...), custom_call_target="tpu_custom_call" | custom-call | flops 1073741824 | bytes 1048576 | tf_op jit(solution)/shard_map/pallas_call | solution.py:341
  21.9 0.9 %collective-permute-done.4.block_ref.far_ref = f32[4,80,128]{2,1,0:T(8,128)S(1)} collective-permute-done((f32[4,80,128]{2,1,0:T(8,128)S(1)}, f32[4,80,128]{2,1,0:T(8,128)S(1)}, u32[]{:S(2)}, u32[]{:S(2)}) %collective-permute-start.4) | collective-permute-done | bytes 163872 | tf_op jit(solution)/shard_map/ppermute | solution.py:310
  22.8 0.1 collective-permute-start.5
  22.9 2.5 %shard_map.89 = (bf16[1024,1024]{1,0:T(8,128)(2,1)S(1)}, bf16[1024,1024]{1,0:T(8,128)(2,1)S(1)}, bf16[1024,1024]{1,0:T(8,128)(2,1)S(1)}, bf16[32,1024]{1,0:T(8,128)(2,1)S(1)}, f32[64,2048]{1,0:T(8,128)S(1)}) custom-call(f32[4,80,128]{2,1,0:T(8,128)S(1)} %collective-permute-done.4.block_ref.far_ref, f32[4,80,128]{2,1,0:T(8,128)S(1)} %pad_maximum_fusion.1.block_ref.near_ref, ...), custom_call_target="tpu_custom_call" | custom-call | flops 8589934592 | bytes 1048576 | tf_op jit(solution)/shard_map/pallas_call | solution.py:358
  25.4 0.0 collective-permute-done.5.other_ref
  25.5 3.1 %shard_map.91 = (f32[32,64]{1,0:T(8,128)}, f32[64,64]{1,0:T(8,128)}) custom-call(s32[1]{0:T(128)} %bitcast.which, f32[4,80,128]{2,1,0:T(8,128)S(1)} %pad_maximum_fusion.1.block_ref.near_ref, f32[4,80,128]{2,1,0:T(8,128)S(1)} %collective-permute-done.4.block_ref.far_ref, f32[8,64,128]{2,1,0:T(8,128)S(1)} %collective-permute-done.5.other_ref, ...), custom_call_target="tpu_custom_call" | custom-call | flops 8589934592 | bytes 1048576 | tf_op jit(solution)/shard_map/pallas_call | solution.py:371
  (6 shorter events, 0.1 us)
Async XLA Ops:
  0.6 14.2 %copy-start = (f32[8,512]{1,0:T(8,128)S(1)}, f32[8,512]{1,0:T(8,128)}, u32[]{:S(2)}) copy-start(f32[8,512]{1,0:T(8,128)} %param.8) | copy-start | bytes 49156
  0.6 5.3 %copy-start.1 = (f32[8,128]{1,0:T(8,128)S(1)}, f32[8,128]{1,0:T(8,128)}, u32[]{:S(2)}) copy-start(f32[8,128]{1,0:T(8,128)} %x_ref.1) | copy-start | bytes 12292
  0.7 14.3 %copy-start.2 = (bf16[2048,64]{0,1:T(8,128)(2,1)S(1)}, bf16[2048,64]{0,1:T(8,128)(2,1)}, u32[]{:S(2)}) copy-start(bf16[2048,64]{0,1:T(8,128)(2,1)} %param.13) | copy-start | bytes 786436
  2.9 4.9 %collective-permute-start = (f32[64,128]{1,0:T(8,128)S(1)}, f32[64,128]{1,0:T(8,128)S(1)}, u32[]{:S(2)}, u32[]{:S(2)}) collective-permute-start(f32[64,128]{1,0:T(8,128)S(1)} %shard_map.86.mine_ref), channel_id=1, source_target_pairs={{0,1},{1,0},{2,3},{3,2},{4,5},{5,4},{6,7},{7,6},{8,9},{9,8},{10,11... | collective-permute-start | bytes 98312 | tf_op jit(solution)/shard_map/ppermute | solution.py:327
  5.9 1.2 %collective-permute-start.1 = (f32[8,128]{1,0:T(8,128)S(1)}, f32[8,128]{1,0:T(8,128)S(1)}, u32[]{:S(2)}, u32[]{:S(2)}) collective-permute-start(f32[8,128]{1,0:T(8,128)S(1)} %copy-done.1), channel_id=1, source_target_pairs={{0,2},{2,0},{4,6},{6,4},{8,10},{10,8},{12,14},{14,12},{16,18},{18,... | collective-permute-start | bytes 12296 | tf_op jit(solution)/shard_map/ppermute | solution.py:310
  7.8 5.1 %collective-permute-start.2 = (f32[1,80,128]{2,1,0:T(8,128)S(1)}, f32[1,80,128]{2,1,0:T(8,128)S(1)}, u32[]{:S(2)}, u32[]{:S(2)}) collective-permute-start(f32[1,80,128]{2,1,0:T(8,128)S(1)} %bitcast.5), channel_id=1, source_target_pairs={{0,16},{2,18},{4,20},{6,22},{8,24},{10,26},{12,28},{14,30},{16,0},... | collective-permute-start | bytes 122888 | tf_op jit(solution)/shard_map/ppermute | solution.py:310
  12.9 4.4 %collective-permute-start.3 = (f32[2,80,128]{2,1,0:T(8,128)S(1)}, f32[2,80,128]{2,1,0:T(8,128)S(1)}, u32[]{:S(2)}, u32[]{:S(2)}) collective-permute-start(f32[2,80,128]{2,1,0:T(8,128)S(1)} %pad_maximum_fusion.2), channel_id=1, source_target_pairs={{0,8},{2,10},{4,12},{6,14},{8,0},{10,2},{12,4},{14,6},{16,24},{18,... | collective-permute-start | bytes 245768 | tf_op jit(solution)/shard_map/ppermute | solution.py:310
  14.9 6.4 %collective-permute-start.6 = (bf16[64,2048]{1,0:T(8,128)(2,1)S(1)}, bf16[64,2048]{1,0:T(8,128)(2,1)S(1)}, u32[]{:S(2)}, u32[]{:S(2)}) collective-permute-start(bf16[64,2048]{1,0:T(8,128)(2,1)S(1)} %bitcast.9), channel_id=1, source_target_pairs={{0,1},{1,0},{2,3},{3,2},{4,5},{5,4},{6,7},{7,6},{8,9},{9,8},{10,11... | collective-permute-start | bytes 786440 | tf_op jit(solution)/shard_map/ppermute | solution.py:332
  17.4 3.9 %copy-start.3 = (f32[8,4096]{1,0:T(8,128)S(1)}, f32[8,4096]{1,0:T(8,128)}, u32[]{:S(2)}) copy-start(f32[8,4096]{1,0:T(8,128)} %omega_ref.1) | copy-start | bytes 393220
  17.4 3.9 %copy-start.4 = (f32[4096]{0:T(1024)S(1)}, f32[4096]{0:T(1024)}, u32[]{:S(2)}) copy-start(f32[4096]{0:T(1024)} %param.12) | copy-start | bytes 49156
  17.4 5.4 %collective-permute-start.4 = (f32[4,80,128]{2,1,0:T(8,128)S(1)}, f32[4,80,128]{2,1,0:T(8,128)S(1)}, u32[]{:S(2)}, u32[]{:S(2)}) collective-permute-start(f32[4,80,128]{2,1,0:T(8,128)S(1)} %pad_maximum_fusion.1.block_ref.near_ref), channel_id=1, source_target_pairs={{0,4},{2,6},{4,0},{6,2},{8,12},{10,14},{12,8},{14,10},{16,20},{18,... | collective-permute-start | bytes 491528 | tf_op jit(solution)/shard_map/ppermute | solution.py:310
  22.8 2.6 %collective-permute-start.5 = (f32[8,64,128]{2,1,0:T(8,128)S(1)}, f32[8,64,128]{2,1,0:T(8,128)S(1)}, u32[]{:S(2)}, u32[]{:S(2)}) collective-permute-start(f32[8,64,128]{2,1,0:T(8,128)S(1)} %pad_maximum_fusion), channel_id=1, source_target_pairs={{0,2},{2,0},{4,6},{6,4},{8,10},{10,8},{12,14},{14,12},{16,18},{18,... | collective-permute-start | bytes 786440 | tf_op jit(solution)/shard_map/ppermute | solution.py:310

commit v3 on v2

--- a/solution.py
+++ b/solution.py
@@ -165,19 +165,31 @@
     return jnp.concatenate([block_ref[k, :samples, :] for k in range(first, last)], axis=1)
 
 
-def near_kernel(block_ref, cand_ref, left_ref, right_ref, cand_left_ref, kernel_ref, tile_ref):
-    samples = block_ref.shape[1] - 2 * cand_ref.shape[0]
+def product(rows, kernel):
+    return jnp.dot(rows, kernel, preferred_element_type=f32)
+
+
+def product_transposed(rows, kernel):
+    return lax.dot_general(rows, kernel, (((1,), (1,)), ((), ())), preferred_element_type=f32)
+
+
+def near_kernel(
+    block_ref, cand_ref, left_ref, right_ref, cand_left_ref, kernel_ref, tile_ref, field_ref
+):
+    samples = field_ref.shape[0]
     points = points_of(block_ref, samples)
     left_ref[...] = left_of(points)
     right_ref[...] = right_of(points)
     cand_left_ref[...] = left_of(cand_ref[...])
     fill(kernel_ref, left_ref, right_ref)
     fill(tile_ref, cand_left_ref, right_ref)
+    half = points.shape[1] // 2
+    field_ref[...] = product(rows_of(block_ref, samples).astype(bf16), kernel_ref[:half, :])
 
 
 def far_kernel(
-    block_ref, near_ref, left_ref, right_ref, cand_left_ref, kernel_ref,
-    near_far_ref, far_near_ref, far_far_ref, tile_ref, field_ref,
+    block_ref, near_ref, left_ref, right_ref, cand_left_ref, before_ref,
+    near_far_ref, far_far_ref, tile_ref, field_ref,
     far_left_ref, far_right_ref,
 ):
     samples = field_ref.shape[0]
@@ -185,32 +197,17 @@
     far_left_ref[...] = left_of(points)
     far_right_ref[...] = right_of(points)
     fill(near_far_ref, left_ref, far_right_ref)
-    fill(far_near_ref, far_left_ref, right_ref)
     fill(far_far_ref, far_left_ref, far_right_ref)
     fill(tile_ref, cand_left_ref, far_right_ref)
-    add_field(
-        field_ref, None, slice(0, points.shape[1] // 2),
-        rows_of(near_ref, samples).astype(bf16), rows_of(block_ref, samples).astype(bf16),
-        kernel_ref, near_far_ref, far_near_ref, far_far_ref,
-    )
-
-
-def add_field(field_ref, before_ref, rows, near, far, near_near, near_far, far_near, far_far):
-    count = near_near.shape[0]
-    for j in range(0, count, TILE):
-        for offset, first, second in ((0, near_near, far_near), (count, near_far, far_far)):
-            width = min(TILE, count - j)
-            columns = slice(offset + j, offset + j + width)
-            value = jnp.dot(near, first[rows, j : j + width], preferred_element_type=f32)
-            value += jnp.dot(far, second[rows, j : j + width], preferred_element_type=f32)
-            if before_ref is not None:
-                value += before_ref[:, columns]
-            field_ref[:, columns] = value
+    half, count = points.shape[1] // 2, points.shape[1]
+    near, far = rows_of(near_ref, samples).astype(bf16), rows_of(block_ref, samples).astype(bf16)
+    field_ref[:, :count] = before_ref[...] + product_transposed(far, near_far_ref[:, :half])
+    field_ref[:, count:] = product(near, near_far_ref[:half, :]) + product(far, far_far_ref[:half, :])
 
 
 def solve_kernel(
     own_rows, which, near_ref, far_ref, other_ref, before_ref,
-    near_near_ref, near_far_ref, far_near_ref, far_far_ref,
+    near_near_ref, near_far_ref, far_far_ref,
     near_tile_ref, far_tile_ref, prior_ref, samples_ref, solution_ref,
     field_ref, start_ref, direction_ref, packed_ref,
 ):
@@ -220,9 +217,14 @@
     count = 2 * half
     near_other = rows_of(other_ref, samples, 0, blocks)
     far_other = rows_of(other_ref, samples, blocks, 2 * blocks)
-    add_field(
-        field_ref, before_ref, slice(half, count), near_other.astype(bf16), far_other.astype(bf16),
-        near_near_ref, near_far_ref, far_near_ref, far_far_ref,
+    near, far = near_other.astype(bf16), far_other.astype(bf16)
+    field_ref[:, :count] = (
+        before_ref[:, :count]
+        + product(near, near_near_ref[half:, :])
+        + product_transposed(far, near_far_ref[:, half:])
+    )
+    field_ref[:, count:] = (
+        before_ref[:, count:] + product(near, near_far_ref[half:, :]) + product(far, far_far_ref[half:, :])
     )
     start_ref[:, :half] = rows_of(near_ref, samples)
     start_ref[:, half:count] = near_other
@@ -328,14 +330,16 @@
     payload = call(pack_kernel, shape((samples + 2 * dim, width), f32), inputs=4)(
         partial, other, x_train, pair
     )
-    payload, late_weights = lax.optimization_barrier((payload, weights))
-    other_weights = lax.ppermute(late_weights, "cand", swap)
-    near = payload[None]
+    other_weights = lax.ppermute(weights, "cand", swap)
+    first = payload[None]
     bit = blocks // 2
-    while bit > 2:
-        near = jnp.concatenate([near, exchange(near, bit)], axis=0)
+    while bit > 4:
+        first = jnp.concatenate([first, exchange(first, bit)], axis=0)
         bit //= 2
-    far = exchange(near, 2)
+    third = exchange(first, 6)
+    second = exchange(first, 4)
+    near = jnp.concatenate([first, exchange(first, 2)], axis=0)
+    far = jnp.concatenate([second, third], axis=0)
     per_device = x_cand.shape[1] // blocks
     mine = lax.dynamic_slice_in_dim(x_cand, train_index * per_device, per_device, 1)
     prior_cand = call(cand_kernel, shape((per_device, samples), f32), scalars=1, inputs=5, flops=1 << 30)(
@@ -343,30 +347,26 @@
     )
     count = blocks * width // 2
     stack = 6 * dim + 16
-    left, right, cand_left, near_near, near_tile = call(
+    square = shape((count, count), bf16)
+    left, right, cand_left, near_near, near_tile, before = call(
         near_kernel,
         (
             shape((count, stack), bf16),
             shape((stack, count), bf16),
             shape((per_device, stack), bf16),
-            shape((count, count), bf16),
+            square,
             shape((per_device, count), bf16),
+            shape((samples, count), f32),
         ),
         inputs=2, flops=1 << 31,
     )(near, mine)
     other = exchange(jnp.concatenate([near[:, :samples], far[:, :samples]], axis=0), 1)
-    near_far, far_near, far_far, far_tile, before = call(
+    near_far, far_far, far_tile, before = call(
         far_kernel,
-        (
-            shape((count, count), bf16),
-            shape((count, count), bf16),
-            shape((count, count), bf16),
-            shape((per_device, count), bf16),
-            shape((samples, 2 * count), f32),
-        ),
+        (square, square, shape((per_device, count), bf16), shape((samples, 2 * count), f32)),
         scratch=[pltpu.VMEM((count, stack), bf16), pltpu.VMEM((stack, count), bf16)],
         inputs=6, flops=1 << 33,
-    )(far, near, left, right, cand_left, near_near)
+    )(far, near, left, right, cand_left, before)
     return tuple(
         call(
             functools.partial(solve_kernel, own_rows),
@@ -377,9 +377,9 @@
                 pltpu.VMEM((samples, 2 * count), f32),
                 pltpu.VMEM((samples, 2 * count), bf16),
             ],
-            scalars=1, inputs=11, flops=1 << 33,
+            scalars=1, inputs=10, flops=1 << 33,
         )(
-            which, near, far, other, before, near_near, near_far, far_near, far_far,
+            which, near, far, other, before, near_near, near_far, far_far,
             near_tile, far_tile, prior_cand,
         )
     )
@@ -389,7 +389,7 @@
     train, cand = mesh.shape["train"], mesh.shape["cand"]
     count = x_train.shape[1]
     tiles = count // 2 % TILE == 0
-    return cand == 2 and train >= 4 and train & (train - 1) == 0 and tiles and 2 * count * count <= KERNEL_BYTES
+    return cand == 2 and train >= 8 and train & (train - 1) == 0 and tiles and 2 * count * count <= KERNEL_BYTES
 
 
 def squares_of(points):
@@ -442,7 +442,7 @@
     residual = rhs
     direction = rhs
     norm_now = squares(residual)
-    for step in range(ITERS):
+    for _ in range(ITERS):
         packed = direction.astype(jnp.bfloat16)
         empty = jnp.zeros((x_train.shape[1], packed.shape[1]), jnp.float32)
         total = empty
@@ -492,6 +492,7 @@
         P(),
         P("cand", None),
     )
+
     def sharded(chosen):
         return jax.shard_map(
             chosen,
@@ -502,7 +503,8 @@
         )
 
     def step(x_train, *rest):
-        chosen = local_body if is_local(mesh, x_train) else body
-        return sharded(chosen)(x_train, *rest)
+        if not is_local(mesh, x_train):
+            return sharded(body)(x_train, *rest)
+        return sharded(local_body)(x_train, *rest)
 
     return step

time: 28.7 us -> 28 us (0.976)
  starting transfers between devices: 11.5 us -> 11.2 us
    ppermute x1, waiting for transfers between devices: 1.15 us -> 0.01 us  [local_body(): other_weights = lax.ppermute(weights, 'cand', swap)]
    ppermute x5 -> x6, waiting for transfers between devices: 4.97 us -> 5.93 us  [exchange(): return lax.ppermute(values, 'train', [(i, i ^ bit) for i in range(blocks)])]
    pallas_call x1, Pallas kernels: 2.52 us -> 1.96 us  [local_body(): call(far_kernel, (square, square, shape((per_device, count), bf16), shape...]
    ppermute x5 -> x6, starting transfers between devices: 7.01 us -> 6.69 us  [exchange(): return lax.ppermute(values, 'train', [(i, i ^ bit) for i in range(blocks)])]
  transfers between devices with their start and end apart: 7 -> 8, of which waited for: 6 -> 5; matrix products, arithmetic and copies ran while one was open for 0% -> 1% of each run, Pallas kernels for 14% -> 13%
where the time goes in v3:
time: 28 us; the launch traced here: 27.8 us
  starting transfers between devices  11.2 us (40%)
  Pallas kernels  9.02 us (32%)
  waiting for transfers between devices  6.66 us (24%)
  between operations  0.76 us (3%)
    ppermute x6, starting transfers between devices, exchange(): return lax.ppermute(values, 'train', [(i, i ^ bit) for i in range(blocks)])  6.69 us
    ppermute x6, waiting for transfers between devices, exchange(): return lax.ppermute(values, 'train', [(i, i ^ bit) for i in range(blocks)])  5.93 us
    pallas_call x1, Pallas kernels, local_body(): call(functools.partial(solve_kernel, own_rows), (shape((per_device, sampl...  3.23 us
    ppermute x1, starting transfers between devices, local_body(): other = lax.ppermute(partial, 'cand', swap)  3.02 us
    pallas_call x1, Pallas kernels, local_body(): call(prior_kernel, shape((samples, width), f32), scalars=1, inputs=6, hbm...  2.22 us
    pallas_call x1, Pallas kernels, local_body(): call(far_kernel, (square, square, shape((per_device, count), bf16), shape...  1.96 us
    ppermute x1, starting transfers between devices, local_body(): other_weights = lax.ppermute(weights, 'cand', swap)  1.49 us
    pallas_call x1, Pallas kernels, local_body(): call(near_kernel, (shape((count, stack), bf16), shape((stack, count), bf1...  0.97 us
  transfers between devices with their start and end apart: 8, of which 5 were waited for; matrix products, arithmetic and copies ran while one was open for 1% of the time, Pallas kernels for 13%

profile of v3, /device:TPU:0, one launch (start us, length us, event | category | flops | bytes accessed | tf_op | source)
XLA Modules:
  0.0 27.8 jit_solution(15063761587075344563)
XLA Ops:
  0.6 0.0 copy-start
  0.6 0.0 copy-start.2
  0.7 0.0 copy-start.1
  0.7 2.2 %shard_map.86.mine_ref = f32[64,128]{1,0:T(8,128)S(1)} custom-call(s32[1]{0:T(128)} %bitcast.which, f32[8,128]{1,0:T(8,128)} %x_ref.1, f32[8,4096]{1,0:T(8,128)} %omega_ref.1, f32[1,4096]{1,0:T(1,128)} %bitcast.11, bf16[64,2048]{1,0:T(8,128)(2,1)} %bitcast.8, f32[1,64]{1,0:T(1,128)} %bitcast.13, f32[64,64]{1,0:T(8,128)} %noise_hbm.1), custom_call_target="tpu_custom_call" | custom-call | flops 1073741824 | bytes 1048576 | tf_op jit(solution)/shard_map/pallas_call | solution.py:315
  2.9 3.0 %collective-permute-start = (f32[64,128]{1,0:T(8,128)S(1)}, f32[64,128]{1,0:T(8,128)S(1)}, u32[]{:S(2)}, u32[]{:S(2)}) collective-permute-start(f32[64,128]{1,0:T(8,128)S(1)} %shard_map.86.mine_ref), channel_id=1, source_target_pairs={{0,1},{1,0},{2,3},{3,2},{4,5},{5,4},{6,7},{7,6},{8,9},{9,8},{10,11... | collective-permute-start | bytes 98312 | tf_op jit(solution)/shard_map/ppermute | solution.py:329
  5.9 0.0 copy-done.1
  5.9 0.0 collective-permute-start.1
  5.9 1.2 %collective-permute-done.1.pair_ref = f32[8,128]{1,0:T(8,128)S(1)} collective-permute-done((f32[8,128]{1,0:T(8,128)S(1)}, f32[8,128]{1,0:T(8,128)S(1)}, u32[]{:S(2)}, u32[]{:S(2)}) %collective-permute-start.1) | collective-permute-done | bytes 4128 | tf_op jit(solution)/shard_map/ppermute | solution.py:312
  7.1 0.7 %collective-permute-done.other_ref = f32[64,128]{1,0:T(8,128)S(1)} collective-permute-done((f32[64,128]{1,0:T(8,128)S(1)}, f32[64,128]{1,0:T(8,128)S(1)}, u32[]{:S(2)}, u32[]{:S(2)}) %collective-permute-start) | collective-permute-done | bytes 32800 | tf_op jit(solution)/shard_map/ppermute | solution.py:329
  7.8 3.1 %collective-permute-start.2 = (f32[1,80,128]{2,1,0:T(8,128)S(1)}, f32[1,80,128]{2,1,0:T(8,128)S(1)}, u32[]{:S(2)}, u32[]{:S(2)}) collective-permute-start(f32[1,80,128]{2,1,0:T(8,128)S(1)} %bitcast.5), channel_id=1, source_target_pairs={{0,16},{2,18},{4,20},{6,22},{8,24},{10,26},{12,28},{14,30},{16,0},... | collective-permute-start | bytes 122888 | tf_op jit(solution)/shard_map/ppermute | solution.py:312
  10.9 0.0 copy-done.2
  11.0 1.5 %collective-permute-start.7 = (bf16[64,2048]{1,0:T(8,128)(2,1)S(1)}, bf16[64,2048]{1,0:T(8,128)(2,1)S(1)}, u32[]{:S(2)}, u32[]{:S(2)}) collective-permute-start(bf16[64,2048]{1,0:T(8,128)(2,1)S(1)} %bitcast.9), channel_id=1, source_target_pairs={{0,1},{1,0},{2,3},{3,2},{4,5},{5,4},{6,7},{7,6},{8,9},{9,8},{10,11... | collective-permute-start | bytes 786440 | tf_op jit(solution)/shard_map/ppermute | solution.py:333
  12.4 0.5 %collective-permute-done.2 = f32[1,80,128]{2,1,0:T(8,128)S(1)} collective-permute-done((f32[1,80,128]{2,1,0:T(8,128)S(1)}, f32[1,80,128]{2,1,0:T(8,128)S(1)}, u32[]{:S(2)}, u32[]{:S(2)}) %collective-permute-start.2) | collective-permute-done | bytes 40992 | tf_op jit(solution)/shard_map/ppermute | solution.py:312
  12.9 1.8 %collective-permute-start.3 = (f32[2,80,128]{2,1,0:T(8,128)S(1)}, f32[2,80,128]{2,1,0:T(8,128)S(1)}, u32[]{:S(2)}, u32[]{:S(2)}) collective-permute-start(f32[2,80,128]{2,1,0:T(8,128)S(1)} %pad_maximum_fusion.2), channel_id=1, source_target_pairs={{0,4},{2,6},{4,0},{6,2},{8,12},{10,14},{12,8},{14,10},{16,20},{18,... | collective-permute-start | bytes 245768 | tf_op jit(solution)/shard_map/ppermute | solution.py:312
  14.8 0.0 copy-done
  14.8 0.1 constant_dynamic-slice_fusion.cand_ref.x_ref
  14.9 1.6 %collective-permute-start.4 = (f32[2,80,128]{2,1,0:T(8,128)S(1)}, f32[2,80,128]{2,1,0:T(8,128)S(1)}, u32[]{:S(2)}, u32[]{:S(2)}) collective-permute-start(f32[2,80,128]{2,1,0:T(8,128)S(1)} %pad_maximum_fusion.2), channel_id=1, source_target_pairs={{0,8},{2,10},{4,12},{6,14},{8,0},{10,2},{12,4},{14,6},{16,24},{18,... | collective-permute-start | bytes 245768 | tf_op jit(solution)/shard_map/ppermute | solution.py:312
  16.4 0.1 collective-permute-start.5
  16.5 1.8 %collective-permute-done.3 = f32[2,80,128]{2,1,0:T(8,128)S(1)} collective-permute-done((f32[2,80,128]{2,1,0:T(8,128)S(1)}, f32[2,80,128]{2,1,0:T(8,128)S(1)}, u32[]{:S(2)}, u32[]{:S(2)}) %collective-permute-start.3) | collective-permute-done | bytes 81952 | tf_op jit(solution)/shard_map/ppermute | solution.py:312
  18.3 1.0 %shard_map.88 = (bf16[1024,64]{1,0:T(8,128)(2,1)S(1)}, bf16[64,1024]{1,0:T(8,128)(2,1)S(1)}, bf16[32,64]{1,0:T(8,128)(2,1)S(1)}, bf16[1024,1024]{1,0:T(8,128)(2,...) custom-call(f32[4,80,128]{2,1,0:T(8,128)S(1)} %pad_maximum_fusion.1.block_ref.near_ref, ...), custom_call_target="tpu_custom_call" | custom-call | flops 2147483648 | bytes 1048576 | tf_op jit(solution)/shard_map/pallas_call | solution.py:351
  19.3 0.0 collective-permute-done.4
  19.3 2.5 %collective-permute-done.5 = f32[2,80,128]{2,1,0:T(8,128)S(1)} collective-permute-done((f32[2,80,128]{2,1,0:T(8,128)S(1)}, f32[2,80,128]{2,1,0:T(8,128)S(1)}, u32[]{:S(2)}, u32[]{:S(2)}) %collective-permute-start.5) | collective-permute-done | bytes 81952 | tf_op jit(solution)/shard_map/ppermute | solution.py:312
  21.8 0.1 collective-permute-start.6
  21.9 0.0 copy-start.3
  21.9 0.0 copy-start.4
  21.9 2.0 %shard_map.89 = (bf16[1024,1024]{1,0:T(8,128)(2,1)S(1)}, bf16[1024,1024]{1,0:T(8,128)(2,1)S(1)}, bf16[32,1024]{1,0:T(8,128)(2,1)S(1)}, f32[64,2048]{1,0:T(8,128)S(1)}) custom-call(f32[4,80,128]{2,1,0:T(8,128)S(1)} %constant_dynamic-update-slice_fusion.block_ref.far_ref, f32[4,80,128]{2,1,0:T(8,128)S(1)} %pad_maximum_fusion.1.block_ref.near_ref, ...), custom_call_target="tpu_custom_call" | custom-call | flops 8589934592 | bytes 1048576 | tf_op jit(solution)/shard_map/pallas_call | solution.py:364
  23.9 0.0 collective-permute-done.7.other_ref
  23.9 0.0 copy-done.3
  23.9 0.0 copy-done.4
  23.9 0.6 %shard_map.90.prior_ref = f32[32,64]{1,0:T(8,128)S(1)} custom-call(s32[1]{0:T(128)} %bitcast.which, f32[8,32]{1,0:T(8,128)S(1)} %constant_dynamic-slice_fusion.cand_ref.x_ref, f32[8,4096]{1,0:T(8,128)S(1)} %copy-done.3, f32[1,4096]{1,0:T(1,128)S(1)} %bitcast.12, bf16[64,2048]{1,0:T(8,128)(2,1)S(1)} %bitcast.10, ...), custom_call_target="tpu_custom_call" | custom-call | flops 1073741824 | bytes 1048576 | tf_op jit(solution)/shard_map/pallas_call | solution.py:345
  24.6 0.0 collective-permute-done.6.other_ref
  24.6 3.2 %shard_map.91 = (f32[32,64]{1,0:T(8,128)}, f32[64,64]{1,0:T(8,128)}) custom-call(s32[1]{0:T(128)} %bitcast.which, f32[4,80,128]{2,1,0:T(8,128)S(1)} %pad_maximum_fusion.1.block_ref.near_ref, f32[4,80,128]{2,1,0:T(8,128)S(1)} %constant_dynamic-update-slice_fusion.block_ref.far_ref, f32[8,64,128]{2,1,0:T(8,128)S(1)} %collective-permute-done.6.other_ref, ...), custom_call_target="tpu_custom_call" | custom-call | flops 8589934592 | bytes 1048576 | tf_op jit(solution)/shard_map/pallas_call | solution.py:371
  (8 shorter events, 0.1 us)
Async XLA Ops:
  0.6 14.2 %copy-start = (f32[8,512]{1,0:T(8,128)S(1)}, f32[8,512]{1,0:T(8,128)}, u32[]{:S(2)}) copy-start(f32[8,512]{1,0:T(8,128)} %param.8) | copy-start | bytes 49156
  0.6 10.3 %copy-start.2 = (bf16[2048,64]{0,1:T(8,128)(2,1)S(1)}, bf16[2048,64]{0,1:T(8,128)(2,1)}, u32[]{:S(2)}) copy-start(bf16[2048,64]{0,1:T(8,128)(2,1)} %param.13) | copy-start | bytes 786436
  0.7 5.3 %copy-start.1 = (f32[8,128]{1,0:T(8,128)S(1)}, f32[8,128]{1,0:T(8,128)}, u32[]{:S(2)}) copy-start(f32[8,128]{1,0:T(8,128)} %x_ref.1) | copy-start | bytes 12292
  2.9 4.9 %collective-permute-start = (f32[64,128]{1,0:T(8,128)S(1)}, f32[64,128]{1,0:T(8,128)S(1)}, u32[]{:S(2)}, u32[]{:S(2)}) collective-permute-start(f32[64,128]{1,0:T(8,128)S(1)} %shard_map.86.mine_ref), channel_id=1, source_target_pairs={{0,1},{1,0},{2,3},{3,2},{4,5},{5,4},{6,7},{7,6},{8,9},{9,8},{10,11... | collective-permute-start | bytes 98312 | tf_op jit(solution)/shard_map/ppermute | solution.py:329
  5.9 1.2 %collective-permute-start.1 = (f32[8,128]{1,0:T(8,128)S(1)}, f32[8,128]{1,0:T(8,128)S(1)}, u32[]{:S(2)}, u32[]{:S(2)}) collective-permute-start(f32[8,128]{1,0:T(8,128)S(1)} %copy-done.1), channel_id=1, source_target_pairs={{0,2},{2,0},{4,6},{6,4},{8,10},{10,8},{12,14},{14,12},{16,18},{18,... | collective-permute-start | bytes 12296 | tf_op jit(solution)/shard_map/ppermute | solution.py:312
  7.8 5.1 %collective-permute-start.2 = (f32[1,80,128]{2,1,0:T(8,128)S(1)}, f32[1,80,128]{2,1,0:T(8,128)S(1)}, u32[]{:S(2)}, u32[]{:S(2)}) collective-permute-start(f32[1,80,128]{2,1,0:T(8,128)S(1)} %bitcast.5), channel_id=1, source_target_pairs={{0,16},{2,18},{4,20},{6,22},{8,24},{10,26},{12,28},{14,30},{16,0},... | collective-permute-start | bytes 122888 | tf_op jit(solution)/shard_map/ppermute | solution.py:312
  11.0 12.9 %collective-permute-start.7 = (bf16[64,2048]{1,0:T(8,128)(2,1)S(1)}, bf16[64,2048]{1,0:T(8,128)(2,1)S(1)}, u32[]{:S(2)}, u32[]{:S(2)}) collective-permute-start(bf16[64,2048]{1,0:T(8,128)(2,1)S(1)} %bitcast.9), channel_id=1, source_target_pairs={{0,1},{1,0},{2,3},{3,2},{4,5},{5,4},{6,7},{7,6},{8,9},{9,8},{10,11... | collective-permute-start | bytes 786440 | tf_op jit(solution)/shard_map/ppermute | solution.py:333
  12.9 5.3 %collective-permute-start.3 = (f32[2,80,128]{2,1,0:T(8,128)S(1)}, f32[2,80,128]{2,1,0:T(8,128)S(1)}, u32[]{:S(2)}, u32[]{:S(2)}) collective-permute-start(f32[2,80,128]{2,1,0:T(8,128)S(1)} %pad_maximum_fusion.2), channel_id=1, source_target_pairs={{0,4},{2,6},{4,0},{6,2},{8,12},{10,14},{12,8},{14,10},{16,20},{18,... | collective-permute-start | bytes 245768 | tf_op jit(solution)/shard_map/ppermute | solution.py:312
  14.9 4.4 %collective-permute-start.4 = (f32[2,80,128]{2,1,0:T(8,128)S(1)}, f32[2,80,128]{2,1,0:T(8,128)S(1)}, u32[]{:S(2)}, u32[]{:S(2)}) collective-permute-start(f32[2,80,128]{2,1,0:T(8,128)S(1)} %pad_maximum_fusion.2), channel_id=1, source_target_pairs={{0,8},{2,10},{4,12},{6,14},{8,0},{10,2},{12,4},{14,6},{16,24},{18,... | collective-permute-start | bytes 245768 | tf_op jit(solution)/shard_map/ppermute | solution.py:312
  16.4 5.3 %collective-permute-start.5 = (f32[2,80,128]{2,1,0:T(8,128)S(1)}, f32[2,80,128]{2,1,0:T(8,128)S(1)}, u32[]{:S(2)}, u32[]{:S(2)}) collective-permute-start(f32[2,80,128]{2,1,0:T(8,128)S(1)} %pad_maximum_fusion.2), channel_id=1, source_target_pairs={{0,12},{2,14},{4,8},{6,10},{8,4},{10,6},{12,0},{14,2},{16,28},{18,... | collective-permute-start | bytes 245768 | tf_op jit(solution)/shard_map/ppermute | solution.py:312
  21.8 2.7 %collective-permute-start.6 = (f32[8,64,128]{2,1,0:T(8,128)S(1)}, f32[8,64,128]{2,1,0:T(8,128)S(1)}, u32[]{:S(2)}, u32[]{:S(2)}) collective-permute-start(f32[8,64,128]{2,1,0:T(8,128)S(1)} %pad_maximum_fusion), channel_id=1, source_target_pairs={{0,2},{2,0},{4,6},{6,4},{8,10},{10,8},{12,14},{14,12},{16,18},{18,... | collective-permute-start | bytes 786440 | tf_op jit(solution)/shard_map/ppermute | solution.py:312
  21.9 2.0 %copy-start.3 = (f32[8,4096]{1,0:T(8,128)S(1)}, f32[8,4096]{1,0:T(8,128)}, u32[]{:S(2)}) copy-start(f32[8,4096]{1,0:T(8,128)} %omega_ref.1) | copy-start | bytes 393220
  21.9 2.0 %copy-start.4 = (f32[4096]{0:T(1024)S(1)}, f32[4096]{0:T(1024)}, u32[]{:S(2)}) copy-start(f32[4096]{0:T(1024)} %param.12) | copy-start | bytes 49156

commit v4 on v3

--- a/solution.py
+++ b/solution.py
@@ -15,13 +15,12 @@
 LOG2E = math.log2(math.e)
 COS = (
     1.0,
-    -19.739208743087787,
-    64.93938905249153,
-    -85.45665775372363,
-    60.24212493122888,
-    -26.404630623401626,
-    7.8000222194698186,
-    -1.4529875517062139,
+    -19.739204466576105,
+    64.93911592834385,
+    -85.4501134274465,
+    60.16742979141158,
+    -25.96688461044869,
+    6.527705959852582,
 )
 KERNEL_BYTES = 16 << 20
 TILE = 256
@@ -66,7 +65,7 @@
     turns = lax.dot_general(
         left.astype(f32).T.astype(bf16), right, (((1,), (0,)), ((), ())), preferred_element_type=f32
     )
-    rest = turns - jnp.floor(turns + 0.5)
+    rest = turns - jnp.round(turns)
     square = rest * rest
     scale = math.sqrt(2.0 / total)
     value = jnp.full(square.shape, COS[-1] * scale, f32)
@@ -209,72 +208,70 @@
     own_rows, which, near_ref, far_ref, other_ref, before_ref,
     near_near_ref, near_far_ref, far_far_ref,
     near_tile_ref, far_tile_ref, prior_ref, samples_ref, solution_ref,
-    field_ref, start_ref, direction_ref, packed_ref,
+    image_ref, start_ref, direction_ref, packed_ref,
 ):
     samples = prior_ref.shape[1]
     blocks, _, width = near_ref.shape
     half = blocks * width
     count = 2 * half
-    near_other = rows_of(other_ref, samples, 0, blocks)
-    far_other = rows_of(other_ref, samples, blocks, 2 * blocks)
-    near, far = near_other.astype(bf16), far_other.astype(bf16)
-    field_ref[:, :count] = (
-        before_ref[:, :count]
-        + product(near, near_near_ref[half:, :])
-        + product_transposed(far, near_far_ref[:, half:])
-    )
-    field_ref[:, count:] = (
-        before_ref[:, count:] + product(near, near_far_ref[half:, :]) + product(far, far_far_ref[half:, :])
-    )
-    start_ref[:, :half] = rows_of(near_ref, samples)
-    start_ref[:, half:count] = near_other
-    start_ref[:, count : count + half] = rows_of(far_ref, samples)
-    start_ref[:, count + half :] = far_other
+    tiles = [(j, slice(j, j + TILE), slice(j % count, j % count + TILE)) for j in range(0, 2 * count, TILE)]
+    for offset, block_ref, first in (
+        (0, near_ref, 0), (half, other_ref, 0), (count, far_ref, 0), (count + half, other_ref, blocks)
+    ):
+        for k in range(blocks):
+            start_ref[:, offset + k * width : offset + (k + 1) * width] = block_ref[first + k, :samples, :]
+    near = start_ref[:, half:count].astype(bf16)
+    far = start_ref[:, count + half :].astype(bf16)
 
     def total(values):
         return jnp.sum(values, axis=1, keepdims=True)
 
-    start = start_ref[...]
-    image = field_ref[...] + noise_level * start
-    norm0 = total(start * start)
-    alpha0 = norm0 / total(start * image)
-    residual = start - alpha0 * image
-    norm1 = total(residual * residual)
-    direction = residual + (norm1 / norm0) * start
-    direction_ref[...] = direction
-    packed_ref[...] = direction.astype(bf16)
-
-    curve = jnp.zeros((samples, min(TILE, count)), f32)
-    for j in range(0, 2 * count, TILE):
-        columns = slice(j, j + TILE)
-        offset = j % count
+    zero = jnp.zeros((samples, TILE), f32)
+    norm0, curve0, norm1, curve1 = zero, zero, zero, zero
+    for j, columns, inner in tiles:
+        value = before_ref[:, columns]
+        if j < count:
+            value += product(near, near_near_ref[half:, inner])
+            value += product_transposed(far, near_far_ref[inner, half:])
+        else:
+            value += product(near, near_far_ref[half:, inner])
+            value += product(far, far_far_ref[half:, inner])
+        start = start_ref[:, columns]
+        image = value + noise_level * start
+        image_ref[:, columns] = image
+        norm0 += start * start
+        curve0 += start * image
+    norm0 = total(norm0)
+    alpha0 = norm0 / total(curve0)
+    for _, columns, _ in tiles:
+        residual = start_ref[:, columns] - alpha0 * image_ref[:, columns]
+        direction_ref[:, columns] = residual
+        norm1 += residual * residual
+    norm1 = total(norm1)
+    beta = norm1 / norm0
+    for _, columns, _ in tiles:
+        direction = direction_ref[:, columns] + beta * start_ref[:, columns]
+        direction_ref[:, columns] = direction
+        packed_ref[:, columns] = direction.astype(bf16)
+
+    for j, columns, inner in tiles:
         diagonal, above = (near_near_ref, None) if j < count else (far_far_ref, near_far_ref)
-        value = jnp.zeros((samples, TILE), f32)
+        value = product(packed_ref[:, columns], diagonal[inner, inner])
         if above is not None:
-            value += jnp.dot(
-                packed_ref[:, :count], above[:, offset : offset + TILE], preferred_element_type=f32
-            )
-        if offset:
-            value += jnp.dot(
-                packed_ref[:, j - offset : j], diagonal[:offset, offset : offset + TILE],
-                preferred_element_type=f32,
-            )
-        value = 2.0 * value + jnp.dot(
-            packed_ref[:, columns], diagonal[offset : offset + TILE, offset : offset + TILE],
-            preferred_element_type=f32,
-        )
-        curve += direction_ref[:, columns] * (value + noise_level * direction_ref[:, columns])
-    alpha1 = norm1 / total(curve)
-    field = alpha0 * start_ref[...] + alpha1 * direction_ref[...]
-    weights = field.astype(bf16)
-    own_solution = field[:, :width].T
-    solution_ref[...] = jnp.where(which[0] == 0, own_solution[:own_rows], own_solution[own_rows:])
-    last = (((1,), (1,)), ((), ()))
-    samples_ref[...] = (
-        prior_ref[...]
-        + lax.dot_general(near_tile_ref[...], weights[:, :count], last, preferred_element_type=f32)
-        + lax.dot_general(far_tile_ref[...], weights[:, count:], last, preferred_element_type=f32)
-    )
+            value += 2.0 * product(packed_ref[:, :count], above[:, inner])
+        if inner.start:
+            value += 2.0 * product(packed_ref[:, j - inner.start : j], diagonal[: inner.start, inner])
+        direction = direction_ref[:, columns]
+        curve1 += direction * (value + noise_level * direction)
+    alpha1 = norm1 / total(curve1)
+    own = (alpha0 * start_ref[:, :width] + alpha1 * direction_ref[:, :width]).T
+    solution_ref[...] = jnp.where(which[0] == 0, own[:own_rows], own[own_rows:])
+    value = prior_ref[...]
+    for j, columns, inner in tiles:
+        weights = (alpha0 * start_ref[:, columns] + alpha1 * direction_ref[:, columns]).astype(bf16)
+        tile_ref = near_tile_ref if j < count else far_tile_ref
+        value += product_transposed(tile_ref[:, inner], weights)
+    samples_ref[...] = value
 
 
 def call(kernel, out_shape, inputs, scratch=(), scalars=0, hbm=False, flops=0):
@@ -334,7 +331,8 @@
     first = payload[None]
     bit = blocks // 2
     while bit > 4:
-        first = jnp.concatenate([first, exchange(first, bit)], axis=0)
+        moved = exchange(first, bit)
+        first = jnp.concatenate([first, moved], axis=0)
         bit //= 2
     third = exchange(first, 6)
     second = exchange(first, 4)

time: 28 us -> 27.8 us (level)
  transfers between devices with their start and end apart: 8 -> 8, of which waited for: 5 -> 6; matrix products, arithmetic and copies ran while one was open for 1% -> 1% of each run, Pallas kernels for 13% -> 13%
where the time goes in v4:
time: 27.8 us; the launch traced here: 27.7 us
  starting transfers between devices  11.2 us (40%)
  Pallas kernels  8.87 us (32%)
  waiting for transfers between devices  6.66 us (24%)
  between operations  0.77 us (3%)
    ppermute x6, starting transfers between devices, exchange(): return lax.ppermute(values, 'train', [(i, i ^ bit) for i in range(blocks)])  6.67 us
    ppermute x6, waiting for transfers between devices, exchange(): return lax.ppermute(values, 'train', [(i, i ^ bit) for i in range(blocks)])  5.93 us
    pallas_call x1, Pallas kernels, local_body(): call(functools.partial(solve_kernel, own_rows), (shape((per_device, sampl...  3.25 us
    ppermute x1, starting transfers between devices, local_body(): other = lax.ppermute(partial, 'cand', swap)  3.04 us
    pallas_call x1, Pallas kernels, local_body(): call(prior_kernel, shape((samples, width), f32), scalars=1, inputs=6, hbm...  2.09 us
    pallas_call x1, Pallas kernels, local_body(): call(far_kernel, (square, square, shape((per_device, count), bf16), shape...  1.96 us
    ppermute x1, starting transfers between devices, local_body(): other_weights = lax.ppermute(weights, 'cand', swap)  1.49 us
    pallas_call x1, Pallas kernels, local_body(): call(near_kernel, (shape((count, stack), bf16), shape((stack, count), bf1...  0.97 us
  transfers between devices with their start and end apart: 8, of which 6 were waited for; matrix products, arithmetic and copies ran while one was open for 1% of the time, Pallas kernels for 13%

profile of v4, /device:TPU:0, one launch (start us, length us, event | category | flops | bytes accessed | tf_op | source)
XLA Modules:
  0.0 27.7 jit_solution(18429469972949412689)
XLA Ops:
  0.6 0.0 copy-start
  0.6 0.0 copy-start.2
  0.7 0.0 copy-start.1
  0.7 2.1 %shard_map.86.mine_ref = f32[64,128]{1,0:T(8,128)S(1)} custom-call(s32[1]{0:T(128)} %bitcast.which, f32[8,128]{1,0:T(8,128)} %x_ref.1, f32[8,4096]{1,0:T(8,128)} %omega_ref.1, f32[1,4096]{1,0:T(1,128)} %bitcast.11, bf16[64,2048]{1,0:T(8,128)(2,1)} %bitcast.8, f32[1,64]{1,0:T(1,128)} %bitcast.13, f32[64,64]{1,0:T(8,128)} %noise_hbm.1), custom_call_target="tpu_custom_call" | custom-call | flops 1073741824 | bytes 1048576 | tf_op jit(solution)/shard_map/pallas_call | solution.py:312
  2.8 3.0 %collective-permute-start = (f32[64,128]{1,0:T(8,128)S(1)}, f32[64,128]{1,0:T(8,128)S(1)}, u32[]{:S(2)}, u32[]{:S(2)}) collective-permute-start(f32[64,128]{1,0:T(8,128)S(1)} %shard_map.86.mine_ref), channel_id=1, source_target_pairs={{0,1},{1,0},{2,3},{3,2},{4,5},{5,4},{6,7},{7,6},{8,9},{9,8},{10,11... | collective-permute-start | bytes 98312 | tf_op jit(solution)/shard_map/ppermute | solution.py:326
  5.8 0.0 copy-done.1
  5.8 0.0 collective-permute-start.1
  5.8 1.2 %collective-permute-done.1.pair_ref = f32[8,128]{1,0:T(8,128)S(1)} collective-permute-done((f32[8,128]{1,0:T(8,128)S(1)}, f32[8,128]{1,0:T(8,128)S(1)}, u32[]{:S(2)}, u32[]{:S(2)}) %collective-permute-start.1) | collective-permute-done | bytes 4128 | tf_op jit(solution)/shard_map/ppermute | solution.py:309
  7.0 0.7 %collective-permute-done.other_ref = f32[64,128]{1,0:T(8,128)S(1)} collective-permute-done((f32[64,128]{1,0:T(8,128)S(1)}, f32[64,128]{1,0:T(8,128)S(1)}, u32[]{:S(2)}, u32[]{:S(2)}) %collective-permute-start) | collective-permute-done | bytes 32800 | tf_op jit(solution)/shard_map/ppermute | solution.py:326
  7.7 3.1 %collective-permute-start.2 = (f32[1,80,128]{2,1,0:T(8,128)S(1)}, f32[1,80,128]{2,1,0:T(8,128)S(1)}, u32[]{:S(2)}, u32[]{:S(2)}) collective-permute-start(f32[1,80,128]{2,1,0:T(8,128)S(1)} %bitcast.5), channel_id=1, source_target_pairs={{0,16},{2,18},{4,20},{6,22},{8,24},{10,26},{12,28},{14,30},{16,0},... | collective-permute-start | bytes 122888 | tf_op jit(solution)/shard_map/ppermute | solution.py:309
  10.8 0.0 copy-done.2
  10.8 1.5 %collective-permute-start.7 = (bf16[64,2048]{1,0:T(8,128)(2,1)S(1)}, bf16[64,2048]{1,0:T(8,128)(2,1)S(1)}, u32[]{:S(2)}, u32[]{:S(2)}) collective-permute-start(bf16[64,2048]{1,0:T(8,128)(2,1)S(1)} %bitcast.9), channel_id=1, source_target_pairs={{0,1},{1,0},{2,3},{3,2},{4,5},{5,4},{6,7},{7,6},{8,9},{9,8},{10,11... | collective-permute-start | bytes 786440 | tf_op jit(solution)/shard_map/ppermute | solution.py:330
  12.3 0.5 %collective-permute-done.2 = f32[1,80,128]{2,1,0:T(8,128)S(1)} collective-permute-done((f32[1,80,128]{2,1,0:T(8,128)S(1)}, f32[1,80,128]{2,1,0:T(8,128)S(1)}, u32[]{:S(2)}, u32[]{:S(2)}) %collective-permute-start.2) | collective-permute-done | bytes 40992 | tf_op jit(solution)/shard_map/ppermute | solution.py:309
  12.8 1.9 %collective-permute-start.3 = (f32[2,80,128]{2,1,0:T(8,128)S(1)}, f32[2,80,128]{2,1,0:T(8,128)S(1)}, u32[]{:S(2)}, u32[]{:S(2)}) collective-permute-start(f32[2,80,128]{2,1,0:T(8,128)S(1)} %pad_maximum_fusion.2), channel_id=1, source_target_pairs={{0,4},{2,6},{4,0},{6,2},{8,12},{10,14},{12,8},{14,10},{16,20},{18,... | collective-permute-start | bytes 245768 | tf_op jit(solution)/shard_map/ppermute | solution.py:309
  14.7 0.0 copy-done
  14.7 0.1 constant_dynamic-slice_fusion.cand_ref.x_ref
  14.8 1.6 %collective-permute-start.4 = (f32[2,80,128]{2,1,0:T(8,128)S(1)}, f32[2,80,128]{2,1,0:T(8,128)S(1)}, u32[]{:S(2)}, u32[]{:S(2)}) collective-permute-start(f32[2,80,128]{2,1,0:T(8,128)S(1)} %pad_maximum_fusion.2), channel_id=1, source_target_pairs={{0,8},{2,10},{4,12},{6,14},{8,0},{10,2},{12,4},{14,6},{16,24},{18,... | collective-permute-start | bytes 245768 | tf_op jit(solution)/shard_map/ppermute | solution.py:309
  16.3 0.1 collective-permute-start.5
  16.4 1.8 %collective-permute-done.3 = f32[2,80,128]{2,1,0:T(8,128)S(1)} collective-permute-done((f32[2,80,128]{2,1,0:T(8,128)S(1)}, f32[2,80,128]{2,1,0:T(8,128)S(1)}, u32[]{:S(2)}, u32[]{:S(2)}) %collective-permute-start.3) | collective-permute-done | bytes 81952 | tf_op jit(solution)/shard_map/ppermute | solution.py:309
  18.1 1.0 %shard_map.88 = (bf16[1024,64]{1,0:T(8,128)(2,1)S(1)}, bf16[64,1024]{1,0:T(8,128)(2,1)S(1)}, bf16[32,64]{1,0:T(8,128)(2,1)S(1)}, bf16[1024,1024]{1,0:T(8,128)(2,...) custom-call(f32[4,80,128]{2,1,0:T(8,128)S(1)} %pad_maximum_fusion.1.block_ref.near_ref, ...), custom_call_target="tpu_custom_call" | custom-call | flops 2147483648 | bytes 1048576 | tf_op jit(solution)/shard_map/pallas_call | solution.py:349
  19.1 0.1 collective-permute-done.4
  19.2 2.5 %collective-permute-done.5 = f32[2,80,128]{2,1,0:T(8,128)S(1)} collective-permute-done((f32[2,80,128]{2,1,0:T(8,128)S(1)}, f32[2,80,128]{2,1,0:T(8,128)S(1)}, u32[]{:S(2)}, u32[]{:S(2)}) %collective-permute-start.5) | collective-permute-done | bytes 81952 | tf_op jit(solution)/shard_map/ppermute | solution.py:309
  21.7 0.1 collective-permute-start.6
  21.8 0.0 copy-start.3
  21.8 0.0 copy-start.4
  21.8 2.0 %shard_map.89 = (bf16[1024,1024]{1,0:T(8,128)(2,1)S(1)}, bf16[1024,1024]{1,0:T(8,128)(2,1)S(1)}, bf16[32,1024]{1,0:T(8,128)(2,1)S(1)}, f32[64,2048]{1,0:T(8,128)S(1)}) custom-call(f32[4,80,128]{2,1,0:T(8,128)S(1)} %constant_dynamic-update-slice_fusion.block_ref.far_ref, f32[4,80,128]{2,1,0:T(8,128)S(1)} %pad_maximum_fusion.1.block_ref.near_ref, ...), custom_call_target="tpu_custom_call" | custom-call | flops 8589934592 | bytes 1048576 | tf_op jit(solution)/shard_map/pallas_call | solution.py:362
  23.8 0.0 collective-permute-done.7.other_ref
  23.8 0.0 copy-done.3
  23.8 0.0 copy-done.4
  23.8 0.6 %shard_map.90.prior_ref = f32[32,64]{1,0:T(8,128)S(1)} custom-call(s32[1]{0:T(128)} %bitcast.which, f32[8,32]{1,0:T(8,128)S(1)} %constant_dynamic-slice_fusion.cand_ref.x_ref, f32[8,4096]{1,0:T(8,128)S(1)} %copy-done.3, f32[1,4096]{1,0:T(1,128)S(1)} %bitcast.12, bf16[64,2048]{1,0:T(8,128)(2,1)S(1)} %bitcast.10, ...), custom_call_target="tpu_custom_call" | custom-call | flops 1073741824 | bytes 1048576 | tf_op jit(solution)/shard_map/pallas_call | solution.py:343
  24.4 0.0 collective-permute-done.6.other_ref
  24.4 3.3 %shard_map.91 = (f32[32,64]{1,0:T(8,128)}, f32[64,64]{1,0:T(8,128)}) custom-call(s32[1]{0:T(128)} %bitcast.which, f32[4,80,128]{2,1,0:T(8,128)S(1)} %pad_maximum_fusion.1.block_ref.near_ref, f32[4,80,128]{2,1,0:T(8,128)S(1)} %constant_dynamic-update-slice_fusion.block_ref.far_ref, f32[8,64,128]{2,1,0:T(8,128)S(1)} %collective-permute-done.6.other_ref, ...), custom_call_target="tpu_custom_call" | custom-call | flops 8589934592 | bytes 1048576 | tf_op jit(solution)/shard_map/pallas_call | solution.py:369
  (8 shorter events, 0.1 us)
Async XLA Ops:
  0.6 14.0 %copy-start = (f32[8,512]{1,0:T(8,128)S(1)}, f32[8,512]{1,0:T(8,128)}, u32[]{:S(2)}) copy-start(f32[8,512]{1,0:T(8,128)} %param.8) | copy-start | bytes 49156
  0.6 10.2 %copy-start.2 = (bf16[2048,64]{0,1:T(8,128)(2,1)S(1)}, bf16[2048,64]{0,1:T(8,128)(2,1)}, u32[]{:S(2)}) copy-start(bf16[2048,64]{0,1:T(8,128)(2,1)} %param.13) | copy-start | bytes 786436
  0.7 5.2 %copy-start.1 = (f32[8,128]{1,0:T(8,128)S(1)}, f32[8,128]{1,0:T(8,128)}, u32[]{:S(2)}) copy-start(f32[8,128]{1,0:T(8,128)} %x_ref.1) | copy-start | bytes 12292
  2.8 4.9 %collective-permute-start = (f32[64,128]{1,0:T(8,128)S(1)}, f32[64,128]{1,0:T(8,128)S(1)}, u32[]{:S(2)}, u32[]{:S(2)}) collective-permute-start(f32[64,128]{1,0:T(8,128)S(1)} %shard_map.86.mine_ref), channel_id=1, source_target_pairs={{0,1},{1,0},{2,3},{3,2},{4,5},{5,4},{6,7},{7,6},{8,9},{9,8},{10,11... | collective-permute-start | bytes 98312 | tf_op jit(solution)/shard_map/ppermute | solution.py:326
  5.8 1.2 %collective-permute-start.1 = (f32[8,128]{1,0:T(8,128)S(1)}, f32[8,128]{1,0:T(8,128)S(1)}, u32[]{:S(2)}, u32[]{:S(2)}) collective-permute-start(f32[8,128]{1,0:T(8,128)S(1)} %copy-done.1), channel_id=1, source_target_pairs={{0,2},{2,0},{4,6},{6,4},{8,10},{10,8},{12,14},{14,12},{16,18},{18,... | collective-permute-start | bytes 12296 | tf_op jit(solution)/shard_map/ppermute | solution.py:309
  7.7 5.1 %collective-permute-start.2 = (f32[1,80,128]{2,1,0:T(8,128)S(1)}, f32[1,80,128]{2,1,0:T(8,128)S(1)}, u32[]{:S(2)}, u32[]{:S(2)}) collective-permute-start(f32[1,80,128]{2,1,0:T(8,128)S(1)} %bitcast.5), channel_id=1, source_target_pairs={{0,16},{2,18},{4,20},{6,22},{8,24},{10,26},{12,28},{14,30},{16,0},... | collective-permute-start | bytes 122888 | tf_op jit(solution)/shard_map/ppermute | solution.py:309
  10.8 12.9 %collective-permute-start.7 = (bf16[64,2048]{1,0:T(8,128)(2,1)S(1)}, bf16[64,2048]{1,0:T(8,128)(2,1)S(1)}, u32[]{:S(2)}, u32[]{:S(2)}) collective-permute-start(bf16[64,2048]{1,0:T(8,128)(2,1)S(1)} %bitcast.9), channel_id=1, source_target_pairs={{0,1},{1,0},{2,3},{3,2},{4,5},{5,4},{6,7},{7,6},{8,9},{9,8},{10,11... | collective-permute-start | bytes 786440 | tf_op jit(solution)/shard_map/ppermute | solution.py:330
  12.8 5.3 %collective-permute-start.3 = (f32[2,80,128]{2,1,0:T(8,128)S(1)}, f32[2,80,128]{2,1,0:T(8,128)S(1)}, u32[]{:S(2)}, u32[]{:S(2)}) collective-permute-start(f32[2,80,128]{2,1,0:T(8,128)S(1)} %pad_maximum_fusion.2), channel_id=1, source_target_pairs={{0,4},{2,6},{4,0},{6,2},{8,12},{10,14},{12,8},{14,10},{16,20},{18,... | collective-permute-start | bytes 245768 | tf_op jit(solution)/shard_map/ppermute | solution.py:309
  14.8 4.4 %collective-permute-start.4 = (f32[2,80,128]{2,1,0:T(8,128)S(1)}, f32[2,80,128]{2,1,0:T(8,128)S(1)}, u32[]{:S(2)}, u32[]{:S(2)}) collective-permute-start(f32[2,80,128]{2,1,0:T(8,128)S(1)} %pad_maximum_fusion.2), channel_id=1, source_target_pairs={{0,8},{2,10},{4,12},{6,14},{8,0},{10,2},{12,4},{14,6},{16,24},{18,... | collective-permute-start | bytes 245768 | tf_op jit(solution)/shard_map/ppermute | solution.py:309
  16.3 5.3 %collective-permute-start.5 = (f32[2,80,128]{2,1,0:T(8,128)S(1)}, f32[2,80,128]{2,1,0:T(8,128)S(1)}, u32[]{:S(2)}, u32[]{:S(2)}) collective-permute-start(f32[2,80,128]{2,1,0:T(8,128)S(1)} %pad_maximum_fusion.2), channel_id=1, source_target_pairs={{0,12},{2,14},{4,8},{6,10},{8,4},{10,6},{12,0},{14,2},{16,28},{18,... | collective-permute-start | bytes 245768 | tf_op jit(solution)/shard_map/ppermute | solution.py:309
  21.7 2.7 %collective-permute-start.6 = (f32[8,64,128]{2,1,0:T(8,128)S(1)}, f32[8,64,128]{2,1,0:T(8,128)S(1)}, u32[]{:S(2)}, u32[]{:S(2)}) collective-permute-start(f32[8,64,128]{2,1,0:T(8,128)S(1)} %pad_maximum_fusion), channel_id=1, source_target_pairs={{0,2},{2,0},{4,6},{6,4},{8,10},{10,8},{12,14},{14,12},{16,18},{18,... | collective-permute-start | bytes 786440 | tf_op jit(solution)/shard_map/ppermute | solution.py:309
  21.8 2.0 %copy-start.3 = (f32[8,4096]{1,0:T(8,128)S(1)}, f32[8,4096]{1,0:T(8,128)}, u32[]{:S(2)}) copy-start(f32[8,4096]{1,0:T(8,128)} %omega_ref.1) | copy-start | bytes 393220
  21.8 2.0 %copy-start.4 = (f32[4096]{0:T(1024)S(1)}, f32[4096]{0:T(1024)}, u32[]{:S(2)}) copy-start(f32[4096]{0:T(1024)} %param.12) | copy-start | bytes 49156

commit v5 on v4

--- a/solution.py
+++ b/solution.py
@@ -139,15 +139,18 @@
     return right_stack(points, eight_rows([1.0] * 3 + halves_of(points), points.shape[1]))
 
 
-def fill(out_ref, left_ref, right_ref):
+def fill(out_ref, left_ref, right_ref, transposed_ref=None):
     rows, columns = out_ref.shape
     for i in range(0, rows, TILE):
-        for j in range(0, columns, TILE):
+        for j in range(i if transposed_ref is out_ref else 0, columns, TILE):
             height, width = min(TILE, rows - i), min(TILE, columns - j)
             exponent = jnp.dot(
                 left_ref[i : i + height, :], right_ref[:, j : j + width], preferred_element_type=f32
             )
-            out_ref[i : i + height, j : j + width] = jnp.exp2(exponent).astype(bf16)
+            tile = jnp.exp2(exponent).astype(bf16)
+            out_ref[i : i + height, j : j + width] = tile
+            if transposed_ref is not None and (transposed_ref is not out_ref or j > i):
+                transposed_ref[j : j + width, i : i + height] = tile.T
 
 
 def points_of(block_ref, samples):
@@ -188,25 +191,31 @@
 
 def far_kernel(
     block_ref, near_ref, left_ref, right_ref, cand_left_ref, before_ref,
-    near_far_ref, far_far_ref, tile_ref, field_ref,
+    near_far_ref, far_near_ref, far_far_ref, tile_ref, field_ref,
     far_left_ref, far_right_ref,
 ):
     samples = field_ref.shape[0]
     points = points_of(block_ref, samples)
     far_left_ref[...] = left_of(points)
     far_right_ref[...] = right_of(points)
-    fill(near_far_ref, left_ref, far_right_ref)
-    fill(far_far_ref, far_left_ref, far_right_ref)
+    fill(near_far_ref, left_ref, far_right_ref, far_near_ref)
+    fill(far_far_ref, far_left_ref, far_right_ref, far_far_ref)
     fill(tile_ref, cand_left_ref, far_right_ref)
     half, count = points.shape[1] // 2, points.shape[1]
     near, far = rows_of(near_ref, samples).astype(bf16), rows_of(block_ref, samples).astype(bf16)
-    field_ref[:, :count] = before_ref[...] + product_transposed(far, near_far_ref[:, :half])
+    field_ref[:, :count] = before_ref[...] + product(far, far_near_ref[:half, :])
     field_ref[:, count:] = product(near, near_far_ref[:half, :]) + product(far, far_far_ref[:half, :])
 
 
+def near_join_kernel(other_ref, before_ref, kernel_ref, field_ref):
+    half = kernel_ref.shape[0] // 2
+    rows = rows_of(other_ref, other_ref.shape[1]).astype(bf16)
+    field_ref[...] = before_ref[...] + product(rows, kernel_ref[half:, :])
+
+
 def solve_kernel(
-    own_rows, which, near_ref, far_ref, other_ref, before_ref,
-    near_near_ref, near_far_ref, far_far_ref,
+    own_rows, which, near_ref, far_ref, near_other_ref, far_other_ref, before_ref,
+    near_near_ref, near_far_ref, far_near_ref, far_far_ref,
     near_tile_ref, far_tile_ref, prior_ref, samples_ref, solution_ref,
     image_ref, start_ref, direction_ref, packed_ref,
 ):
@@ -215,11 +224,10 @@
     half = blocks * width
     count = 2 * half
     tiles = [(j, slice(j, j + TILE), slice(j % count, j % count + TILE)) for j in range(0, 2 * count, TILE)]
-    for offset, block_ref, first in (
-        (0, near_ref, 0), (half, other_ref, 0), (count, far_ref, 0), (count + half, other_ref, blocks)
-    ):
+    for quarter, block_ref in enumerate((near_ref, near_other_ref, far_ref, far_other_ref)):
         for k in range(blocks):
-            start_ref[:, offset + k * width : offset + (k + 1) * width] = block_ref[first + k, :samples, :]
+            offset = quarter * half + k * width
+            start_ref[:, offset : offset + width] = block_ref[k, :samples, :]
     near = start_ref[:, half:count].astype(bf16)
     far = start_ref[:, count + half :].astype(bf16)
 
@@ -231,8 +239,7 @@
     for j, columns, inner in tiles:
         value = before_ref[:, columns]
         if j < count:
-            value += product(near, near_near_ref[half:, inner])
-            value += product_transposed(far, near_far_ref[inner, half:])
+            value += product(far, far_near_ref[half:, inner])
         else:
             value += product(near, near_far_ref[half:, inner])
             value += product(far, far_far_ref[half:, inner])
@@ -358,10 +365,14 @@
         ),
         inputs=2, flops=1 << 31,
     )(near, mine)
-    other = exchange(jnp.concatenate([near[:, :samples], far[:, :samples]], axis=0), 1)
-    near_far, far_far, far_tile, before = call(
+    near_other = exchange(near[:, :samples], 1)
+    before = call(near_join_kernel, shape((samples, count), f32), inputs=3, flops=1 << 30)(
+        near_other, before, near_near
+    )
+    far_other = exchange(far[:, :samples], 1)
+    near_far, far_near, far_far, far_tile, before = call(
         far_kernel,
-        (square, square, shape((per_device, count), bf16), shape((samples, 2 * count), f32)),
+        (square, square, square, shape((per_device, count), bf16), shape((samples, 2 * count), f32)),
         scratch=[pltpu.VMEM((count, stack), bf16), pltpu.VMEM((stack, count), bf16)],
         inputs=6, flops=1 << 33,
     )(far, near, left, right, cand_left, before)
@@ -375,9 +386,9 @@
                 pltpu.VMEM((samples, 2 * count), f32),
                 pltpu.VMEM((samples, 2 * count), bf16),
             ],
-            scalars=1, inputs=10, flops=1 << 33,
+            scalars=1, inputs=12, flops=1 << 33,
         )(
-            which, near, far, other, before, near_near, near_far, far_far,
+            which, near, far, near_other, far_other, before, near_near, near_far, far_near, far_far,
             near_tile, far_tile, prior_cand,
         )
     )

time: 27.8 us -> 27.6 us (level)
    pallas_call x1, Pallas kernels: 3.25 us -> 2.93 us  [local_body(): call(functools.partial(solve_kernel, own_rows), (shape((per_device, sampl...]
    pallas_call x1 -> x2, Pallas kernels: 1.96 us -> 2.14 us  [the longest x1 1.82 us: local_body(): call(far_kernel, (square, square, square, shape((per_device, count), bf16...]
    ppermute x6 -> x7, waiting for transfers between devices: 5.93 us -> 5.81 us  [exchange(): return lax.ppermute(values, 'train', [(i, i ^ bit) for i in range(blocks)])]
    ppermute x6 -> x7, starting transfers between devices: 6.67 us -> 6.74 us  [exchange(): return lax.ppermute(values, 'train', [(i, i ^ bit) for i in range(blocks)])]
  transfers between devices with their start and end apart: 8 -> 9, of which waited for: 6 -> 5; matrix products, arithmetic and copies ran while one was open for 1% -> 0% of each run, Pallas kernels for 13% -> 13%
where the time goes in v5:
time: 27.6 us; the launch traced here: 27.5 us
  starting transfers between devices  11.3 us (41%)
  Pallas kernels  8.73 us (32%)
  waiting for transfers between devices  6.54 us (24%)
  between operations  0.79 us (3%)
    ppermute x7, starting transfers between devices, exchange(): return lax.ppermute(values, 'train', [(i, i ^ bit) for i in range(blocks)])  6.74 us
    ppermute x7, waiting for transfers between devices, exchange(): return lax.ppermute(values, 'train', [(i, i ^ bit) for i in range(blocks)])  5.81 us
    ppermute x1, starting transfers between devices, local_body(): other = lax.ppermute(partial, 'cand', swap)  3.04 us
    pallas_call x1, Pallas kernels, local_body(): call(functools.partial(solve_kernel, own_rows), (shape((per_device, sampl...  2.93 us
    pallas_call x1, Pallas kernels, local_body(): call(prior_kernel, shape((samples, width), f32), scalars=1, inputs=6, hbm...  2.09 us
    pallas_call x1, Pallas kernels, local_body(): call(far_kernel, (square, square, square, shape((per_device, count), bf16...  1.82 us
    ppermute x1, starting transfers between devices, local_body(): other_weights = lax.ppermute(weights, 'cand', swap)  1.49 us
    pallas_call x1, Pallas kernels, local_body(): call(near_kernel, (shape((count, stack), bf16), shape((stack, count), bf1...  0.97 us
  transfers between devices with their start and end apart: 9, of which 5 were waited for; matrix products, arithmetic and copies ran while one was open for 0% of the time, Pallas kernels for 13%

profile of v5, /device:TPU:0, one launch (start us, length us, event | category | flops | bytes accessed | tf_op | source)
XLA Modules:
  0.0 27.5 jit_solution(2745785624328716254)
XLA Ops:
  0.6 0.0 copy-start
  0.6 0.0 copy-start.2
  0.7 0.0 copy-start.1
  0.7 2.1 %shard_map.86.mine_ref = f32[64,128]{1,0:T(8,128)S(1)} custom-call(s32[1]{0:T(128)} %bitcast.which, f32[8,128]{1,0:T(8,128)} %x_ref.1, f32[8,4096]{1,0:T(8,128)} %omega_ref.1, f32[1,4096]{1,0:T(1,128)} %bitcast.11, bf16[64,2048]{1,0:T(8,128)(2,1)} %bitcast.8, f32[1,64]{1,0:T(1,128)} %bitcast.13, f32[64,64]{1,0:T(8,128)} %noise_hbm.1), custom_call_target="tpu_custom_call" | custom-call | flops 1073741824 | bytes 1048576 | tf_op jit(solution)/shard_map/pallas_call | solution.py:319
  2.8 3.0 %collective-permute-start = (f32[64,128]{1,0:T(8,128)S(1)}, f32[64,128]{1,0:T(8,128)S(1)}, u32[]{:S(2)}, u32[]{:S(2)}) collective-permute-start(f32[64,128]{1,0:T(8,128)S(1)} %shard_map.86.mine_ref), channel_id=1, source_target_pairs={{0,1},{1,0},{2,3},{3,2},{4,5},{5,4},{6,7},{7,6},{8,9},{9,8},{10,11... | collective-permute-start | bytes 98312 | tf_op jit(solution)/shard_map/ppermute | solution.py:333
  5.8 0.0 copy-done.1
  5.8 0.0 collective-permute-start.1
  5.8 1.2 %collective-permute-done.1.pair_ref = f32[8,128]{1,0:T(8,128)S(1)} collective-permute-done((f32[8,128]{1,0:T(8,128)S(1)}, f32[8,128]{1,0:T(8,128)S(1)}, u32[]{:S(2)}, u32[]{:S(2)}) %collective-permute-start.1) | collective-permute-done | bytes 4128 | tf_op jit(solution)/shard_map/ppermute | solution.py:316
  7.0 0.7 %collective-permute-done.other_ref = f32[64,128]{1,0:T(8,128)S(1)} collective-permute-done((f32[64,128]{1,0:T(8,128)S(1)}, f32[64,128]{1,0:T(8,128)S(1)}, u32[]{:S(2)}, u32[]{:S(2)}) %collective-permute-start) | collective-permute-done | bytes 32800 | tf_op jit(solution)/shard_map/ppermute | solution.py:333
  7.7 3.1 %collective-permute-start.2 = (f32[1,80,128]{2,1,0:T(8,128)S(1)}, f32[1,80,128]{2,1,0:T(8,128)S(1)}, u32[]{:S(2)}, u32[]{:S(2)}) collective-permute-start(f32[1,80,128]{2,1,0:T(8,128)S(1)} %bitcast.5), channel_id=1, source_target_pairs={{0,16},{2,18},{4,20},{6,22},{8,24},{10,26},{12,28},{14,30},{16,0},... | collective-permute-start | bytes 122888 | tf_op jit(solution)/shard_map/ppermute | solution.py:316
  10.8 0.0 copy-done.2
  10.8 1.5 %collective-permute-start.8 = (bf16[64,2048]{1,0:T(8,128)(2,1)S(1)}, bf16[64,2048]{1,0:T(8,128)(2,1)S(1)}, u32[]{:S(2)}, u32[]{:S(2)}) collective-permute-start(bf16[64,2048]{1,0:T(8,128)(2,1)S(1)} %bitcast.9), channel_id=1, source_target_pairs={{0,1},{1,0},{2,3},{3,2},{4,5},{5,4},{6,7},{7,6},{8,9},{9,8},{10,11... | collective-permute-start | bytes 786440 | tf_op jit(solution)/shard_map/ppermute | solution.py:337
  12.3 0.5 %collective-permute-done.2 = f32[1,80,128]{2,1,0:T(8,128)S(1)} collective-permute-done((f32[1,80,128]{2,1,0:T(8,128)S(1)}, f32[1,80,128]{2,1,0:T(8,128)S(1)}, u32[]{:S(2)}, u32[]{:S(2)}) %collective-permute-start.2) | collective-permute-done | bytes 40992 | tf_op jit(solution)/shard_map/ppermute | solution.py:316
  12.8 1.9 %collective-permute-start.3 = (f32[2,80,128]{2,1,0:T(8,128)S(1)}, f32[2,80,128]{2,1,0:T(8,128)S(1)}, u32[]{:S(2)}, u32[]{:S(2)}) collective-permute-start(f32[2,80,128]{2,1,0:T(8,128)S(1)} %pad_maximum_fusion.1), channel_id=1, source_target_pairs={{0,4},{2,6},{4,0},{6,2},{8,12},{10,14},{12,8},{14,10},{16,20},{18,... | collective-permute-start | bytes 245768 | tf_op jit(solution)/shard_map/ppermute | solution.py:316
  14.7 0.1 constant_dynamic-slice_fusion.cand_ref.x_ref
  14.8 1.6 %collective-permute-start.4 = (f32[2,80,128]{2,1,0:T(8,128)S(1)}, f32[2,80,128]{2,1,0:T(8,128)S(1)}, u32[]{:S(2)}, u32[]{:S(2)}) collective-permute-start(f32[2,80,128]{2,1,0:T(8,128)S(1)} %pad_maximum_fusion.1), channel_id=1, source_target_pairs={{0,8},{2,10},{4,12},{6,14},{8,0},{10,2},{12,4},{14,6},{16,24},{18,... | collective-permute-start | bytes 245768 | tf_op jit(solution)/shard_map/ppermute | solution.py:316
  16.3 0.1 collective-permute-start.5
  16.4 1.8 %collective-permute-done.3 = f32[2,80,128]{2,1,0:T(8,128)S(1)} collective-permute-done((f32[2,80,128]{2,1,0:T(8,128)S(1)}, f32[2,80,128]{2,1,0:T(8,128)S(1)}, u32[]{:S(2)}, u32[]{:S(2)}) %collective-permute-start.3) | collective-permute-done | bytes 81952 | tf_op jit(solution)/shard_map/ppermute | solution.py:316
  18.1 0.0 copy-start.3
  18.2 0.0 copy-start.4
  18.2 1.0 %shard_map.88 = (bf16[1024,64]{1,0:T(8,128)(2,1)S(1)}, bf16[64,1024]{1,0:T(8,128)(2,1)S(1)}, bf16[32,64]{1,0:T(8,128)(2,1)S(1)}, bf16[1024,1024]{1,0:T(8,128)(2,...) custom-call(f32[4,80,128]{2,1,0:T(8,128)S(1)} %pad_maximum_fusion.block_ref.near_ref, ...), custom_call_target="tpu_custom_call" | custom-call | flops 2147483648 | bytes 1048576 | tf_op jit(solution)/shard_map/pallas_call | solution.py:356
  19.2 0.1 collective-permute-start.6
  19.2 0.0 collective-permute-done.4
  19.3 2.4 %collective-permute-done.5 = f32[2,80,128]{2,1,0:T(8,128)S(1)} collective-permute-done((f32[2,80,128]{2,1,0:T(8,128)S(1)}, f32[2,80,128]{2,1,0:T(8,128)S(1)}, u32[]{:S(2)}, u32[]{:S(2)}) %collective-permute-start.5) | collective-permute-done | bytes 81952 | tf_op jit(solution)/shard_map/ppermute | solution.py:316
  21.7 0.1 collective-permute-start.7
  21.8 0.0 collective-permute-done.8.other_ref
  21.8 0.6 %shard_map.91.prior_ref = f32[32,64]{1,0:T(8,128)S(1)} custom-call(s32[1]{0:T(128)} %bitcast.which, f32[8,32]{1,0:T(8,128)S(1)} %constant_dynamic-slice_fusion.cand_ref.x_ref, f32[8,4096]{1,0:T(8,128)S(1)} %copy-done.3, f32[1,4096]{1,0:T(1,128)S(1)} %bitcast.12, bf16[64,2048]{1,0:T(8,128)(2,1)S(1)} %bitcast.10, ...), custom_call_target="tpu_custom_call" | custom-call | flops 1073741824 | bytes 1048576 | tf_op jit(solution)/shard_map/pallas_call | solution.py:350
  22.4 0.0 collective-permute-done.6.other_ref.near_other_ref
  22.4 0.3 %shard_map.89.before_ref = f32[64,1024]{1,0:T(8,128)S(1)} custom-call(f32[4,64,128]{2,1,0:T(8,128)S(1)} %collective-permute-done.6.other_ref.near_other_ref, f32[64,1024]{1,0:T(8,128)S(1)} %get-tuple-element.16.before_ref, bf16[1024,1024]{1,0:T(8,128)(2,1)S(1)} %get-tuple-element.17.kernel_ref.near_near_ref), custom_call_target="tpu_custom_call" | custom-call | flops 1073741824 | bytes 1048576 | tf_op jit(solution)/shard_map/pallas_call | solution.py:369
  22.7 1.8 %shard_map.90 = (bf16[1024,1024]{1,0:T(8,128)(2,1)S(1)}, bf16[1024,1024]{1,0:T(8,128)(2,1)S(1)}, bf16[1024,1024]{1,0:T(8,128)(2,1)S(1)}, bf16[32,1024]{1,0:T(8,128)(2,1)S(1)}, f32[64,2048]{1,0:T(8,128)S(1)}) custom-call(f32[4,80,128]{2,1,0:T(8,128)S(1)} %constant_dynamic-update-slice_fusion.block_ref.far_ref, ...), custom_call_target="tpu_custom_call" | custom-call | flops 8589934592 | bytes 1048576 | tf_op jit(solution)/shard_map/pallas_call | solution.py:373
  24.5 0.0 collective-permute-done.7.far_other_ref
  24.6 2.9 %shard_map.92 = (f32[32,64]{1,0:T(8,128)}, f32[64,64]{1,0:T(8,128)}) custom-call(s32[1]{0:T(128)} %bitcast.which, f32[4,80,128]{2,1,0:T(8,128)S(1)} %pad_maximum_fusion.block_ref.near_ref, f32[4,80,128]{2,1,0:T(8,128)S(1)} %constant_dynamic-update-slice_fusion.block_ref.far_ref, f32[4,64,128]{2,1,0:T(8,128)S(1)} %collective-permute-done.6.other_ref.near_other_ref, ...), custom_call_target="tpu_custom_call" | custom-call | flops 8589934592 | bytes 1048576 | tf_op jit(solution)/shard_map/pallas_call | solution.py:380
  (10 shorter events, 0.1 us)
Async XLA Ops:
  0.6 14.0 %copy-start = (f32[8,512]{1,0:T(8,128)S(1)}, f32[8,512]{1,0:T(8,128)}, u32[]{:S(2)}) copy-start(f32[8,512]{1,0:T(8,128)} %param.8) | copy-start | bytes 49156
  0.6 10.2 %copy-start.2 = (bf16[2048,64]{0,1:T(8,128)(2,1)S(1)}, bf16[2048,64]{0,1:T(8,128)(2,1)}, u32[]{:S(2)}) copy-start(bf16[2048,64]{0,1:T(8,128)(2,1)} %param.13) | copy-start | bytes 786436
  0.7 5.2 %copy-start.1 = (f32[8,128]{1,0:T(8,128)S(1)}, f32[8,128]{1,0:T(8,128)}, u32[]{:S(2)}) copy-start(f32[8,128]{1,0:T(8,128)} %x_ref.1) | copy-start | bytes 12292
  2.8 4.9 %collective-permute-start = (f32[64,128]{1,0:T(8,128)S(1)}, f32[64,128]{1,0:T(8,128)S(1)}, u32[]{:S(2)}, u32[]{:S(2)}) collective-permute-start(f32[64,128]{1,0:T(8,128)S(1)} %shard_map.86.mine_ref), channel_id=1, source_target_pairs={{0,1},{1,0},{2,3},{3,2},{4,5},{5,4},{6,7},{7,6},{8,9},{9,8},{10,11... | collective-permute-start | bytes 98312 | tf_op jit(solution)/shard_map/ppermute | solution.py:333
  5.8 1.2 %collective-permute-start.1 = (f32[8,128]{1,0:T(8,128)S(1)}, f32[8,128]{1,0:T(8,128)S(1)}, u32[]{:S(2)}, u32[]{:S(2)}) collective-permute-start(f32[8,128]{1,0:T(8,128)S(1)} %copy-done.1), channel_id=1, source_target_pairs={{0,2},{2,0},{4,6},{6,4},{8,10},{10,8},{12,14},{14,12},{16,18},{18,... | collective-permute-start | bytes 12296 | tf_op jit(solution)/shard_map/ppermute | solution.py:316
  7.7 5.1 %collective-permute-start.2 = (f32[1,80,128]{2,1,0:T(8,128)S(1)}, f32[1,80,128]{2,1,0:T(8,128)S(1)}, u32[]{:S(2)}, u32[]{:S(2)}) collective-permute-start(f32[1,80,128]{2,1,0:T(8,128)S(1)} %bitcast.5), channel_id=1, source_target_pairs={{0,16},{2,18},{4,20},{6,22},{8,24},{10,26},{12,28},{14,30},{16,0},... | collective-permute-start | bytes 122888 | tf_op jit(solution)/shard_map/ppermute | solution.py:316
  10.8 10.9 %collective-permute-start.8 = (bf16[64,2048]{1,0:T(8,128)(2,1)S(1)}, bf16[64,2048]{1,0:T(8,128)(2,1)S(1)}, u32[]{:S(2)}, u32[]{:S(2)}) collective-permute-start(bf16[64,2048]{1,0:T(8,128)(2,1)S(1)} %bitcast.9), channel_id=1, source_target_pairs={{0,1},{1,0},{2,3},{3,2},{4,5},{5,4},{6,7},{7,6},{8,9},{9,8},{10,11... | collective-permute-start | bytes 786440 | tf_op jit(solution)/shard_map/ppermute | solution.py:337
  12.8 5.3 %collective-permute-start.3 = (f32[2,80,128]{2,1,0:T(8,128)S(1)}, f32[2,80,128]{2,1,0:T(8,128)S(1)}, u32[]{:S(2)}, u32[]{:S(2)}) collective-permute-start(f32[2,80,128]{2,1,0:T(8,128)S(1)} %pad_maximum_fusion.1), channel_id=1, source_target_pairs={{0,4},{2,6},{4,0},{6,2},{8,12},{10,14},{12,8},{14,10},{16,20},{18,... | collective-permute-start | bytes 245768 | tf_op jit(solution)/shard_map/ppermute | solution.py:316
  14.8 4.5 %collective-permute-start.4 = (f32[2,80,128]{2,1,0:T(8,128)S(1)}, f32[2,80,128]{2,1,0:T(8,128)S(1)}, u32[]{:S(2)}, u32[]{:S(2)}) collective-permute-start(f32[2,80,128]{2,1,0:T(8,128)S(1)} %pad_maximum_fusion.1), channel_id=1, source_target_pairs={{0,8},{2,10},{4,12},{6,14},{8,0},{10,2},{12,4},{14,6},{16,24},{18,... | collective-permute-start | bytes 245768 | tf_op jit(solution)/shard_map/ppermute | solution.py:316
  16.3 5.3 %collective-permute-start.5 = (f32[2,80,128]{2,1,0:T(8,128)S(1)}, f32[2,80,128]{2,1,0:T(8,128)S(1)}, u32[]{:S(2)}, u32[]{:S(2)}) collective-permute-start(f32[2,80,128]{2,1,0:T(8,128)S(1)} %pad_maximum_fusion.1), channel_id=1, source_target_pairs={{0,12},{2,14},{4,8},{6,10},{8,4},{10,6},{12,0},{14,2},{16,28},{18,... | collective-permute-start | bytes 245768 | tf_op jit(solution)/shard_map/ppermute | solution.py:316
  18.1 3.6 %copy-start.3 = (f32[8,4096]{1,0:T(8,128)S(1)}, f32[8,4096]{1,0:T(8,128)}, u32[]{:S(2)}) copy-start(f32[8,4096]{1,0:T(8,128)} %omega_ref.1) | copy-start | bytes 393220
  18.2 3.6 %copy-start.4 = (f32[4096]{0:T(1024)S(1)}, f32[4096]{0:T(1024)}, u32[]{:S(2)}) copy-start(f32[4096]{0:T(1024)} %param.12) | copy-start | bytes 49156
  19.2 3.2 %collective-permute-start.6 = (f32[4,64,128]{2,1,0:T(8,128)S(1)}, f32[4,64,128]{2,1,0:T(8,128)S(1)}, u32[]{:S(2)}, u32[]{:S(2)}) collective-permute-start(f32[4,64,128]{2,1,0:T(8,128)S(1)} %slice.8), channel_id=1, source_target_pairs={{0,2},{2,0},{4,6},{6,4},{8,10},{10,8},{12,14},{14,12},{16,18},{18,... | collective-permute-start | bytes 393224 | tf_op jit(solution)/shard_map/ppermute | solution.py:316
  21.7 2.9 %collective-permute-start.7 = (f32[4,64,128]{2,1,0:T(8,128)S(1)}, f32[4,64,128]{2,1,0:T(8,128)S(1)}, u32[]{:S(2)}, u32[]{:S(2)}) collective-permute-start(f32[4,64,128]{2,1,0:T(8,128)S(1)} %slice.9), channel_id=1, source_target_pairs={{0,2},{2,0},{4,6},{6,4},{8,10},{10,8},{12,14},{14,12},{16,18},{18,... | collective-permute-start | bytes 393224 | tf_op jit(solution)/shard_map/ppermute | solution.py:316

commit v6 on v5

--- a/solution.py
+++ b/solution.py
@@ -189,60 +189,105 @@
     field_ref[...] = product(rows_of(block_ref, samples).astype(bf16), kernel_ref[:half, :])
 
 
-def far_kernel(
+def side_kernel(
     block_ref, near_ref, left_ref, right_ref, cand_left_ref, before_ref,
-    near_far_ref, far_near_ref, far_far_ref, tile_ref, field_ref,
-    far_left_ref, far_right_ref,
+    side_left_ref, side_right_ref, near_side_ref, side_near_ref, side_ref, tile_ref, near_field_ref, field_ref,
+):
+    samples, size = field_ref.shape
+    points = points_of(block_ref, samples)
+    side_left_ref[...] = left_of(points)
+    side_right_ref[...] = right_of(points)
+    fill(near_side_ref, left_ref, side_right_ref, side_near_ref)
+    fill(side_ref, side_left_ref, side_right_ref, side_ref)
+    fill(tile_ref, cand_left_ref, side_right_ref)
+    near, side = rows_of(near_ref, samples).astype(bf16), rows_of(block_ref, samples).astype(bf16)
+    near_field_ref[...] = before_ref[...] + product(side, side_near_ref[: size // 2, :])
+    field_ref[...] = product(near, near_side_ref[: near.shape[1], :]) + product(side, side_ref[: size // 2, :])
+
+
+def last_kernel(
+    block_ref, near_ref, side_block_ref, left_ref, right_ref, cand_left_ref, side_left_ref, side_right_ref,
+    near_before_ref, side_before_ref, near_other_ref, near_near_ref,
+    near_last_ref, last_near_ref, side_last_ref, last_side_ref, last_ref, tile_ref, field_ref,
+    last_left_ref, last_right_ref,
 ):
     samples = field_ref.shape[0]
     points = points_of(block_ref, samples)
-    far_left_ref[...] = left_of(points)
-    far_right_ref[...] = right_of(points)
-    fill(near_far_ref, left_ref, far_right_ref, far_near_ref)
-    fill(far_far_ref, far_left_ref, far_right_ref, far_far_ref)
-    fill(tile_ref, cand_left_ref, far_right_ref)
-    half, count = points.shape[1] // 2, points.shape[1]
-    near, far = rows_of(near_ref, samples).astype(bf16), rows_of(block_ref, samples).astype(bf16)
-    field_ref[:, :count] = before_ref[...] + product(far, far_near_ref[:half, :])
-    field_ref[:, count:] = product(near, near_far_ref[:half, :]) + product(far, far_far_ref[:half, :])
-
-
-def near_join_kernel(other_ref, before_ref, kernel_ref, field_ref):
-    half = kernel_ref.shape[0] // 2
-    rows = rows_of(other_ref, other_ref.shape[1]).astype(bf16)
-    field_ref[...] = before_ref[...] + product(rows, kernel_ref[half:, :])
+    last_left_ref[...] = left_of(points)
+    last_right_ref[...] = right_of(points)
+    fill(near_last_ref, left_ref, last_right_ref, last_near_ref)
+    fill(side_last_ref, side_left_ref, last_right_ref, last_side_ref)
+    fill(last_ref, last_left_ref, last_right_ref, last_ref)
+    fill(tile_ref, cand_left_ref, last_right_ref)
+    count, size = near_before_ref.shape[1], points.shape[1]
+    half = size // 2
+    near, side, last = (
+        rows_of(ref, samples).astype(bf16) for ref in (near_ref, side_block_ref, block_ref)
+    )
+    other = rows_of(near_other_ref, samples).astype(bf16)
+    field_ref[:, :count] = (
+        near_before_ref[...] + product(last, last_near_ref[:half, :]) + product(other, near_near_ref[size:, :])
+    )
+    field_ref[:, count : count + size] = side_before_ref[...] + product(last, last_side_ref[:half, :])
+    field_ref[:, count + size :] = (
+        product(near, near_last_ref[: near.shape[1], :])
+        + product(side, side_last_ref[:half, :])
+        + product(last, last_ref[:half, :])
+    )
 
 
 def solve_kernel(
-    own_rows, which, near_ref, far_ref, near_other_ref, far_other_ref, before_ref,
-    near_near_ref, near_far_ref, far_near_ref, far_far_ref,
-    near_tile_ref, far_tile_ref, prior_ref, samples_ref, solution_ref,
+    own_rows, which, near_ref, side_block_ref, last_block_ref, near_other_ref, far_other_ref, before_ref,
+    near_near_ref, near_side_ref, side_near_ref, side_ref,
+    near_last_ref, last_near_ref, side_last_ref, last_side_ref, last_ref,
+    near_tile_ref, side_tile_ref, last_tile_ref, prior_ref, samples_ref, solution_ref,
     image_ref, start_ref, direction_ref, packed_ref,
 ):
     samples = prior_ref.shape[1]
-    blocks, _, width = near_ref.shape
-    half = blocks * width
-    count = 2 * half
-    tiles = [(j, slice(j, j + TILE), slice(j % count, j % count + TILE)) for j in range(0, 2 * count, TILE)]
-    for quarter, block_ref in enumerate((near_ref, near_other_ref, far_ref, far_other_ref)):
-        for k in range(blocks):
-            offset = quarter * half + k * width
-            start_ref[:, offset : offset + width] = block_ref[k, :samples, :]
-    near = start_ref[:, half:count].astype(bf16)
-    far = start_ref[:, count + half :].astype(bf16)
+    width = near_ref.shape[2]
+    count, size = near_side_ref.shape
+    half = size // 2
+    few = half // width
+    position = 0
+    for block_ref, first, blocks in (
+        (near_ref, 0, 2 * few), (near_other_ref, 0, 2 * few),
+        (side_block_ref, 0, few), (far_other_ref, few, few),
+        (last_block_ref, 0, few), (far_other_ref, 0, few),
+    ):
+        for k in range(first, first + blocks):
+            start_ref[:, position : position + width] = block_ref[k, :samples, :]
+            position += width
+    near = start_ref[:, size:count].astype(bf16)
+    side = start_ref[:, count + half : count + size].astype(bf16)
+    last = start_ref[:, count + size + half :].astype(bf16)
+    segments = (
+        (0, count, ((side, side_near_ref, half), (last, last_near_ref, half)), (), near_near_ref, near_tile_ref),
+        (
+            count, size,
+            ((near, near_side_ref, size), (side, side_ref, half), (last, last_side_ref, half)),
+            ((0, near_side_ref),), side_ref, side_tile_ref,
+        ),
+        (
+            count + size, size,
+            ((near, near_last_ref, size), (side, side_last_ref, half), (last, last_ref, half)),
+            ((0, near_last_ref), (count, side_last_ref)), last_ref, last_tile_ref,
+        ),
+    )
+    tiles = [
+        (slice(offset + j, offset + j + TILE), slice(j, j + TILE), offset, *segment)
+        for offset, extent, *segment in segments
+        for j in range(0, extent, TILE)
+    ]
 
     def total(values):
         return jnp.sum(values, axis=1, keepdims=True)
 
     zero = jnp.zeros((samples, TILE), f32)
     norm0, curve0, norm1, curve1 = zero, zero, zero, zero
-    for j, columns, inner in tiles:
+    for columns, inner, _, products, *_ in tiles:
         value = before_ref[:, columns]
-        if j < count:
-            value += product(far, far_near_ref[half:, inner])
-        else:
-            value += product(near, near_far_ref[half:, inner])
-            value += product(far, far_far_ref[half:, inner])
+        for rows, kernel_ref, first in products:
+            value += product(rows, kernel_ref[first:, inner])
         start = start_ref[:, columns]
         image = value + noise_level * start
         image_ref[:, columns] = image
@@ -250,33 +295,33 @@
         curve0 += start * image
     norm0 = total(norm0)
     alpha0 = norm0 / total(curve0)
-    for _, columns, _ in tiles:
+    for columns, *_ in tiles:
         residual = start_ref[:, columns] - alpha0 * image_ref[:, columns]
         direction_ref[:, columns] = residual
         norm1 += residual * residual
     norm1 = total(norm1)
     beta = norm1 / norm0
-    for _, columns, _ in tiles:
+    for columns, *_ in tiles:
         direction = direction_ref[:, columns] + beta * start_ref[:, columns]
         direction_ref[:, columns] = direction
         packed_ref[:, columns] = direction.astype(bf16)
 
-    for j, columns, inner in tiles:
-        diagonal, above = (near_near_ref, None) if j < count else (far_far_ref, near_far_ref)
+    for columns, inner, offset, _, above, diagonal, _ in tiles:
         value = product(packed_ref[:, columns], diagonal[inner, inner])
-        if above is not None:
-            value += 2.0 * product(packed_ref[:, :count], above[:, inner])
+        for first, kernel_ref in above:
+            rows = packed_ref[:, first : first + kernel_ref.shape[0]]
+            value += 2.0 * product(rows, kernel_ref[:, inner])
         if inner.start:
-            value += 2.0 * product(packed_ref[:, j - inner.start : j], diagonal[: inner.start, inner])
+            rows = packed_ref[:, offset : offset + inner.start]
+            value += 2.0 * product(rows, diagonal[: inner.start, inner])
         direction = direction_ref[:, columns]
         curve1 += direction * (value + noise_level * direction)
     alpha1 = norm1 / total(curve1)
     own = (alpha0 * start_ref[:, :width] + alpha1 * direction_ref[:, :width]).T
     solution_ref[...] = jnp.where(which[0] == 0, own[:own_rows], own[own_rows:])
     value = prior_ref[...]
-    for j, columns, inner in tiles:
+    for columns, inner, *_, tile_ref in tiles:
         weights = (alpha0 * start_ref[:, columns] + alpha1 * direction_ref[:, columns]).astype(bf16)
-        tile_ref = near_tile_ref if j < count else far_tile_ref
         value += product_transposed(tile_ref[:, inner], weights)
     samples_ref[...] = value
 
@@ -344,7 +389,6 @@
     third = exchange(first, 6)
     second = exchange(first, 4)
     near = jnp.concatenate([first, exchange(first, 2)], axis=0)
-    far = jnp.concatenate([second, third], axis=0)
     per_device = x_cand.shape[1] // blocks
     mine = lax.dynamic_slice_in_dim(x_cand, train_index * per_device, per_device, 1)
     prior_cand = call(cand_kernel, shape((per_device, samples), f32), scalars=1, inputs=5, flops=1 << 30)(
@@ -366,16 +410,28 @@
         inputs=2, flops=1 << 31,
     )(near, mine)
     near_other = exchange(near[:, :samples], 1)
-    before = call(near_join_kernel, shape((samples, count), f32), inputs=3, flops=1 << 30)(
-        near_other, before, near_near
-    )
-    far_other = exchange(far[:, :samples], 1)
-    near_far, far_near, far_far, far_tile, before = call(
-        far_kernel,
-        (square, square, square, shape((per_device, count), bf16), shape((samples, 2 * count), f32)),
-        scratch=[pltpu.VMEM((count, stack), bf16), pltpu.VMEM((stack, count), bf16)],
-        inputs=6, flops=1 << 33,
-    )(far, near, left, right, cand_left, before)
+    size = count // 2
+
+    def kernels(*shapes):
+        return tuple(shape(dims, bf16) for dims in shapes)
+
+    (side_left, side_right, near_side, side_near, side, side_tile, before, side_before) = call(
+        side_kernel,
+        kernels((size, stack), (stack, size), (count, size), (size, count), (size, size), (per_device, size))
+        + (shape((samples, count), f32), shape((samples, size), f32)),
+        inputs=6, flops=1 << 31,
+    )(third, near, left, right, cand_left, before)
+    far_other = exchange(jnp.concatenate([second[:, :samples], third[:, :samples]], axis=0), 1)
+    near_last, last_near, side_last, last_side, last, last_tile, before = call(
+        last_kernel,
+        kernels((count, size), (size, count), (size, size), (size, size), (size, size), (per_device, size))
+        + (shape((samples, 2 * count), f32),),
+        scratch=[pltpu.VMEM((size, stack), bf16), pltpu.VMEM((stack, size), bf16)],
+        inputs=12, flops=1 << 32,
+    )(
+        second, near, third, left, right, cand_left, side_left, side_right, before, side_before,
+        near_other, near_near,
+    )
     return tuple(
         call(
             functools.partial(solve_kernel, own_rows),
@@ -386,10 +442,12 @@
                 pltpu.VMEM((samples, 2 * count), f32),
                 pltpu.VMEM((samples, 2 * count), bf16),
             ],
-            scalars=1, inputs=12, flops=1 << 33,
+            scalars=1, inputs=19, flops=1 << 33,
         )(
-            which, near, far, near_other, far_other, before, near_near, near_far, far_near, far_far,
-            near_tile, far_tile, prior_cand,
+            which, near, third, second, near_other, far_other, before,
+            near_near, near_side, side_near, side,
+            near_last, last_near, side_last, last_side, last,
+            near_tile, side_tile, last_tile, prior_cand,
         )
     )
 
@@ -397,7 +455,7 @@
 def is_local(mesh, x_train):
     train, cand = mesh.shape["train"], mesh.shape["cand"]
     count = x_train.shape[1]
-    tiles = count // 2 % TILE == 0
+    tiles = count // 4 % TILE == 0
     return cand == 2 and train >= 8 and train & (train - 1) == 0 and tiles and 2 * count * count <= KERNEL_BYTES
 
 

time: 27.6 us -> 26.7 us (0.967)
  waiting for transfers between devices: 6.54 us -> 5.61 us
    ppermute x7, waiting for transfers between devices: 5.81 us -> 4.88 us  [exchange(): return lax.ppermute(values, 'train', [(i, i ^ bit) for i in range(blocks)])]
  transfers between devices with their start and end apart: 9 -> 9, of which waited for: 5 -> 6; matrix products, arithmetic and copies ran while one was open for 0% -> 0% of each run, Pallas kernels for 13% -> 14%
where the time goes in v6:
time: 26.7 us; the launch traced here: 26.5 us
  starting transfers between devices  11.3 us (42%)
  Pallas kernels  8.68 us (33%)
  waiting for transfers between devices  5.61 us (21%)
  between operations  0.75 us (3%)
    ppermute x7, starting transfers between devices, exchange(): return lax.ppermute(values, 'train', [(i, i ^ bit) for i in range(blocks)])  6.76 us
    ppermute x7, waiting for transfers between devices, exchange(): return lax.ppermute(values, 'train', [(i, i ^ bit) for i in range(blocks)])  4.88 us
    ppermute x1, starting transfers between devices, local_body(): other = lax.ppermute(partial, 'cand', swap)  3.04 us
    pallas_call x1, Pallas kernels, local_body(): call(functools.partial(solve_kernel, own_rows), (shape((per_device, sampl...  2.92 us
    pallas_call x1, Pallas kernels, local_body(): call(prior_kernel, shape((samples, width), f32), scalars=1, inputs=6, hbm...  2.09 us
    ppermute x1, starting transfers between devices, local_body(): other_weights = lax.ppermute(weights, 'cand', swap)  1.49 us
    pallas_call x1, Pallas kernels, local_body(): call(last_kernel, kernels((count, size), (size, count), (size, size), (si...  1.29 us
    pallas_call x1, Pallas kernels, local_body(): call(near_kernel, (shape((count, stack), bf16), shape((stack, count), bf1...  0.97 us
  transfers between devices with their start and end apart: 9, of which 6 were waited for; matrix products, arithmetic and copies ran while one was open for 0% of the time, Pallas kernels for 14%

profile of v6, /device:TPU:0, one launch (start us, length us, event | category | flops | bytes accessed | tf_op | source)
XLA Modules:
  0.0 26.5 jit_solution(4682251477912121683)
XLA Ops:
  0.6 0.0 copy-start
  0.6 0.0 copy-start.2
  0.7 0.0 copy-start.1
  0.7 2.1 %shard_map.86.mine_ref = f32[64,128]{1,0:T(8,128)S(1)} custom-call(s32[1]{0:T(128)} %bitcast.which, f32[8,128]{1,0:T(8,128)} %x_ref.1, f32[8,4096]{1,0:T(8,128)} %omega_ref.1, f32[1,4096]{1,0:T(1,128)} %bitcast.11, bf16[64,2048]{1,0:T(8,128)(2,1)} %bitcast.8, f32[1,64]{1,0:T(1,128)} %bitcast.13, f32[64,64]{1,0:T(8,128)} %noise_hbm.1), custom_call_target="tpu_custom_call" | custom-call | flops 1073741824 | bytes 1048576 | tf_op jit(solution)/shard_map/pallas_call | solution.py:364
  2.8 3.0 %collective-permute-start = (f32[64,128]{1,0:T(8,128)S(1)}, f32[64,128]{1,0:T(8,128)S(1)}, u32[]{:S(2)}, u32[]{:S(2)}) collective-permute-start(f32[64,128]{1,0:T(8,128)S(1)} %shard_map.86.mine_ref), channel_id=1, source_target_pairs={{0,1},{1,0},{2,3},{3,2},{4,5},{5,4},{6,7},{7,6},{8,9},{9,8},{10,11... | collective-permute-start | bytes 98312 | tf_op jit(solution)/shard_map/ppermute | solution.py:378
  5.8 0.0 collective-permute-start.1
  5.8 1.2 %collective-permute-done.1.pair_ref = f32[8,128]{1,0:T(8,128)S(1)} collective-permute-done((f32[8,128]{1,0:T(8,128)S(1)}, f32[8,128]{1,0:T(8,128)S(1)}, u32[]{:S(2)}, u32[]{:S(2)}) %collective-permute-start.1) | collective-permute-done | bytes 4128 | tf_op jit(solution)/shard_map/ppermute | solution.py:361
  7.0 0.7 %collective-permute-done.other_ref = f32[64,128]{1,0:T(8,128)S(1)} collective-permute-done((f32[64,128]{1,0:T(8,128)S(1)}, f32[64,128]{1,0:T(8,128)S(1)}, u32[]{:S(2)}, u32[]{:S(2)}) %collective-permute-start) | collective-permute-done | bytes 32800 | tf_op jit(solution)/shard_map/ppermute | solution.py:378
  7.7 3.1 %collective-permute-start.2 = (f32[1,80,128]{2,1,0:T(8,128)S(1)}, f32[1,80,128]{2,1,0:T(8,128)S(1)}, u32[]{:S(2)}, u32[]{:S(2)}) collective-permute-start(f32[1,80,128]{2,1,0:T(8,128)S(1)} %bitcast.5), channel_id=1, source_target_pairs={{0,16},{2,18},{4,20},{6,22},{8,24},{10,26},{12,28},{14,30},{16,0},... | collective-permute-start | bytes 122888 | tf_op jit(solution)/shard_map/ppermute | solution.py:361
  10.8 1.5 %collective-permute-start.8 = (bf16[64,2048]{1,0:T(8,128)(2,1)S(1)}, bf16[64,2048]{1,0:T(8,128)(2,1)S(1)}, u32[]{:S(2)}, u32[]{:S(2)}) collective-permute-start(bf16[64,2048]{1,0:T(8,128)(2,1)S(1)} %bitcast.9), channel_id=1, source_target_pairs={{0,1},{1,0},{2,3},{3,2},{4,5},{5,4},{6,7},{7,6},{8,9},{9,8},{10,11... | collective-permute-start | bytes 786440 | tf_op jit(solution)/shard_map/ppermute | solution.py:382
  12.3 0.5 %collective-permute-done.2 = f32[1,80,128]{2,1,0:T(8,128)S(1)} collective-permute-done((f32[1,80,128]{2,1,0:T(8,128)S(1)}, f32[1,80,128]{2,1,0:T(8,128)S(1)}, u32[]{:S(2)}, u32[]{:S(2)}) %collective-permute-start.2) | collective-permute-done | bytes 40992 | tf_op jit(solution)/shard_map/ppermute | solution.py:361
  12.8 1.9 %collective-permute-start.3 = (f32[2,80,128]{2,1,0:T(8,128)S(1)}, f32[2,80,128]{2,1,0:T(8,128)S(1)}, u32[]{:S(2)}, u32[]{:S(2)}) collective-permute-start(f32[2,80,128]{2,1,0:T(8,128)S(1)} %pad_maximum_fusion.2), channel_id=1, source_target_pairs={{0,4},{2,6},{4,0},{6,2},{8,12},{10,14},{12,8},{14,10},{16,20},{18,... | collective-permute-start | bytes 245768 | tf_op jit(solution)/shard_map/ppermute | solution.py:361
  14.7 0.1 constant_dynamic-slice_fusion.cand_ref.x_ref
  14.8 1.5 %collective-permute-start.4 = (f32[2,80,128]{2,1,0:T(8,128)S(1)}, f32[2,80,128]{2,1,0:T(8,128)S(1)}, u32[]{:S(2)}, u32[]{:S(2)}) collective-permute-start(f32[2,80,128]{2,1,0:T(8,128)S(1)} %pad_maximum_fusion.2), channel_id=1, source_target_pairs={{0,12},{2,14},{4,8},{6,10},{8,4},{10,6},{12,0},{14,2},{16,28},{18,... | collective-permute-start | bytes 245768 | tf_op jit(solution)/shard_map/ppermute | solution.py:361
  16.3 0.1 collective-permute-start.5
  16.4 1.2 %collective-permute-done.3 = f32[2,80,128]{2,1,0:T(8,128)S(1)} collective-permute-done((f32[2,80,128]{2,1,0:T(8,128)S(1)}, f32[2,80,128]{2,1,0:T(8,128)S(1)}, u32[]{:S(2)}, u32[]{:S(2)}) %collective-permute-start.3) | collective-permute-done | bytes 81952 | tf_op jit(solution)/shard_map/ppermute | solution.py:361
  17.6 1.0 %shard_map.88 = (bf16[1024,64]{1,0:T(8,128)(2,1)S(1)}, bf16[64,1024]{1,0:T(8,128)(2,1)S(1)}, bf16[32,64]{1,0:T(8,128)(2,1)S(1)}, bf16[1024,1024]{1,0:T(8,128)(2,...) custom-call(f32[4,80,128]{2,1,0:T(8,128)S(1)} %pad_maximum_fusion.block_ref.near_ref, ...), custom_call_target="tpu_custom_call" | custom-call | flops 2147483648 | bytes 1048576 | tf_op jit(solution)/shard_map/pallas_call | solution.py:400
  18.6 0.1 collective-permute-start.6
  18.6 1.5 %collective-permute-done.4.block_ref.side_block_ref = f32[2,80,128]{2,1,0:T(8,128)S(1)} collective-permute-done((f32[2,80,128]{2,1,0:T(8,128)S(1)}, f32[2,80,128]{2,1,0:T(8,128)S(1)}, u32[]{:S(2)}, u32[]{:S(2)}) %collective-permute-start.4) | collective-permute-done | bytes 81952 | tf_op jit(solution)/shard_map/ppermute | solution.py:361
  20.1 0.6 %collective-permute-done.5.block_ref.last_block_ref = f32[2,80,128]{2,1,0:T(8,128)S(1)} collective-permute-done((f32[2,80,128]{2,1,0:T(8,128)S(1)}, f32[2,80,128]{2,1,0:T(8,128)S(1)}, u32[]{:S(2)}, u32[]{:S(2)}) %collective-permute-start.5) | collective-permute-done | bytes 81952 | tf_op jit(solution)/shard_map/ppermute | solution.py:361
  20.7 0.1 collective-permute-start.7
  20.8 0.0 copy-start.3
  20.8 0.0 copy-start.4
  20.8 0.8 %shard_map.89 = (bf16[512,64]{1,0:T(8,128)(2,1)S(1)}, bf16[64,512]{1,0:T(8,128)(2,1)S(1)}, bf16[1024,512]{1,0:T(8,128)(2,1)S(1)}, bf16[512,1024]{1,0:T(8,128)(2,...) custom-call(f32[2,80,128]{2,1,0:T(8,128)S(1)} %collective-permute-do, ...), custom_call_target="tpu_custom_call" | custom-call | flops 2147483648 | bytes 1048576 | tf_op jit(solution)/shard_map/pallas_call | solution.py:418
  21.6 0.0 collective-permute-done.8.other_ref
  21.7 0.1 copy-done.3
  21.7 0.0 copy-done.4
  21.7 0.6 %shard_map.91.prior_ref = f32[32,64]{1,0:T(8,128)S(1)} custom-call(s32[1]{0:T(128)} %bitcast.which, f32[8,32]{1,0:T(8,128)S(1)} %constant_dynamic-slice_fusion.cand_ref.x_ref, f32[8,4096]{1,0:T(8,128)S(1)} %copy-done.3, f32[1,4096]{1,0:T(1,128)S(1)} %bitcast.12, bf16[64,2048]{1,0:T(8,128)(2,1)S(1)} %bitcast.10, ...), custom_call_target="tpu_custom_call" | custom-call | flops 1073741824 | bytes 1048576 | tf_op jit(solution)/shard_map/pallas_call | solution.py:394
  22.3 0.0 collective-permute-done.6.near_other_ref
  22.3 1.3 %shard_map.90 = (bf16[1024,512]{1,0:T(8,128)(2,1)S(1)}, bf16[512,1024]{1,0:T(8,128)(2,1)S(1)}, bf16[512,512]{1,0:T(8,128)(2,1)S(1)}, bf16[512,512]{1,0:T(8,128)(...) custom-call(f32[2,80,128]{2,1,0:T(8,128)S(1)} %collective-permute-done.5.block_ref.last_, ...), custom_call_target="tpu_custom_call" | custom-call | flops 4294967296 | bytes 1048576 | tf_op jit(solution)/shard_map/pallas_call | solution.py:425
  23.6 0.0 collective-permute-done.7.far_other_ref
  23.6 2.9 %shard_map.92 = (f32[32,64]{1,0:T(8,128)}, f32[64,64]{1,0:T(8,128)}) custom-call(s32[1]{0:T(128)} %bitcast.which, f32[4,80,128]{2,1,0:T(8,128)S(1)} %pad_maximum_fusion.block_ref.near_ref, f32[2,80,128]{2,1,0:T(8,128)S(1)} %collective-permute-done.4.block_ref.side_block_ref, f32[2,80,128]{2,1,0:T(8,128)S(1)} %collective-permute-done.5.block_ref.last_block_ref, ...), custom_call_target="tpu_custom_call" | custom-call | flops 8589934592 | bytes 1048576 | tf_op jit(solution)/shard_map/pallas_call | solution.py:436
  (10 shorter events, 0.1 us)
Async XLA Ops:
  0.6 14.0 %copy-start = (f32[8,512]{1,0:T(8,128)S(1)}, f32[8,512]{1,0:T(8,128)}, u32[]{:S(2)}) copy-start(f32[8,512]{1,0:T(8,128)} %param.8) | copy-start | bytes 49156
  0.6 10.2 %copy-start.2 = (bf16[2048,64]{0,1:T(8,128)(2,1)S(1)}, bf16[2048,64]{0,1:T(8,128)(2,1)}, u32[]{:S(2)}) copy-start(bf16[2048,64]{0,1:T(8,128)(2,1)} %param.13) | copy-start | bytes 786436
  0.7 5.2 %copy-start.1 = (f32[8,128]{1,0:T(8,128)S(1)}, f32[8,128]{1,0:T(8,128)}, u32[]{:S(2)}) copy-start(f32[8,128]{1,0:T(8,128)} %x_ref.1) | copy-start | bytes 12292
  2.8 4.9 %collective-permute-start = (f32[64,128]{1,0:T(8,128)S(1)}, f32[64,128]{1,0:T(8,128)S(1)}, u32[]{:S(2)}, u32[]{:S(2)}) collective-permute-start(f32[64,128]{1,0:T(8,128)S(1)} %shard_map.86.mine_ref), channel_id=1, source_target_pairs={{0,1},{1,0},{2,3},{3,2},{4,5},{5,4},{6,7},{7,6},{8,9},{9,8},{10,11... | collective-permute-start | bytes 98312 | tf_op jit(solution)/shard_map/ppermute | solution.py:378
  5.8 1.2 %collective-permute-start.1 = (f32[8,128]{1,0:T(8,128)S(1)}, f32[8,128]{1,0:T(8,128)S(1)}, u32[]{:S(2)}, u32[]{:S(2)}) collective-permute-start(f32[8,128]{1,0:T(8,128)S(1)} %copy-done.1), channel_id=1, source_target_pairs={{0,2},{2,0},{4,6},{6,4},{8,10},{10,8},{12,14},{14,12},{16,18},{18,... | collective-permute-start | bytes 12296 | tf_op jit(solution)/shard_map/ppermute | solution.py:361
  7.7 5.1 %collective-permute-start.2 = (f32[1,80,128]{2,1,0:T(8,128)S(1)}, f32[1,80,128]{2,1,0:T(8,128)S(1)}, u32[]{:S(2)}, u32[]{:S(2)}) collective-permute-start(f32[1,80,128]{2,1,0:T(8,128)S(1)} %bitcast.5), channel_id=1, source_target_pairs={{0,16},{2,18},{4,20},{6,22},{8,24},{10,26},{12,28},{14,30},{16,0},... | collective-permute-start | bytes 122888 | tf_op jit(solution)/shard_map/ppermute | solution.py:361
  10.8 10.8 %collective-permute-start.8 = (bf16[64,2048]{1,0:T(8,128)(2,1)S(1)}, bf16[64,2048]{1,0:T(8,128)(2,1)S(1)}, u32[]{:S(2)}, u32[]{:S(2)}) collective-permute-start(bf16[64,2048]{1,0:T(8,128)(2,1)S(1)} %bitcast.9), channel_id=1, source_target_pairs={{0,1},{1,0},{2,3},{3,2},{4,5},{5,4},{6,7},{7,6},{8,9},{9,8},{10,11... | collective-permute-start | bytes 786440 | tf_op jit(solution)/shard_map/ppermute | solution.py:382
  12.8 4.7 %collective-permute-start.3 = (f32[2,80,128]{2,1,0:T(8,128)S(1)}, f32[2,80,128]{2,1,0:T(8,128)S(1)}, u32[]{:S(2)}, u32[]{:S(2)}) collective-permute-start(f32[2,80,128]{2,1,0:T(8,128)S(1)} %pad_maximum_fusion.2), channel_id=1, source_target_pairs={{0,4},{2,6},{4,0},{6,2},{8,12},{10,14},{12,8},{14,10},{16,20},{18,... | collective-permute-start | bytes 245768 | tf_op jit(solution)/shard_map/ppermute | solution.py:361
  14.8 5.3 %collective-permute-start.4 = (f32[2,80,128]{2,1,0:T(8,128)S(1)}, f32[2,80,128]{2,1,0:T(8,128)S(1)}, u32[]{:S(2)}, u32[]{:S(2)}) collective-permute-start(f32[2,80,128]{2,1,0:T(8,128)S(1)} %pad_maximum_fusion.2), channel_id=1, source_target_pairs={{0,12},{2,14},{4,8},{6,10},{8,4},{10,6},{12,0},{14,2},{16,28},{18,... | collective-permute-start | bytes 245768 | tf_op jit(solution)/shard_map/ppermute | solution.py:361
  16.3 4.4 %collective-permute-start.5 = (f32[2,80,128]{2,1,0:T(8,128)S(1)}, f32[2,80,128]{2,1,0:T(8,128)S(1)}, u32[]{:S(2)}, u32[]{:S(2)}) collective-permute-start(f32[2,80,128]{2,1,0:T(8,128)S(1)} %pad_maximum_fusion.2), channel_id=1, source_target_pairs={{0,8},{2,10},{4,12},{6,14},{8,0},{10,2},{12,4},{14,6},{16,24},{18,... | collective-permute-start | bytes 245768 | tf_op jit(solution)/shard_map/ppermute | solution.py:361
  18.6 3.8 %collective-permute-start.6 = (f32[4,64,128]{2,1,0:T(8,128)S(1)}, f32[4,64,128]{2,1,0:T(8,128)S(1)}, u32[]{:S(2)}, u32[]{:S(2)}) collective-permute-start(f32[4,64,128]{2,1,0:T(8,128)S(1)} %slice.12), channel_id=1, source_target_pairs={{0,2},{2,0},{4,6},{6,4},{8,10},{10,8},{12,14},{14,12},{16,18},{18,... | collective-permute-start | bytes 393224 | tf_op jit(solution)/shard_map/ppermute | solution.py:361
  20.7 2.9 %collective-permute-start.7 = (f32[4,64,128]{2,1,0:T(8,128)S(1)}, f32[4,64,128]{2,1,0:T(8,128)S(1)}, u32[]{:S(2)}, u32[]{:S(2)}) collective-permute-start(f32[4,64,128]{2,1,0:T(8,128)S(1)} %pad_maximum_fusion.1), channel_id=1, source_target_pairs={{0,2},{2,0},{4,6},{6,4},{8,10},{10,8},{12,14},{14,12},{16,18},{18,... | collective-permute-start | bytes 393224 | tf_op jit(solution)/shard_map/ppermute | solution.py:361
  20.8 0.9 %copy-start.3 = (f32[8,4096]{1,0:T(8,128)S(1)}, f32[8,4096]{1,0:T(8,128)}, u32[]{:S(2)}) copy-start(f32[8,4096]{1,0:T(8,128)} %omega_ref.1) | copy-start | bytes 393220
  20.8 0.9 %copy-start.4 = (f32[4096]{0:T(1024)S(1)}, f32[4096]{0:T(1024)}, u32[]{:S(2)}) copy-start(f32[4096]{0:T(1024)} %param.12) | copy-start | bytes 49156

commit v7 on v6

--- a/solution.py
+++ b/solution.py
@@ -190,8 +190,8 @@
 
 
 def side_kernel(
-    block_ref, near_ref, left_ref, right_ref, cand_left_ref, before_ref,
-    side_left_ref, side_right_ref, near_side_ref, side_near_ref, side_ref, tile_ref, near_field_ref, field_ref,
+    block_ref, near_ref, left_ref, right_ref, cand_left_ref,
+    side_left_ref, side_right_ref, near_side_ref, side_near_ref, side_ref, tile_ref, field_ref,
 ):
     samples, size = field_ref.shape
     points = points_of(block_ref, samples)
@@ -201,13 +201,12 @@
     fill(side_ref, side_left_ref, side_right_ref, side_ref)
     fill(tile_ref, cand_left_ref, side_right_ref)
     near, side = rows_of(near_ref, samples).astype(bf16), rows_of(block_ref, samples).astype(bf16)
-    near_field_ref[...] = before_ref[...] + product(side, side_near_ref[: size // 2, :])
     field_ref[...] = product(near, near_side_ref[: near.shape[1], :]) + product(side, side_ref[: size // 2, :])
 
 
 def last_kernel(
     block_ref, near_ref, side_block_ref, left_ref, right_ref, cand_left_ref, side_left_ref, side_right_ref,
-    near_before_ref, side_before_ref, near_other_ref, near_near_ref,
+    near_before_ref, side_before_ref, near_other_ref, near_near_ref, side_near_ref,
     near_last_ref, last_near_ref, side_last_ref, last_side_ref, last_ref, tile_ref, field_ref,
     last_left_ref, last_right_ref,
 ):
@@ -226,7 +225,10 @@
     )
     other = rows_of(near_other_ref, samples).astype(bf16)
     field_ref[:, :count] = (
-        near_before_ref[...] + product(last, last_near_ref[:half, :]) + product(other, near_near_ref[size:, :])
+        near_before_ref[...]
+        + product(side, side_near_ref[:half, :])
+        + product(last, last_near_ref[:half, :])
+        + product(other, near_near_ref[size:, :])
     )
     field_ref[:, count : count + size] = side_before_ref[...] + product(last, last_side_ref[:half, :])
     field_ref[:, count + size :] = (
@@ -415,22 +417,22 @@
     def kernels(*shapes):
         return tuple(shape(dims, bf16) for dims in shapes)
 
-    (side_left, side_right, near_side, side_near, side, side_tile, before, side_before) = call(
+    (side_left, side_right, near_side, side_near, side, side_tile, side_before) = call(
         side_kernel,
         kernels((size, stack), (stack, size), (count, size), (size, count), (size, size), (per_device, size))
-        + (shape((samples, count), f32), shape((samples, size), f32)),
-        inputs=6, flops=1 << 31,
-    )(third, near, left, right, cand_left, before)
+        + (shape((samples, size), f32),),
+        inputs=5, flops=1 << 31,
+    )(third, near, left, right, cand_left)
     far_other = exchange(jnp.concatenate([second[:, :samples], third[:, :samples]], axis=0), 1)
     near_last, last_near, side_last, last_side, last, last_tile, before = call(
         last_kernel,
         kernels((count, size), (size, count), (size, size), (size, size), (size, size), (per_device, size))
         + (shape((samples, 2 * count), f32),),
         scratch=[pltpu.VMEM((size, stack), bf16), pltpu.VMEM((stack, size), bf16)],
-        inputs=12, flops=1 << 32,
+        inputs=13, flops=1 << 32,
     )(
         second, near, third, left, right, cand_left, side_left, side_right, before, side_before,
-        near_other, near_near,
+        near_other, near_near, side_near,
     )
     return tuple(
         call(

time: 26.7 us -> 26.8 us (level)
  no operation moved by 1% of the time
where the time goes in v7:
time: 26.8 us; the launch traced here: 26.7 us
  starting transfers between devices  11.3 us (42%)
  Pallas kernels  8.79 us (33%)
  waiting for transfers between devices  5.61 us (21%)
  between operations  0.75 us (3%)
    ppermute x7, starting transfers between devices, exchange(): return lax.ppermute(values, 'train', [(i, i ^ bit) for i in range(blocks)])  6.76 us
    ppermute x7, waiting for transfers between devices, exchange(): return lax.ppermute(values, 'train', [(i, i ^ bit) for i in range(blocks)])  4.88 us
    ppermute x1, starting transfers between devices, local_body(): other = lax.ppermute(partial, 'cand', swap)  3.04 us
    pallas_call x1, Pallas kernels, local_body(): call(functools.partial(solve_kernel, own_rows), (shape((per_device, sampl...  2.94 us
    pallas_call x1, Pallas kernels, local_body(): call(prior_kernel, shape((samples, width), f32), scalars=1, inputs=6, hbm...  2.09 us
    ppermute x1, starting transfers between devices, local_body(): other_weights = lax.ppermute(weights, 'cand', swap)  1.49 us
    pallas_call x1, Pallas kernels, local_body(): call(last_kernel, kernels((count, size), (size, count), (size, size), (si...  1.4 us
    pallas_call x1, Pallas kernels, local_body(): call(near_kernel, (shape((count, stack), bf16), shape((stack, count), bf1...  0.97 us
  transfers between devices with their start and end apart: 9, of which 6 were waited for; matrix products, arithmetic and copies ran while one was open for 0% of the time, Pallas kernels for 14%

profile of v7, /device:TPU:0, one launch (start us, length us, event | category | flops | bytes accessed | tf_op | source)
XLA Modules:
  0.0 26.7 jit_solution(1672902752634740060)
XLA Ops:
  0.6 0.0 copy-start
  0.6 0.0 copy-start.2
  0.7 0.0 copy-start.1
  0.7 2.1 %shard_map.86.mine_ref = f32[64,128]{1,0:T(8,128)S(1)} custom-call(s32[1]{0:T(128)} %bitcast.which, f32[8,128]{1,0:T(8,128)} %x_ref.1, f32[8,4096]{1,0:T(8,128)} %omega_ref.1, f32[1,4096]{1,0:T(1,128)} %bitcast.11, bf16[64,2048]{1,0:T(8,128)(2,1)} %bitcast.8, f32[1,64]{1,0:T(1,128)} %bitcast.13, f32[64,64]{1,0:T(8,128)} %noise_hbm.1), custom_call_target="tpu_custom_call" | custom-call | flops 1073741824 | bytes 1048576 | tf_op jit(solution)/shard_map/pallas_call | solution.py:366
  2.8 3.0 %collective-permute-start = (f32[64,128]{1,0:T(8,128)S(1)}, f32[64,128]{1,0:T(8,128)S(1)}, u32[]{:S(2)}, u32[]{:S(2)}) collective-permute-start(f32[64,128]{1,0:T(8,128)S(1)} %shard_map.86.mine_ref), channel_id=1, source_target_pairs={{0,1},{1,0},{2,3},{3,2},{4,5},{5,4},{6,7},{7,6},{8,9},{9,8},{10,11... | collective-permute-start | bytes 98312 | tf_op jit(solution)/shard_map/ppermute | solution.py:380
  5.8 0.0 collective-permute-start.1
  5.8 1.2 %collective-permute-done.1.pair_ref = f32[8,128]{1,0:T(8,128)S(1)} collective-permute-done((f32[8,128]{1,0:T(8,128)S(1)}, f32[8,128]{1,0:T(8,128)S(1)}, u32[]{:S(2)}, u32[]{:S(2)}) %collective-permute-start.1) | collective-permute-done | bytes 4128 | tf_op jit(solution)/shard_map/ppermute | solution.py:363
  7.0 0.7 %collective-permute-done.other_ref = f32[64,128]{1,0:T(8,128)S(1)} collective-permute-done((f32[64,128]{1,0:T(8,128)S(1)}, f32[64,128]{1,0:T(8,128)S(1)}, u32[]{:S(2)}, u32[]{:S(2)}) %collective-permute-start) | collective-permute-done | bytes 32800 | tf_op jit(solution)/shard_map/ppermute | solution.py:380
  7.7 3.1 %collective-permute-start.2 = (f32[1,80,128]{2,1,0:T(8,128)S(1)}, f32[1,80,128]{2,1,0:T(8,128)S(1)}, u32[]{:S(2)}, u32[]{:S(2)}) collective-permute-start(f32[1,80,128]{2,1,0:T(8,128)S(1)} %bitcast.5), channel_id=1, source_target_pairs={{0,16},{2,18},{4,20},{6,22},{8,24},{10,26},{12,28},{14,30},{16,0},... | collective-permute-start | bytes 122888 | tf_op jit(solution)/shard_map/ppermute | solution.py:363
  10.8 1.5 %collective-permute-start.8 = (bf16[64,2048]{1,0:T(8,128)(2,1)S(1)}, bf16[64,2048]{1,0:T(8,128)(2,1)S(1)}, u32[]{:S(2)}, u32[]{:S(2)}) collective-permute-start(bf16[64,2048]{1,0:T(8,128)(2,1)S(1)} %bitcast.9), channel_id=1, source_target_pairs={{0,1},{1,0},{2,3},{3,2},{4,5},{5,4},{6,7},{7,6},{8,9},{9,8},{10,11... | collective-permute-start | bytes 786440 | tf_op jit(solution)/shard_map/ppermute | solution.py:384
  12.3 0.5 %collective-permute-done.2 = f32[1,80,128]{2,1,0:T(8,128)S(1)} collective-permute-done((f32[1,80,128]{2,1,0:T(8,128)S(1)}, f32[1,80,128]{2,1,0:T(8,128)S(1)}, u32[]{:S(2)}, u32[]{:S(2)}) %collective-permute-start.2) | collective-permute-done | bytes 40992 | tf_op jit(solution)/shard_map/ppermute | solution.py:363
  12.8 1.9 %collective-permute-start.3 = (f32[2,80,128]{2,1,0:T(8,128)S(1)}, f32[2,80,128]{2,1,0:T(8,128)S(1)}, u32[]{:S(2)}, u32[]{:S(2)}) collective-permute-start(f32[2,80,128]{2,1,0:T(8,128)S(1)} %pad_maximum_fusion.2), channel_id=1, source_target_pairs={{0,4},{2,6},{4,0},{6,2},{8,12},{10,14},{12,8},{14,10},{16,20},{18,... | collective-permute-start | bytes 245768 | tf_op jit(solution)/shard_map/ppermute | solution.py:363
  14.7 0.1 constant_dynamic-slice_fusion.cand_ref.x_ref
  14.8 1.5 %collective-permute-start.4 = (f32[2,80,128]{2,1,0:T(8,128)S(1)}, f32[2,80,128]{2,1,0:T(8,128)S(1)}, u32[]{:S(2)}, u32[]{:S(2)}) collective-permute-start(f32[2,80,128]{2,1,0:T(8,128)S(1)} %pad_maximum_fusion.2), channel_id=1, source_target_pairs={{0,12},{2,14},{4,8},{6,10},{8,4},{10,6},{12,0},{14,2},{16,28},{18,... | collective-permute-start | bytes 245768 | tf_op jit(solution)/shard_map/ppermute | solution.py:363
  16.3 0.1 collective-permute-start.5
  16.4 1.2 %collective-permute-done.3 = f32[2,80,128]{2,1,0:T(8,128)S(1)} collective-permute-done((f32[2,80,128]{2,1,0:T(8,128)S(1)}, f32[2,80,128]{2,1,0:T(8,128)S(1)}, u32[]{:S(2)}, u32[]{:S(2)}) %collective-permute-start.3) | collective-permute-done | bytes 81952 | tf_op jit(solution)/shard_map/ppermute | solution.py:363
  17.6 1.0 %shard_map.88 = (bf16[1024,64]{1,0:T(8,128)(2,1)S(1)}, bf16[64,1024]{1,0:T(8,128)(2,1)S(1)}, bf16[32,64]{1,0:T(8,128)(2,1)S(1)}, bf16[1024,1024]{1,0:T(8,128)(2,...) custom-call(f32[4,80,128]{2,1,0:T(8,128)S(1)} %pad_maximum_fusion.block_ref.near_ref, ...), custom_call_target="tpu_custom_call" | custom-call | flops 2147483648 | bytes 1048576 | tf_op jit(solution)/shard_map/pallas_call | solution.py:402
  18.6 0.1 collective-permute-start.6
  18.6 1.5 %collective-permute-done.4.block_ref.side_block_ref = f32[2,80,128]{2,1,0:T(8,128)S(1)} collective-permute-done((f32[2,80,128]{2,1,0:T(8,128)S(1)}, f32[2,80,128]{2,1,0:T(8,128)S(1)}, u32[]{:S(2)}, u32[]{:S(2)}) %collective-permute-start.4) | collective-permute-done | bytes 81952 | tf_op jit(solution)/shard_map/ppermute | solution.py:363
  20.1 0.6 %collective-permute-done.5.block_ref.last_block_ref = f32[2,80,128]{2,1,0:T(8,128)S(1)} collective-permute-done((f32[2,80,128]{2,1,0:T(8,128)S(1)}, f32[2,80,128]{2,1,0:T(8,128)S(1)}, u32[]{:S(2)}, u32[]{:S(2)}) %collective-permute-start.5) | collective-permute-done | bytes 81952 | tf_op jit(solution)/shard_map/ppermute | solution.py:363
  20.7 0.1 collective-permute-start.7
  20.8 0.0 copy-start.3
  20.8 0.0 copy-start.4
  20.8 0.8 %shard_map.89 = (bf16[512,64]{1,0:T(8,128)(2,1)S(1)}, bf16[64,512]{1,0:T(8,128)(2,1)S(1)}, bf16[1024,512]{1,0:T(8,128)(2,1)S(1)}, bf16[512,1024]{1,0:T(8,128)(2,...) custom-call(f32[2,80,128]{2,1,0:T(8,128)S(1)} %collective-permute-done.4.block_ref.side_blo, ...), custom_call_target="tpu_custom_call" | custom-call | flops 2147483648 | bytes 1048576 | tf_op jit(solution)/shard_map/pallas_call | solution.py:420
  21.6 0.0 collective-permute-done.8.other_ref
  21.6 0.1 copy-done.3
  21.7 0.0 copy-done.4
  21.7 0.6 %shard_map.91.prior_ref = f32[32,64]{1,0:T(8,128)S(1)} custom-call(s32[1]{0:T(128)} %bitcast.which, f32[8,32]{1,0:T(8,128)S(1)} %constant_dynamic-slice_fusion.cand_ref.x_ref, f32[8,4096]{1,0:T(8,128)S(1)} %copy-done.3, f32[1,4096]{1,0:T(1,128)S(1)} %bitcast.12, bf16[64,2048]{1,0:T(8,128)(2,1)S(1)} %bitcast.10, ...), custom_call_target="tpu_custom_call" | custom-call | flops 1073741824 | bytes 1048576 | tf_op jit(solution)/shard_map/pallas_call | solution.py:396
  22.3 0.0 collective-permute-done.6.near_other_ref
  22.3 1.4 %shard_map.90 = (bf16[1024,512]{1,0:T(8,128)(2,1)S(1)}, bf16[512,1024]{1,0:T(8,128)(2,1)S(1)}, bf16[512,512]{1,0:T(8,128)(2,1)S(1)}, bf16[512,512]{1,0:T(8,128)(...) custom-call(f32[2,80,128]{2,1,0:T(8,128)S(1)} %collective-permute-done.5.block_ref.last_, ...), custom_call_target="tpu_custom_call" | custom-call | flops 4294967296 | bytes 1048576 | tf_op jit(solution)/shard_map/pallas_call | solution.py:427
  23.7 0.0 collective-permute-done.7.far_other_ref
  23.7 2.9 %shard_map.92 = (f32[32,64]{1,0:T(8,128)}, f32[64,64]{1,0:T(8,128)}) custom-call(s32[1]{0:T(128)} %bitcast.which, f32[4,80,128]{2,1,0:T(8,128)S(1)} %pad_maximum_fusion.block_ref.near_ref, f32[2,80,128]{2,1,0:T(8,128)S(1)} %collective-permute-done.4.block_ref.side_block_ref, f32[2,80,128]{2,1,0:T(8,128)S(1)} %collective-permute-done.5.block_ref.last_block_ref, ...), custom_call_target="tpu_custom_call" | custom-call | flops 8589934592 | bytes 1048576 | tf_op jit(solution)/shard_map/pallas_call | solution.py:438
  (10 shorter events, 0.1 us)
Async XLA Ops:
  0.6 14.0 %copy-start = (f32[8,512]{1,0:T(8,128)S(1)}, f32[8,512]{1,0:T(8,128)}, u32[]{:S(2)}) copy-start(f32[8,512]{1,0:T(8,128)} %param.8) | copy-start | bytes 49156
  0.6 10.2 %copy-start.2 = (bf16[2048,64]{0,1:T(8,128)(2,1)S(1)}, bf16[2048,64]{0,1:T(8,128)(2,1)}, u32[]{:S(2)}) copy-start(bf16[2048,64]{0,1:T(8,128)(2,1)} %param.13) | copy-start | bytes 786436
  0.7 5.2 %copy-start.1 = (f32[8,128]{1,0:T(8,128)S(1)}, f32[8,128]{1,0:T(8,128)}, u32[]{:S(2)}) copy-start(f32[8,128]{1,0:T(8,128)} %x_ref.1) | copy-start | bytes 12292
  2.8 4.9 %collective-permute-start = (f32[64,128]{1,0:T(8,128)S(1)}, f32[64,128]{1,0:T(8,128)S(1)}, u32[]{:S(2)}, u32[]{:S(2)}) collective-permute-start(f32[64,128]{1,0:T(8,128)S(1)} %shard_map.86.mine_ref), channel_id=1, source_target_pairs={{0,1},{1,0},{2,3},{3,2},{4,5},{5,4},{6,7},{7,6},{8,9},{9,8},{10,11... | collective-permute-start | bytes 98312 | tf_op jit(solution)/shard_map/ppermute | solution.py:380
  5.8 1.2 %collective-permute-start.1 = (f32[8,128]{1,0:T(8,128)S(1)}, f32[8,128]{1,0:T(8,128)S(1)}, u32[]{:S(2)}, u32[]{:S(2)}) collective-permute-start(f32[8,128]{1,0:T(8,128)S(1)} %copy-done.1), channel_id=1, source_target_pairs={{0,2},{2,0},{4,6},{6,4},{8,10},{10,8},{12,14},{14,12},{16,18},{18,... | collective-permute-start | bytes 12296 | tf_op jit(solution)/shard_map/ppermute | solution.py:363
  7.7 5.1 %collective-permute-start.2 = (f32[1,80,128]{2,1,0:T(8,128)S(1)}, f32[1,80,128]{2,1,0:T(8,128)S(1)}, u32[]{:S(2)}, u32[]{:S(2)}) collective-permute-start(f32[1,80,128]{2,1,0:T(8,128)S(1)} %bitcast.5), channel_id=1, source_target_pairs={{0,16},{2,18},{4,20},{6,22},{8,24},{10,26},{12,28},{14,30},{16,0},... | collective-permute-start | bytes 122888 | tf_op jit(solution)/shard_map/ppermute | solution.py:363
  10.8 10.8 %collective-permute-start.8 = (bf16[64,2048]{1,0:T(8,128)(2,1)S(1)}, bf16[64,2048]{1,0:T(8,128)(2,1)S(1)}, u32[]{:S(2)}, u32[]{:S(2)}) collective-permute-start(bf16[64,2048]{1,0:T(8,128)(2,1)S(1)} %bitcast.9), channel_id=1, source_target_pairs={{0,1},{1,0},{2,3},{3,2},{4,5},{5,4},{6,7},{7,6},{8,9},{9,8},{10,11... | collective-permute-start | bytes 786440 | tf_op jit(solution)/shard_map/ppermute | solution.py:384
  12.8 4.7 %collective-permute-start.3 = (f32[2,80,128]{2,1,0:T(8,128)S(1)}, f32[2,80,128]{2,1,0:T(8,128)S(1)}, u32[]{:S(2)}, u32[]{:S(2)}) collective-permute-start(f32[2,80,128]{2,1,0:T(8,128)S(1)} %pad_maximum_fusion.2), channel_id=1, source_target_pairs={{0,4},{2,6},{4,0},{6,2},{8,12},{10,14},{12,8},{14,10},{16,20},{18,... | collective-permute-start | bytes 245768 | tf_op jit(solution)/shard_map/ppermute | solution.py:363
  14.8 5.3 %collective-permute-start.4 = (f32[2,80,128]{2,1,0:T(8,128)S(1)}, f32[2,80,128]{2,1,0:T(8,128)S(1)}, u32[]{:S(2)}, u32[]{:S(2)}) collective-permute-start(f32[2,80,128]{2,1,0:T(8,128)S(1)} %pad_maximum_fusion.2), channel_id=1, source_target_pairs={{0,12},{2,14},{4,8},{6,10},{8,4},{10,6},{12,0},{14,2},{16,28},{18,... | collective-permute-start | bytes 245768 | tf_op jit(solution)/shard_map/ppermute | solution.py:363
  16.3 4.4 %collective-permute-start.5 = (f32[2,80,128]{2,1,0:T(8,128)S(1)}, f32[2,80,128]{2,1,0:T(8,128)S(1)}, u32[]{:S(2)}, u32[]{:S(2)}) collective-permute-start(f32[2,80,128]{2,1,0:T(8,128)S(1)} %pad_maximum_fusion.2), channel_id=1, source_target_pairs={{0,8},{2,10},{4,12},{6,14},{8,0},{10,2},{12,4},{14,6},{16,24},{18,... | collective-permute-start | bytes 245768 | tf_op jit(solution)/shard_map/ppermute | solution.py:363
  18.6 3.8 %collective-permute-start.6 = (f32[4,64,128]{2,1,0:T(8,128)S(1)}, f32[4,64,128]{2,1,0:T(8,128)S(1)}, u32[]{:S(2)}, u32[]{:S(2)}) collective-permute-start(f32[4,64,128]{2,1,0:T(8,128)S(1)} %slice.12), channel_id=1, source_target_pairs={{0,2},{2,0},{4,6},{6,4},{8,10},{10,8},{12,14},{14,12},{16,18},{18,... | collective-permute-start | bytes 393224 | tf_op jit(solution)/shard_map/ppermute | solution.py:363
  20.7 3.0 %collective-permute-start.7 = (f32[4,64,128]{2,1,0:T(8,128)S(1)}, f32[4,64,128]{2,1,0:T(8,128)S(1)}, u32[]{:S(2)}, u32[]{:S(2)}) collective-permute-start(f32[4,64,128]{2,1,0:T(8,128)S(1)} %pad_maximum_fusion.1), channel_id=1, source_target_pairs={{0,2},{2,0},{4,6},{6,4},{8,10},{10,8},{12,14},{14,12},{16,18},{18,... | collective-permute-start | bytes 393224 | tf_op jit(solution)/shard_map/ppermute | solution.py:363
  20.8 0.9 %copy-start.3 = (f32[8,4096]{1,0:T(8,128)S(1)}, f32[8,4096]{1,0:T(8,128)}, u32[]{:S(2)}) copy-start(f32[8,4096]{1,0:T(8,128)} %omega_ref.1) | copy-start | bytes 393220
  20.8 0.9 %copy-start.4 = (f32[4096]{0:T(1024)S(1)}, f32[4096]{0:T(1024)}, u32[]{:S(2)}) copy-start(f32[4096]{0:T(1024)} %param.12) | copy-start | bytes 49156
